TPU v7x, 32 devices: a whole 2x2x4 slice. The times are simulated.
32 devices in a mesh: scene: 2 (over x), tile: 8 (over z, y), date: 2 (over core).
Axes of the slice: x: 2, y: 2, z: 4, core: 2. Of those that a mesh axis runs over, the one named last changes fastest.
Arguments:
- slc_real: bfloat16 [32, 512, 256], P('date', ('scene', 'tile')), parts along dimension 1, may hold values from -4.5 to 4.5
- slc_imag: bfloat16 [32, 512, 256], P('date', ('scene', 'tile')), parts along dimension 1, may hold values from -4.5 to 4.5
- pair_offset: int32 [32, 4], replicated, may hold values from 1 to 5, as said below
- pair_weight: int32 [128, 512, 256], P(None, ('scene', 'tile', 'date')), parts along dimension 1, may hold values from 1 to 255
Outputs:
- increments: float32 [31, 512, 256], P(None, ('scene', 'tile', 'date')), parts along dimension 1
There are 2 independent parts, one for each index of `scene`. A program takes and returns all parts, laid end to end along the dimension named above; an argument that names none is the same for every part. Nothing has to cross between parts.
Inputs may be any that keep to these rules, and one draw needn't show every extreme that they name: `pair_offset`: each row holds 4 different offsets in increasing order; 1 and 5 are in every row.
All inputs are finite; a program needn't handle non-finite values.
Results may differ from a plain program's by a relative error of at most 0.0003.
Values may be sent and summed in bfloat16 or wider, within the bound.
No kernel may reach another device: no remote copies, remote signals or barrier semaphores. Data moves between devices by JAX's collectives and lax.ppermute only.
A program may use at most 128 MiB of HBM per device.

v0:
```python
import jax
import jax.numpy as jnp
from jax import lax
from jax.sharding import PartitionSpec as P

K = 4
SPAN = 5
SWEEPS = 8
PASSES = 3
STEPS = 2


unwrap_damping = 0.08
column_weight = 0.15
solve_damping = 0.1
residual_scale = 0.3


def extended(block, sides, width):
    for axis, dim in sides:
        count = lax.axis_size(axis)
        forward = [(i, i + 1) for i in range(count - 1)]
        backward = [(target, source) for source, target in forward]
        low = lax.ppermute(
            lax.slice_in_dim(block, block.shape[dim] - width, None, axis=dim), axis, forward
        )
        high = lax.ppermute(lax.slice_in_dim(block, 0, width, axis=dim), axis, backward)
        block = jnp.concatenate([low, block, high], axis=dim)
    return block


def from_left(values):
    widths = [(0, 0)] * (values.ndim - 1) + [(1, 0)]
    return jnp.pad(values[..., :-1], widths)


def from_right(values):
    widths = [(0, 0)] * (values.ndim - 1) + [(0, 1)]
    return jnp.pad(values[..., 1:], widths)


def coupling(here_re, here_im, there_re, there_im, weight):
    magnitude = jnp.sqrt(
        (here_re * here_re + here_im * here_im) * (there_re * there_re + there_im * there_im)
    )
    link_value = weight * magnitude / (magnitude + 1.0)
    slope_value = (here_im * there_re - here_re * there_im) / (magnitude + 1.0)
    return (link_value, slope_value)


def box_mean(values):
    row_sum = values[..., :-2, :] + values[..., 1:-1, :] + values[..., 2:, :]
    return (from_left(row_sum) + row_sum + from_right(row_sum)) / 9.0


def cell_terms(smooth_re, smooth_im):
    centre_re = smooth_re[..., 1:-1, :]
    centre_im = smooth_im[..., 1:-1, :]
    link_up, slope_up = coupling(
        centre_re, centre_im, smooth_re[..., :-2, :], smooth_im[..., :-2, :], 1.0
    )
    link_down, slope_down = coupling(
        centre_re, centre_im, smooth_re[..., 2:, :], smooth_im[..., 2:, :], 1.0
    )
    link_left, slope_left = coupling(
        centre_re, centre_im, from_left(centre_re), from_left(centre_im), column_weight
    )
    link_right, slope_right = coupling(
        centre_re, centre_im, from_right(centre_re), from_right(centre_im), column_weight
    )
    denominator = link_up + link_down + link_left + link_right + unwrap_damping
    source = (
        link_up * slope_up
        + link_down * slope_down
        + link_left * slope_left
        + link_right * slope_right
    )
    return (link_up, link_down, link_left, link_right, denominator, source)


def relax_once(unwrapped, above, below, stencil):
    link_up, link_down, link_left, link_right, denominator, source = stencil
    summed = (
        source
        + link_up * above
        + link_down * below
        + link_left * from_left(unwrapped)
        + link_right * from_right(unwrapped)
    )
    return summed / denominator


def pair_tables(pair_offset):
    date_count = pair_offset.shape[0]
    per_date = pair_offset.shape[1]
    first_date = jnp.arange(date_count * per_date, dtype=jnp.int32) // per_date
    second = first_date + pair_offset.reshape(-1)
    validity = (second < date_count).astype(jnp.float32)
    unknown = jnp.arange(date_count - 1, dtype=jnp.int32)
    design = (
        (unknown[None, :] >= first_date[:, None]) & (unknown[None, :] < second[:, None])
    ).astype(jnp.float32)
    return (validity, design)


def forward(design, values):
    return jnp.dot(
        design, values, precision=lax.Precision.HIGHEST, preferred_element_type=jnp.float32
    )


def backward(design, values):
    return jnp.dot(
        design.T, values, precision=lax.Precision.HIGHEST, preferred_element_type=jnp.float32
    )


def invert(phases, base_weight, design):
    increments = jnp.zeros((design.shape[1], phases.shape[1]), jnp.float32)
    for pass_index in range(PASSES):
        scaled = (phases - forward(design, increments)) / residual_scale
        weights = base_weight / (1.0 + scaled * scaled)
        diagonal = backward(design, weights) + solve_damping
        for step_index in range(STEPS):
            gradient = (
                backward(design, weights * (phases - forward(design, increments)))
                - solve_damping * increments
            )
            increments = increments + 1.0 / SPAN * gradient / diagonal
    return increments


def interfere(source_stack, first_count, second_date, validity):
    height = source_stack.shape[2]
    columns = source_stack.shape[3]
    last_index = source_stack.shape[1] - 1
    picked = jnp.minimum(second_date, last_index)
    shape_out = (first_count, K, height, columns)
    first_re = (
        jnp.broadcast_to(source_stack[0, :first_count, None], shape_out)
        .reshape(first_count * K, height, columns)
        .astype(jnp.float32)
    )
    first_im = (
        jnp.broadcast_to(source_stack[1, :first_count, None], shape_out)
        .reshape(first_count * K, height, columns)
        .astype(jnp.float32)
    )
    second_re = jnp.take(source_stack[0], picked, axis=0).astype(jnp.float32)
    second_im = jnp.take(source_stack[1], picked, axis=0).astype(jnp.float32)
    pair_real = validity * (first_re * second_re + first_im * second_im)
    pair_imag = validity * (first_im * second_re - first_re * second_im)
    return jnp.stack([pair_real, pair_imag])


def unwrap(formed, first_row, shard_rows, image_rows, rim_depth, refresh):
    smooth_rows = formed.shape[2] - 2
    global_row = first_row - rim_depth + jnp.arange(smooth_rows, dtype=jnp.int32)
    inside = ((global_row >= 0) & (global_row < image_rows)).astype(jnp.float32)[:, None]
    smooth_re = box_mean(formed[0]) * inside
    smooth_im = box_mean(formed[1]) * inside
    stencil = cell_terms(smooth_re, smooth_im)
    pair_count = formed.shape[1]
    columns = formed.shape[3]
    unwrapped = jnp.zeros((pair_count, shard_rows + 2 * rim_depth, columns), jnp.float32)
    for sweep_index in range(SWEEPS):
        if sweep_index > 0 and sweep_index % rim_depth == 0:
            unwrapped = refresh(unwrapped[:, rim_depth : rim_depth + shard_rows])
        interior = relax_once(unwrapped[:, 1:-1], unwrapped[:, :-2], unwrapped[:, 2:], stencil)
        unwrapped = jnp.concatenate([unwrapped[:, :1], interior, unwrapped[:, -1:]], axis=1)
    return unwrapped[:, rim_depth : rim_depth + shard_rows]


def local(slc_real, slc_imag, pair_offset, pair_weight):
    tile_rows = slc_real.shape[1]
    columns = slc_real.shape[2]
    date_count = pair_offset.shape[0]
    date_group = lax.axis_index("date")
    tile_index = lax.axis_index("tile")
    group_count = lax.axis_size("date")
    image_rows = tile_rows * lax.axis_size("tile")
    rim_depth = 1
    images = jnp.stack([slc_real, slc_imag])
    validity, design = pair_tables(pair_offset)
    row_blocks = lax.all_to_all(images, "date", split_axis=2, concat_axis=1, tiled=True)
    shard_rows = row_blocks.shape[2]
    first_row = (tile_index * group_count + date_group) * shard_rows
    second_date = (jnp.arange(date_count, dtype=jnp.int32)[:, None] + pair_offset).reshape(-1)
    pair_maps = interfere(row_blocks, date_count, second_date, validity[:, None, None])
    formed = extended(pair_maps, ((("tile", "date"), 2),), rim_depth + 1)

    def refresh(values):
        return extended(values, ((("tile", "date"), 1),), rim_depth)

    phases = unwrap(formed, first_row, shard_rows, image_rows, rim_depth, refresh)
    base_weight = pair_weight.astype(jnp.float32) / 255.0 * validity[:, None, None]
    pair_count = phases.shape[0]
    local_rows = phases.shape[1]
    increments = invert(phases.reshape(pair_count, -1), base_weight.reshape(pair_count, -1), design)
    return increments.reshape(design.shape[1], local_rows, columns)


def solution(mesh):
    placed = (
        P("date", ("scene", "tile"), None),
        P("date", ("scene", "tile"), None),
        P(),
        P(None, ("scene", "tile", "date"), None),
    )
    return jax.shard_map(
        local,
        mesh=mesh,
        in_specs=placed,
        out_specs=P(None, ("scene", "tile", "date"), None),
        check_vma=False,
    )
```

profile of v0, /device:TPU:1, one launch (start us, length us, event | category | flops | bytes accessed | tf_op | source)
XLA Modules:
  0.0 168.7 jit_solution(14839721943044974520)
XLA Ops:
  2.2 3.5 %all-to-all-start = ((bf16[2,16,32,256]{3,1,0,2:T(8,128)(2,1)}), bf16[2,16,32,256]{3,1,0,2:T(8,128)(2,1)S(1)}, u32[]{:S(2)}, u32[]{:S(2)}) async-start(bf16[2,16,32,256]{3,1,0,2:T(8,128)(2,1)} %pad_maximum_fusion.17), calls=%async_computation | async-start | bytes 1048576 | tf_op jit(solution)/shard_map/all_to_all | solution.py:185
  15.8 4.9 %collective-permute-start = (f32[2,128,2,256]{3,2,1,0:T(2,128)}, f32[2,128,2,256]{3,2,1,0:T(2,128)S(1)}, u32[]{:S(2)}, u32[]{:S(2)}) collective-permute-start(f32[2,128,2,256]{3,2,1,0:T(2,128)} %get-tuple-element.14), channel_id=1, source_target_pairs={{0,1},{1,2},{2,3},{3,4},{4,5},{5,6},{6,7},{7,8},{8,9},{9,10},{10,1... | collective-permute-start | bytes 1572872 | tf_op jit(solution)/shard_map/ppermute | solution.py:24
  24.9 2.9 %copy.20 = f32[16,8,16,256]{3,1,2,0:T(8,128)} copy(f32[16,8,16,256]{3,2,1,0:T(8,128)S(1)} %bitcast.63) | data formatting | bytes 4194304
  27.9 4.8 %collective-permute-done = f32[2,128,2,256]{3,2,1,0:T(2,128)S(1)} collective-permute-done((f32[2,128,2,256]{3,2,1,0:T(2,128)}, f32[2,128,2,256]{3,2,1,0:T(2,128)S(1)}, u32[]{:S(2)}, u32[]{:S(2)}) %collective-permute-start) | collective-permute-done | bytes 524320 | tf_op jit(solution)/shard_map/ppermute | solution.py:24
  32.7 2.6 %pad_maximum_fusion = f32[2,128,20,256]{3,2,1,0:T(8,128)S(1)} fusion(f32[2,128,2,256]{3,2,1,0:T(2,128)} %collective-permute-done.1, f32[1,128,16,256]{3,2,1,0:T(8,128)} %bitcast.59, f32[1,128,16,256]{3,2,1,0:T(8,128)S(1)} %bitcast.57, f32[2,128,2,256]{3,2,1,0:T(2,128)S(1)} %collective-permute-done), kind=kLoop, calls=%fused_computation.2 | loop fusion | flops 3932160 | bytes 10485760 | tf_op jit(solution)/shard_map/concatenate | solution.py:28
  36.4 2.7 %fusion.103 = (f32[128,18,255]{2,1,0:T(8,128)S(1)}, f32[128,18,255]{2,1,0:T(8,128)}) fusion(f32[128,18,256]{2,1,0:T(8,128)S(1)} %slice_add_fusion.2), kind=kLoop, calls=%fused_computation.169 | loop fusion | bytes 9400320 | tf_op jit(solution)/shard_map/slice | solution.py:34
  39.7 3.8 %fusion.104 = (f32[128,18,255]{2,1,0:T(8,128)}, f32[128,18,255]{2,1,0:T(8,128)}) fusion(f32[128,18,256]{2,1,0:T(8,128)S(1)} %slice_add_fusion), kind=kLoop, calls=%fused_computation.170 | loop fusion | bytes 9400320 | tf_op jit(solution)/shard_map/slice | solution.py:34
  43.5 5.3 %add_multiply_fusion.1 = (f32[128,18,256]{2,1,0:T(8,128)S(1)}, f32[128,18,256]{2,1,0:T(8,128)S(1)}) fusion(f32[128,18,255]{2,1,0:T(8,128)} %get-tuple-element.23, f32[128,18,255]{2,1,0:T(8,128)S(1)} %get-tuple-element.22, f32[18]{0:T(128)S(1)} %and_select_fusion, f32[128,18,255]{2,1,0:T(8,128)} %get-tuple-element.25, f32[128,18,255]{2,1,0:T(8,128)} %get-tuple-element.24, ...), kind=kLoop, calls=%fused_computation.48 | loop fusion | flops 5898240 | bytes 28274760 | tf_op jit(solution)/shard_map/mul | solution.py:160
  51.0 2.9 %fusion.102 = (f32[128,16,255]{2,1,0:T(8,128)}, f32[128,16,255]{2,1,0:T(8,128)}) fusion(f32[128,18,256]{2,1,0:T(8,128)S(1)} %get-tuple-element.57), kind=kLoop, calls=%fused_computation.168 | loop fusion | bytes 8355840 | tf_op jit(solution)/shard_map/slice | solution.py:34
  54.1 9.2 %fusion.80 = (f32[128,16,256]{2,1,0:T(8,128)S(1)}, f32[128,16,256]{2,1,0:T(8,128)S(1)}, f32[128,16,256]{2,1,0:T(8,128)S(1)}, f32[128,16,256]{2,1,0:T(8,128)S(1)}...) fusion(f32[128,16,255]{2,1,0:T(8,128)S(1)} %broadcast.202, f32[128,16,255]{2,1,0:T(8,128)} %get-tuple-element.21, ...), kind=kLoop, calls=%fused_computation.132 | loop fusion | flops 34078720 | bytes 35610624 | tf_op jit(solution)/shard_map/div | solution.py:90
  63.5 4.3 %collective-permute-start.2 = (f32[128,1,256]{2,1,0:T(1,128)S(1)}, f32[128,1,256]{2,1,0:T(1,128)S(1)}, u32[]{:S(2)}, u32[]{:S(2)}) collective-permute-start(f32[128,1,256]{2,1,0:T(1,128)S(1)} %get-tuple-element.52), channel_id=1, source_target_pairs={{0,1},{1,2},{2,3},{3,4},{4,5},{5,6},{6,7},{7,8},{8,9},{9,10},{10,1... | collective-permute-start | bytes 393224 | tf_op jit(solution)/shard_map/ppermute | solution.py:24
  70.6 3.4 %collective-permute-done.3 = f32[128,1,256]{2,1,0:T(1,128)S(1)} collective-permute-done((f32[128,1,256]{2,1,0:T(1,128)S(1)}, f32[128,1,256]{2,1,0:T(1,128)S(1)}, u32[]{:S(2)}, u32[]{:S(2)}) %collective-permute-start.3) | collective-permute-done | bytes 131104 | tf_op jit(solution)/shard_map/ppermute | solution.py:27
  74.0 2.7 %fusion.74 = f32[128,16,256]{2,1,0:T(8,128)S(1)} fusion(f32[128,16,256]{2,1,0:T(8,128)S(1)} %get-tuple-element.11, f32[128,1,256]{2,1,0:T(1,128)S(1)} %collective-permute-done.3, f32[128,16,256]{2,1,0:T(8,128)S(1)} %get-tuple-element.6, f32[128,16,256]{2,1,0:T(8,128)S(1)} %get-tuple-element.7, f32[128,16,256]{2,1,0:T(8,128)S(1)} %get-tuple-element.8, ...), kind=kLoop, calls=%fused_computation.121 | loop fusion | flops 7864320 | bytes 19120128 | tf_op jit(solution)/shard_map/div | solution.py:90
  82.0 3.1 %collective-permute-done.5 = f32[128,1,256]{2,1,0:T(1,128)S(1)} collective-permute-done((f32[128,1,256]{2,1,0:T(1,128)S(1)}, f32[128,1,256]{2,1,0:T(1,128)S(1)}, u32[]{:S(2)}, u32[]{:S(2)}) %collective-permute-start.5) | collective-permute-done | bytes 131104 | tf_op jit(solution)/shard_map/ppermute | solution.py:27
  85.1 2.6 %fusion.67 = f32[128,16,256]{2,1,0:T(8,128)S(1)} fusion(f32[128,16,256]{2,1,0:T(8,128)S(1)} %get-tuple-element.11, f32[128,1,256]{2,1,0:T(1,128)S(1)} %collective-permute-done.5, f32[128,16,256]{2,1,0:T(8,128)S(1)} %fusion.74, f32[128,16,256]{2,1,0:T(8,128)S(1)} %get-tuple-element.7, f32[128,16,256]{2,1,0:T(8,128)S(1)} %get-tuple-element.8, ...), kind=kLoop, calls=%fused_computation.112 | loop fusion | flops 7864320 | bytes 19120128 | tf_op jit(solution)/shard_map/div | solution.py:90
  93.1 3.1 %collective-permute-done.7 = f32[128,1,256]{2,1,0:T(1,128)S(1)} collective-permute-done((f32[128,1,256]{2,1,0:T(1,128)S(1)}, f32[128,1,256]{2,1,0:T(1,128)S(1)}, u32[]{:S(2)}, u32[]{:S(2)}) %collective-permute-start.7) | collective-permute-done | bytes 131104 | tf_op jit(solution)/shard_map/ppermute | solution.py:27
  96.1 2.6 %fusion.60 = f32[128,16,256]{2,1,0:T(8,128)S(1)} fusion(f32[128,16,256]{2,1,0:T(8,128)S(1)} %get-tuple-element.11, f32[128,1,256]{2,1,0:T(1,128)S(1)} %collective-permute-done.7, f32[128,16,256]{2,1,0:T(8,128)S(1)} %fusion.67, f32[128,16,256]{2,1,0:T(8,128)S(1)} %get-tuple-element.7, f32[128,16,256]{2,1,0:T(8,128)S(1)} %get-tuple-element.8, ...), kind=kLoop, calls=%fused_computation.103 | loop fusion | flops 7864320 | bytes 19120128 | tf_op jit(solution)/shard_map/div | solution.py:90
  104.1 3.9 %collective-permute-done.9 = f32[128,1,256]{2,1,0:T(1,128)S(1)} collective-permute-done((f32[128,1,256]{2,1,0:T(1,128)S(1)}, f32[128,1,256]{2,1,0:T(1,128)S(1)}, u32[]{:S(2)}, u32[]{:S(2)}) %collective-permute-start.9) | collective-permute-done | bytes 131104 | tf_op jit(solution)/shard_map/ppermute | solution.py:27
  115.9 4.0 %collective-permute-done.11 = f32[128,1,256]{2,1,0:T(1,128)S(1)} collective-permute-done((f32[128,1,256]{2,1,0:T(1,128)S(1)}, f32[128,1,256]{2,1,0:T(1,128)S(1)}, u32[]{:S(2)}, u32[]{:S(2)}) %collective-permute-start.11) | collective-permute-done | bytes 131104 | tf_op jit(solution)/shard_map/ppermute | solution.py:27
  119.9 2.6 %fusion.46 = f32[128,16,256]{2,1,0:T(8,128)S(1)} fusion(f32[128,16,256]{2,1,0:T(8,128)S(1)} %get-tuple-element.11, f32[128,1,256]{2,1,0:T(1,128)S(1)} %collective-permute-done.11, f32[128,16,256]{2,1,0:T(8,128)S(1)} %fusion.53, f32[128,16,256]{2,1,0:T(8,128)S(1)} %get-tuple-element.7, f32[128,16,256]{2,1,0:T(8,128)S(1)} %get-tuple-element.8, ...), kind=kLoop, calls=%fused_computation.85 | loop fusion | flops 7864320 | bytes 19120128 | tf_op jit(solution)/shard_map/div | solution.py:90
  127.8 4.0 %collective-permute-done.13 = f32[128,1,256]{2,1,0:T(1,128)S(1)} collective-permute-done((f32[128,1,256]{2,1,0:T(1,128)S(1)}, f32[128,1,256]{2,1,0:T(1,128)S(1)}, u32[]{:S(2)}, u32[]{:S(2)}) %collective-permute-start.13) | collective-permute-done | bytes 131104 | tf_op jit(solution)/shard_map/ppermute | solution.py:27
  131.8 2.6 %fusion.39 = f32[128,16,256]{2,1,0:T(8,128)S(1)} fusion(f32[128,16,256]{2,1,0:T(8,128)S(1)} %get-tuple-element.11, f32[128,1,256]{2,1,0:T(1,128)S(1)} %collective-permute-done.13, f32[128,16,256]{2,1,0:T(8,128)S(1)} %fusion.46, f32[128,16,256]{2,1,0:T(8,128)S(1)} %get-tuple-element.7, f32[128,16,256]{2,1,0:T(8,128)S(1)} %get-tuple-element.8, ...), kind=kLoop, calls=%fused_computation.76 | loop fusion | flops 7864320 | bytes 19120128 | tf_op jit(solution)/shard_map/div | solution.py:90
  139.8 4.0 %collective-permute-done.15 = f32[128,1,256]{2,1,0:T(1,128)S(1)} collective-permute-done((f32[128,1,256]{2,1,0:T(1,128)S(1)}, f32[128,1,256]{2,1,0:T(1,128)S(1)}, u32[]{:S(2)}, u32[]{:S(2)}) %collective-permute-start.15) | collective-permute-done | bytes 131104 | tf_op jit(solution)/shard_map/ppermute | solution.py:27
  143.8 2.8 %fusion.32 = f32[128,16,256]{2,1,0:T(8,128)S(1)} fusion(f32[128,16,256]{2,1,0:T(8,128)S(1)} %get-tuple-element.11, f32[128,1,256]{2,1,0:T(1,128)S(1)} %collective-permute-done.15, f32[128,16,256]{2,1,0:T(8,128)S(1)} %fusion.39, f32[128,16,256]{2,1,0:T(8,128)S(1)} %get-tuple-element.7, f32[128,16,256]{2,1,0:T(8,128)S(1)} %get-tuple-element.8, ...), kind=kLoop, calls=%fused_computation.67 | loop fusion | flops 7864320 | bytes 19120128 | tf_op jit(solution)/shard_map/div | solution.py:90
  (91 shorter events, 79.4 us)
Async XLA Ops:
  0.0 5.7 %copy-start.2 = (s32[32,4]{0,1:T(4,128)S(1)}, s32[32,4]{0,1:T(4,128)}, u32[]{:S(2)}) copy-start(s32[32,4]{0,1:T(4,128)} %param.8) | copy-start | bytes 1540
  2.2 4.9 %all-to-all-start = ((bf16[2,16,32,256]{3,1,0,2:T(8,128)(2,1)}), bf16[2,16,32,256]{3,1,0,2:T(8,128)(2,1)S(1)}, u32[]{:S(2)}, u32[]{:S(2)}) async-start(bf16[2,16,32,256]{3,1,0,2:T(8,128)(2,1)} %pad_maximum_fusion.17), calls=%async_computation | async-start | bytes 1048576 | tf_op jit(solution)/shard_map/all_to_all | solution.py:185
  14.3 1.5 copy-start
  15.8 16.9 %collective-permute-start = (f32[2,128,2,256]{3,2,1,0:T(2,128)}, f32[2,128,2,256]{3,2,1,0:T(2,128)S(1)}, u32[]{:S(2)}, u32[]{:S(2)}) collective-permute-start(f32[2,128,2,256]{3,2,1,0:T(2,128)} %get-tuple-element.14), channel_id=1, source_target_pairs={{0,1},{1,2},{2,3},{3,4},{4,5},{5,6},{6,7},{7,8},{8,9},{9,10},{10,1... | collective-permute-start | bytes 1572872 | tf_op jit(solution)/shard_map/ppermute | solution.py:24
  20.7 12.0 %collective-permute-start.1 = (f32[2,128,2,256]{3,2,1,0:T(2,128)S(1)}, f32[2,128,2,256]{3,2,1,0:T(2,128)}, u32[]{:S(2)}, u32[]{:S(2)}) collective-permute-start(f32[2,128,2,256]{3,2,1,0:T(2,128)S(1)} %get-tuple-element.15), channel_id=1, source_target_pairs={{1,0},{2,1},{3,2},{4,3},{5,4},{6,5},{7,6},{8,7},{9,8},{10,9},{11,1... | collective-permute-start | bytes 1572872 | tf_op jit(solution)/shard_map/ppermute | solution.py:27
  63.5 7.1 %collective-permute-start.2 = (f32[128,1,256]{2,1,0:T(1,128)S(1)}, f32[128,1,256]{2,1,0:T(1,128)S(1)}, u32[]{:S(2)}, u32[]{:S(2)}) collective-permute-start(f32[128,1,256]{2,1,0:T(1,128)S(1)} %get-tuple-element.52), channel_id=1, source_target_pairs={{0,1},{1,2},{2,3},{3,4},{4,5},{5,6},{6,7},{7,8},{8,9},{9,10},{10,1... | collective-permute-start | bytes 393224 | tf_op jit(solution)/shard_map/ppermute | solution.py:24
  67.8 6.3 %collective-permute-start.3 = (f32[128,1,256]{2,1,0:T(1,128)S(1)}, f32[128,1,256]{2,1,0:T(1,128)S(1)}, u32[]{:S(2)}, u32[]{:S(2)}) collective-permute-start(f32[128,1,256]{2,1,0:T(1,128)S(1)} %get-tuple-element.53), channel_id=1, source_target_pairs={{1,0},{2,1},{3,2},{4,3},{5,4},{6,5},{7,6},{8,7},{9,8},{10,9},{11,1... | collective-permute-start | bytes 393224 | tf_op jit(solution)/shard_map/ppermute | solution.py:27
  76.9 5.1 %collective-permute-start.4 = (f32[128,1,256]{2,1,0:T(1,128)S(1)}, f32[128,1,256]{2,1,0:T(1,128)S(1)}, u32[]{:S(2)}, u32[]{:S(2)}) collective-permute-start(f32[128,1,256]{2,1,0:T(1,128)S(1)} %get-tuple-element.48), channel_id=1, source_target_pairs={{0,1},{1,2},{2,3},{3,4},{4,5},{5,6},{6,7},{7,8},{8,9},{9,10},{10,1... | collective-permute-start | bytes 393224 | tf_op jit(solution)/shard_map/ppermute | solution.py:24
  78.8 6.3 %collective-permute-start.5 = (f32[128,1,256]{2,1,0:T(1,128)S(1)}, f32[128,1,256]{2,1,0:T(1,128)S(1)}, u32[]{:S(2)}, u32[]{:S(2)}) collective-permute-start(f32[128,1,256]{2,1,0:T(1,128)S(1)} %get-tuple-element.49), channel_id=1, source_target_pairs={{1,0},{2,1},{3,2},{4,3},{5,4},{6,5},{7,6},{8,7},{9,8},{10,9},{11,1... | collective-permute-start | bytes 393224 | tf_op jit(solution)/shard_map/ppermute | solution.py:27
  87.9 5.1 %collective-permute-start.6 = (f32[128,1,256]{2,1,0:T(1,128)S(1)}, f32[128,1,256]{2,1,0:T(1,128)S(1)}, u32[]{:S(2)}, u32[]{:S(2)}) collective-permute-start(f32[128,1,256]{2,1,0:T(1,128)S(1)} %get-tuple-element.44), channel_id=1, source_target_pairs={{0,1},{1,2},{2,3},{3,4},{4,5},{5,6},{6,7},{7,8},{8,9},{9,10},{10,1... | collective-permute-start | bytes 393224 | tf_op jit(solution)/shard_map/ppermute | solution.py:24
  89.9 6.3 %collective-permute-start.7 = (f32[128,1,256]{2,1,0:T(1,128)S(1)}, f32[128,1,256]{2,1,0:T(1,128)S(1)}, u32[]{:S(2)}, u32[]{:S(2)}) collective-permute-start(f32[128,1,256]{2,1,0:T(1,128)S(1)} %get-tuple-element.45), channel_id=1, source_target_pairs={{1,0},{2,1},{3,2},{4,3},{5,4},{6,5},{7,6},{8,7},{9,8},{10,9},{11,1... | collective-permute-start | bytes 393224 | tf_op jit(solution)/shard_map/ppermute | solution.py:27
  99.0 5.1 %collective-permute-start.8 = (f32[128,1,256]{2,1,0:T(1,128)S(1)}, f32[128,1,256]{2,1,0:T(1,128)S(1)}, u32[]{:S(2)}, u32[]{:S(2)}) collective-permute-start(f32[128,1,256]{2,1,0:T(1,128)S(1)} %get-tuple-element.40), channel_id=1, source_target_pairs={{0,1},{1,2},{2,3},{3,4},{4,5},{5,6},{6,7},{7,8},{8,9},{9,10},{10,1... | collective-permute-start | bytes 393224 | tf_op jit(solution)/shard_map/ppermute | solution.py:24
  100.9 7.1 %collective-permute-start.9 = (f32[128,1,256]{2,1,0:T(1,128)S(1)}, f32[128,1,256]{2,1,0:T(1,128)S(1)}, u32[]{:S(2)}, u32[]{:S(2)}) collective-permute-start(f32[128,1,256]{2,1,0:T(1,128)S(1)} %get-tuple-element.41), channel_id=1, source_target_pairs={{1,0},{2,1},{3,2},{4,3},{5,4},{6,5},{7,6},{8,7},{9,8},{10,9},{11,1... | collective-permute-start | bytes 393224 | tf_op jit(solution)/shard_map/ppermute | solution.py:27
  110.8 5.1 %collective-permute-start.10 = (f32[128,1,256]{2,1,0:T(1,128)S(1)}, f32[128,1,256]{2,1,0:T(1,128)S(1)}, u32[]{:S(2)}, u32[]{:S(2)}) collective-permute-start(f32[128,1,256]{2,1,0:T(1,128)S(1)} %get-tuple-element.36), channel_id=1, source_target_pairs={{0,1},{1,2},{2,3},{3,4},{4,5},{5,6},{6,7},{7,8},{8,9},{9,10},{10,1... | collective-permute-start | bytes 393224 | tf_op jit(solution)/shard_map/ppermute | solution.py:24
  112.7 7.2 %collective-permute-start.11 = (f32[128,1,256]{2,1,0:T(1,128)S(1)}, f32[128,1,256]{2,1,0:T(1,128)S(1)}, u32[]{:S(2)}, u32[]{:S(2)}) collective-permute-start(f32[128,1,256]{2,1,0:T(1,128)S(1)} %get-tuple-element.37), channel_id=1, source_target_pairs={{1,0},{2,1},{3,2},{4,3},{5,4},{6,5},{7,6},{8,7},{9,8},{10,9},{11,1... | collective-permute-start | bytes 393224 | tf_op jit(solution)/shard_map/ppermute | solution.py:27
  122.7 5.1 %collective-permute-start.12 = (f32[128,1,256]{2,1,0:T(1,128)S(1)}, f32[128,1,256]{2,1,0:T(1,128)S(1)}, u32[]{:S(2)}, u32[]{:S(2)}) collective-permute-start(f32[128,1,256]{2,1,0:T(1,128)S(1)} %get-tuple-element.32), channel_id=1, source_target_pairs={{0,1},{1,2},{2,3},{3,4},{4,5},{5,6},{6,7},{7,8},{8,9},{9,10},{10,1... | collective-permute-start | bytes 393224 | tf_op jit(solution)/shard_map/ppermute | solution.py:24
  124.6 7.2 %collective-permute-start.13 = (f32[128,1,256]{2,1,0:T(1,128)S(1)}, f32[128,1,256]{2,1,0:T(1,128)S(1)}, u32[]{:S(2)}, u32[]{:S(2)}) collective-permute-start(f32[128,1,256]{2,1,0:T(1,128)S(1)} %get-tuple-element.33), channel_id=1, source_target_pairs={{1,0},{2,1},{3,2},{4,3},{5,4},{6,5},{7,6},{8,7},{9,8},{10,9},{11,1... | collective-permute-start | bytes 393224 | tf_op jit(solution)/shard_map/ppermute | solution.py:27
  134.6 5.1 %collective-permute-start.14 = (f32[128,1,256]{2,1,0:T(1,128)S(1)}, f32[128,1,256]{2,1,0:T(1,128)S(1)}, u32[]{:S(2)}, u32[]{:S(2)}) collective-permute-start(f32[128,1,256]{2,1,0:T(1,128)S(1)} %get-tuple-element.28), channel_id=1, source_target_pairs={{0,1},{1,2},{2,3},{3,4},{4,5},{5,6},{6,7},{7,8},{8,9},{9,10},{10,1... | collective-permute-start | bytes 393224 | tf_op jit(solution)/shard_map/ppermute | solution.py:24
  136.6 7.2 %collective-permute-start.15 = (f32[128,1,256]{2,1,0:T(1,128)S(1)}, f32[128,1,256]{2,1,0:T(1,128)S(1)}, u32[]{:S(2)}, u32[]{:S(2)}) collective-permute-start(f32[128,1,256]{2,1,0:T(1,128)S(1)} %get-tuple-element.29), channel_id=1, source_target_pairs={{1,0},{2,1},{3,2},{4,3},{5,4},{6,5},{7,6},{8,7},{9,8},{10,9},{11,1... | collective-permute-start | bytes 393224 | tf_op jit(solution)/shard_map/ppermute | solution.py:27
  148.2 1.6 copy-start.1
where the time goes:
time: 172 us; the launch traced here: 169 us
  other arithmetic  45.2 us (26%)
  starting transfers between devices  43.2 us (25%)
  waiting for transfers between devices  31.5 us (18%)
  local copies, waits for them, and re-layouts  29.7 us (17%)
  matrix products  18 us (10%)
    div x8, other arithmetic, relax_once(): return summed / denominator  27.8 us
    ppermute x8, waiting for transfers between devices, extended(): lax.ppermute(lax.slice_in_dim(block, 0, width, axis=dim), axis, backward)  25.5 us
    ppermute x8, starting transfers between devices, extended(): lax.ppermute(lax.slice_in_dim(block, block.shape[dim] - width, None, axis...  20.7 us
    ppermute x8, starting transfers between devices, extended(): lax.ppermute(lax.slice_in_dim(block, 0, width, axis=dim), axis, backward)  19 us
    slice x11, local copies, waits for them, and re-layouts, from_left(): return jnp.pad(values[..., :-1], widths)  16.9 us
    dot_general x9, matrix products, backward(): jnp.dot(design.T, values, precision=lax.Precision.HIGHEST, preferred_elem...  10.8 us
    dot_general x6, matrix products, forward(): jnp.dot(design, values, precision=lax.Precision.HIGHEST, preferred_elemen...  7.19 us
    unnamed x10, local copies, waits for them, and re-layouts  5.75 us
  transfers between devices with their start and end apart: 17, of which 9 were waited for; matrix products, arithmetic and copies ran while one was open for 6% of the time, Pallas kernels for 0%

commit v1 on v0

v1 whole, which is shorter than its diff:
```python
import functools

import jax
import jax.numpy as jnp
from jax import lax
from jax.experimental import pallas as pl
from jax.experimental.pallas import tpu as pltpu
from jax.sharding import PartitionSpec as P

K = 4
SPAN = 5
SWEEPS = 8
PASSES = 3
STEPS = 2

unwrap_damping = 0.08
column_weight = 0.15
solve_damping = 0.1
residual_scale = 0.3

LANES = 128
SUB = 8
HALO = SWEEPS + 1
F32 = jnp.float32
BF16 = jnp.bfloat16


def al(x):
    return pl.multiple_of(x, SUB)


def vreg(ref, row):
    return ref[pl.ds(row, SUB), :]


def perm_matrix(transpose):
    n = 2 * LANES
    a = lax.broadcasted_iota(jnp.int32, (n, n), 0)
    b = lax.broadcasted_iota(jnp.int32, (n, n), 1)
    col, place = (b, a) if transpose else (a, b)
    target = (col % 2) * LANES + col // 2
    return jnp.where(place == target, 1.0, 0.0).astype(BF16)


def pack_kernel(halo, re_ref, im_ref, all_ref, same_ref, cross_ref, flat):
    dates, rows, columns = re_ref.shape
    side = lax.axis_index("date")
    perm = perm_matrix(False)
    for part, ref in enumerate((re_ref, im_ref)):
        block = ref[...].reshape(dates * rows, columns)
        out = jnp.dot(block, perm, preferred_element_type=F32)
        for half in range(2):
            flat[part, half] = out[:, half * LANES : (half + 1) * LANES]
    for row in range(rows):
        for part in range(2):
            for half in range(2):
                tile = flat[part, half, pl.ds(row, dates, stride=rows), :]
                all_ref[row, part, half] = tile.astype(BF16)
    last = rows - halo
    same_ref[...] = all_ref[pl.ds(last * (1 - side), halo)]
    cross_ref[...] = all_ref[pl.ds(last * side, halo)]


def pack(slc_real, slc_imag):
    dates, rows, columns = slc_real.shape
    shape = lambda count: jax.ShapeDtypeStruct((count, 2, 2, dates, LANES), BF16)
    vm = pl.BlockSpec(memory_space=pltpu.VMEM)
    return pl.pallas_call(
        functools.partial(pack_kernel, HALO),
        out_shape=(shape(rows), shape(HALO), shape(HALO)),
        in_specs=[vm, vm],
        out_specs=(vm, vm, vm),
        scratch_shapes=[pltpu.VMEM((2, 2, dates * rows, LANES), F32)],
        name="pack",
    )(slc_real, slc_imag)


def main_kernel(
    own_ref, partner_ref, same_ref, cross_ref, offset_ref, weight_hbm, out_hbm,
    img, cre, cim, zre, zim, mag, hle, hlo, dh, sh, rr, ss, aa, ya, yb,
    yy, wraw, wf, vv, aw, ag, wk, msk, vfin, obuf, wsem, osem,
):
    half_dates = own_ref.shape[3]
    dates = 2 * half_dates
    tile_rows = own_ref.shape[0]
    R = tile_rows // 2
    H = HALO
    NR = R + 2 * H
    NZ = NR - 2
    DP = dates + SUB
    NF = dates // SUB
    side = lax.axis_index("date")
    tile = lax.axis_index("tile")
    tiles = lax.axis_size("tile")

    copies = []
    for half in range(2):
        copies.append(
            pltpu.make_async_copy(
                weight_hbm.at[:, :, pl.ds(half * LANES, LANES)], wraw.at[half], wsem.at[half]
            )
        )
    for copy in copies:
        copy.start()

    offsets = offset_ref[...]
    m1 = jnp.where(offsets[:, 1:2] == 2, 1.0, 0.0).astype(F32)
    m2 = jnp.where(offsets[:, 2:3] == 4, 1.0, 0.0).astype(F32)
    msk[0] = jnp.broadcast_to(m1, (dates, LANES))
    msk[1] = jnp.broadcast_to(m2, (dates, LANES))
    first = lax.broadcasted_iota(jnp.int32, (dates, 1), 0)
    for k in range(K):
        ok = jnp.where(first + offsets[:, k : k + 1] < dates, 1.0, 0.0).astype(F32)
        msk[2 + k] = jnp.broadcast_to(ok, (dates, LANES))

    lane = lax.broadcasted_iota(jnp.int32, (SUB, LANES), 1)
    at_first = lane == 0
    at_last = lane == LANES - 1
    zero = jnp.zeros((SUB, LANES), F32)

    third = 1.0 / 3.0
    o_date = al(half_dates * side)
    p_date = al(half_dates * (1 - side))

    def put(rho, o_tile_ref, o_row, p_tile_ref, p_row):
        for part in range(2):
            for half in range(2):
                base = ((rho * 2 + part) * 2 + half) * DP
                img[pl.ds(al(base + o_date), half_dates), :] = (
                    o_tile_ref[o_row, part, half].astype(F32) * third
                )
                img[pl.ds(al(base + p_date), half_dates), :] = (
                    p_tile_ref[p_row, part, half].astype(F32) * third
                )
                img[pl.ds(al(base + dates), SUB), :] = zero

    base_row = (R - H) * side
    base_rho = H * (1 - side)

    def put_tile(i, c):
        put(base_rho + i, own_ref, base_row + i, partner_ref, base_row + i)
        return c

    lax.fori_loop(0, R + H, put_tile, 0)
    halo_rho = (R + H) * side

    def put_halo(i, c):
        put(halo_rho + i, same_ref, i, cross_ref, i)
        return c

    lax.fori_loop(0, H, put_halo, 0)

    def roll_right(x):
        return pltpu.roll(x, 1, 1)

    def roll_left(x):
        return pltpu.roll(x, LANES - 1, 1)

    def gix(row, k, half):
        return al(((row * K + k) * 2 + half) * SUB)

    def block(ft, carry):
        f0 = al(ft * SUB)
        sel1 = vreg(msk.at[0], f0) > 0.5
        sel2 = vreg(msk.at[1], f0) > 0.5

        def form(rho):
            def image(part, half, shift):
                return vreg(img, ((rho * 2 + part) * 2 + half) * DP + f0 + shift)

            pair = {}
            for half in range(2):
                a_re, a_im = image(0, half, 0), image(1, half, 0)
                second = [(image(0, half, o), image(1, half, o)) for o in range(1, SPAN + 1)]
                pick = lambda mask, i, j: tuple(
                    jnp.where(mask, x, y) for x, y in zip(second[i - 1], second[j - 1])
                )
                chosen = (second[0], pick(sel1, 2, 3), pick(sel2, 4, 3), second[4])
                for k in range(K):
                    b_re, b_im = chosen[k]
                    pair[0, k, half] = a_re * b_re + a_im * b_im
                    pair[1, k, half] = a_im * b_re - a_re * b_im
            for part, ref in enumerate((cre, cim)):
                for k in range(K):
                    even, odd = pair[part, k, 0], pair[part, k, 1]
                    both = even + odd
                    ref[pl.ds(gix(rho, k, 0), SUB), :] = both + jnp.where(at_first, 0.0, roll_right(odd))
                    ref[pl.ds(gix(rho, k, 1), SUB), :] = both + jnp.where(at_last, 0.0, roll_left(even))

        UA = 2

        def phase_a(i, c):
            for u in range(UA):
                form(i * UA + u)
            return c

        lax.fori_loop(0, NR // UA, phase_a, 0)

        def edge(m, cross, scale):
            q = 1.0 / (m + 1.0)
            link = m * q
            if scale is not None:
                link = link * scale
            return link, link * (cross * q)

        def smooth(j):
            z = {}
            for k in range(K):
                for half in range(2):
                    i0, i1, i2 = (gix(j + d, k, half) for d in range(3))
                    re = vreg(cre, i0) + vreg(cre, i1) + vreg(cre, i2)
                    im = vreg(cim, i0) + vreg(cim, i1) + vreg(cim, i2)
                    sq = re * re + im * im
                    mg = sq * lax.rsqrt(jnp.maximum(sq, 1e-30))
                    zre[pl.ds(i0, SUB), :] = re
                    zim[pl.ds(i0, SUB), :] = im
                    mag[pl.ds(i0, SUB), :] = mg
                    z[k, half] = re, im, mg
            for k in range(K):
                e_re, e_im, e_mg = z[k, 0]
                o_re, o_im, o_mg = z[k, 1]
                le, ge = edge(e_mg * o_mg, e_im * o_re - e_re * o_im, column_weight)
                n_re, n_im, n_mg = roll_left(e_re), roll_left(e_im), roll_left(e_mg)
                m = jnp.where(at_last, 0.0, o_mg * n_mg)
                lo, go = edge(m, o_im * n_re - o_re * n_im, column_weight)
                i0, i1 = gix(j, k, 0), gix(j, k, 1)
                damped = le + unwrap_damping
                hle[pl.ds(i0, SUB), :] = le
                hle[pl.ds(i1, SUB), :] = lo
                dh[pl.ds(i0, SUB), :] = damped + roll_right(lo)
                dh[pl.ds(i1, SUB), :] = damped + lo
                sh[pl.ds(i0, SUB), :] = ge - roll_right(go)
                sh[pl.ds(i1, SUB), :] = go - ge

        UB = 2

        def phase_b(i, c):
            for u in range(UB):
                smooth(i * UB + u)
            return c

        lax.fori_loop(0, NZ // UB, phase_b, 0)

        @pl.when((tile == 0) & (side == 0))
        def _():
            for k in range(K):
                for half in range(2):
                    mag[pl.ds(gix(H - 2, k, half), SUB), :] = zero

        @pl.when((tile == tiles - 1) & (side == 1))
        def _():
            for k in range(K):
                for half in range(2):
                    mag[pl.ds(gix(H - 1 + R, k, half), SUB), :] = zero

        def vertical(j, k, half):
            i0, i1 = gix(j, k, half), gix(j + 1, k, half)
            m = vreg(mag, i0) * vreg(mag, i1)
            return edge(m, vreg(zim, i0) * vreg(zre, i1) - vreg(zre, i0) * vreg(zim, i1), None)

        start = []
        for k in range(K):
            for half in range(2):
                start += [*vertical(0, k, half), zero]

        def stencil(j, before):
            after = []
            for k in range(K):
                root = {}
                for half in range(2):
                    i0 = gix(j, k, half)
                    v, f = vertical(j, k, half)
                    n = (k * 2 + half) * 3
                    vm, fm, rm = before[n : n + 3]
                    den = vreg(dh, i0) + vm + v
                    src = vreg(sh, i0) + f - fm
                    r = lax.rsqrt(den)
                    rr[pl.ds(i0, SUB), :] = r
                    ss[pl.ds(i0, SUB), :] = src * r
                    aa[pl.ds(i0, SUB), :] = vm * (r * rm)
                    root[half] = r
                    after += [v, f, r]
                i0, i1 = gix(j, k, 0), gix(j, k, 1)
                hlo[pl.ds(i0, SUB), :] = vreg(hle, i0) * (root[0] * root[1])
                hlo[pl.ds(i1, SUB), :] = vreg(hle, i1) * (root[1] * roll_left(root[0]))
            return after

        UC = 2

        def phase_c(i, c):
            for u in range(UC):
                c = stencil(1 + i * UC + u, c)
            return tuple(c)

        lax.fori_loop(0, (NZ - 2) // UC, phase_c, tuple(start))

        def sweeps(k, c):
            src_ref = ss
            for s in range(1, SWEEPS):
                left = SWEEPS - 1 - s
                dst_ref = (ya, yb)[s % 2]
                lo, hi = H - 1 - left, H - 1 + R + left
                for j in range(lo, hi):
                    y = [[vreg(src_ref, gix(j + d, k, half)) for half in range(2)] for d in (-1, 0, 1)]
                    i0, i1 = gix(j, k, 0), gix(j, k, 1)
                    e, o = vreg(hlo, i0), vreg(hlo, i1)
                    new = []
                    for half in range(2):
                        i = (i0, i1)[half]
                        up, dn = vreg(aa, i), vreg(aa, gix(j + 1, k, half))
                        new.append(vreg(ss, i) + up * y[0][half] + dn * y[2][half])
                    even = new[0] + e * y[1][1] + roll_right(o * y[1][1])
                    odd = new[1] + e * y[1][0] + o * roll_left(y[1][0])
                    if s < SWEEPS - 1:
                        dst_ref[pl.ds(i0, SUB), :] = even
                        dst_ref[pl.ds(i1, SUB), :] = odd
                    else:
                        row = j - (H - 1)
                        for half, value in enumerate((even, odd)):
                            r = vreg(rr, gix(j, k, half)) * (1.0 / residual_scale)
                            place = (((row * K + k) * NF + ft) * 2 + half) * SUB
                            yy[pl.ds(al(place), SUB), :] = value * r
                src_ref = dst_ref
            return c

        lax.fori_loop(0, K, sweeps, 0)
        return carry

    lax.fori_loop(0, NF, block, 0)

    for copy in copies:
        copy.wait()
    perm = perm_matrix(False)

    def weights(row, c):
        rows = []
        for k in range(K):
            halves = [
                wraw.at[half].reshape(K * dates * R, LANES)[pl.ds(k * R + row, dates, stride=K * R), :]
                for half in range(2)
            ]
            rows.append(jnp.concatenate(halves, axis=1).astype(F32).astype(BF16))
        out = jnp.dot(jnp.concatenate(rows, axis=0), perm, preferred_element_type=F32)
        for k in range(K):
            for t in range(NF):
                for half in range(2):
                    place = (((row * K + k) * NF + t) * 2 + half) * SUB
                    x = out[(k * NF + t) * SUB : (k * NF + t + 1) * SUB, half * LANES : (half + 1) * LANES]
                    if (t + 1) * SUB + SPAN - 1 >= dates:
                        x = x * msk[2 + k, pl.ds(t * SUB, SUB), :]
                    wf[pl.ds(al(place), SUB), :] = x
        return c

    lax.fori_loop(0, R, weights, 0)

    damping = solve_damping * 255.0
    inv_span = 1.0 / SPAN
    VP = dates + SUB
    for u in range(vv.shape[0]):
        for half in range(2):
            vv[u, half, pl.ds(dates, SUB), :] = zero
            for m in range(SPAN):
                aw[u, half, m, pl.ds(0, SUB), :] = zero
                ag[u, half, m, pl.ds(0, SUB), :] = zero

    groups = [(t, half) for t in range(NF) for half in range(2)]

    def spread(ref, u, t, half, q):
        m_1 = vreg(msk.at[0], t * SUB)
        m_2 = vreg(msk.at[1], t * SUB)
        q0, q1, q2, q3 = q
        two = q2 + q3
        a1 = two + q1
        for m, value in enumerate(
            (a1 + q0, a1, jnp.where(m_1 > 0.5, two, a1), jnp.where(m_2 > 0.5, two, q3), q3)
        ):
            ref[u, half, m, pl.ds(SUB + t * SUB, SUB), :] = value

    def collect(ref, u, t, half):
        total = ref[u, half, 0, pl.ds(SUB + t * SUB, SUB), :]
        for m in range(1, SPAN):
            total = total + ref[u, half, m, pl.ds(SUB + t * SUB - m, SUB), :]
        return total

    def residual(u, row, t, half):
        y = [vreg(yy, al((((row * K + k) * NF + t) * 2 + half) * SUB)) for k in range(K)]
        s = [vv[u, half, pl.ds(t * SUB + m, SUB), :] for m in range(SPAN)]
        for m in range(1, SPAN):
            s[m] = s[m - 1] + s[m]
        m_1 = vreg(msk.at[0], t * SUB) > 0.5
        m_2 = vreg(msk.at[1], t * SUB) > 0.5
        model = (s[0], jnp.where(m_1, s[1], s[2]), jnp.where(m_2, s[3], s[2]), s[4])
        return [a - b for a, b in zip(y, model)]

    U = vv.shape[0]

    def invert_rows(i, c):
        rows = [(u, i * U + u) for u in range(U)]
        inverse = {}
        for p in range(PASSES):
            for step in range(STEPS):
                start = p == 0 and step == 0
                for u, row in rows:
                    for t, half in groups:
                        if start:
                            res = [
                                vreg(yy, al((((row * K + k) * NF + t) * 2 + half) * SUB)) for k in range(K)
                            ]
                        else:
                            res = residual(u, row, t, half)
                        g = []
                        w_all = []
                        for k in range(K):
                            if step == 0:
                                place = al((((row * K + k) * NF + t) * 2 + half) * SUB)
                                w = vreg(wf, place) * (1.0 / (1.0 + res[k] * res[k]))
                                wk[u, t, half, k] = w
                                w_all.append(w)
                            else:
                                w = wk[u, t, half, k]
                            g.append(w * res[k])
                        if step == 0:
                            spread(aw, u, t, half, w_all)
                        spread(ag, u, t, half, g)
                for u, row in rows:
                    for t, half in groups:
                        if step == 0:
                            inverse[u, t, half] = inv_span / (collect(aw, u, t, half) + damping)
                        grad = collect(ag, u, t, half)
                        place = pl.ds(t * SUB, SUB)
                        if start:
                            v = grad * inverse[u, t, half]
                        else:
                            old = vv[u, half, place, :]
                            v = old + (grad - damping * old) * inverse[u, t, half]
                        if p == PASSES - 1 and step == STEPS - 1:
                            vfin[row, half, place, :] = v * residual_scale
                        else:
                            vv[u, half, place, :] = v
        return c

    lax.fori_loop(0, R // U, invert_rows, 0)

    back = perm_matrix(True)
    unknowns = dates - 1

    def finish(row, c):
        value = jnp.concatenate([vfin[row, 0], vfin[row, 1]], axis=1)
        high = value.astype(BF16)
        rest = value - high.astype(F32)
        mid = rest.astype(BF16)
        low = (rest - mid.astype(F32)).astype(BF16)
        stack = jnp.concatenate([high, mid, low], axis=0)
        out = jnp.dot(stack, back, preferred_element_type=F32)
        out = out[:dates] + out[dates : 2 * dates] + out[2 * dates :]
        for half in range(2):
            obuf.at[half].reshape(dates * R, LANES)[pl.ds(row, dates, stride=R), :] = out[
                :, half * LANES : (half + 1) * LANES
            ]
        return c

    lax.fori_loop(0, R, finish, 0)
    outs = []
    for half in range(2):
        outs.append(
            pltpu.make_async_copy(
                obuf.at[half, pl.ds(0, unknowns)],
                out_hbm.at[:, :, pl.ds(half * LANES, LANES)],
                osem.at[half],
            )
        )
    for copy in outs:
        copy.start()
    for copy in outs:
        copy.wait()


def solve(own, partner, same, cross, pair_offset, pair_weight):
    tile_rows = own.shape[0]
    dates = 2 * own.shape[3]
    pairs, R, columns = pair_weight.shape
    H = HALO
    NR = R + 2 * H
    NZ = NR - 2
    NF = dates // SUB
    group = K * 2 * SUB
    vm = pl.BlockSpec(memory_space=pltpu.VMEM)
    hbm = pl.BlockSpec(memory_space=pl.ANY)
    U = 1
    v2 = lambda rows: pltpu.VMEM((rows, LANES), F32)
    scratch = [
        v2(NR * 4 * (dates + SUB)),
        v2(NR * group), v2(NR * group),
        v2(NZ * group), v2(NZ * group), v2(NZ * group),
        v2(NZ * group), v2(NZ * group),
        v2(NZ * group), v2(NZ * group),
        v2(NZ * group), v2(NZ * group), v2(NZ * group),
        v2(NZ * group), v2(NZ * group),
        v2(R * NF * group),
        pltpu.VMEM((2, pairs, R, LANES), jnp.int32),
        v2(R * NF * group),
        pltpu.VMEM((U, 2, dates + SUB, LANES), F32),
        pltpu.VMEM((U, 2, SPAN, dates + SUB, LANES), F32),
        pltpu.VMEM((U, 2, SPAN, dates + SUB, LANES), F32),
        pltpu.VMEM((U, NF, 2, K, SUB, LANES), F32),
        pltpu.VMEM((2 + K, dates, LANES), F32),
        pltpu.VMEM((R, 2, dates, LANES), F32),
        pltpu.VMEM((2, dates, R, LANES), F32),
        pltpu.SemaphoreType.DMA((2,)),
        pltpu.SemaphoreType.DMA((2,)),
    ]
    return pl.pallas_call(
        main_kernel,
        out_shape=jax.ShapeDtypeStruct((dates - 1, R, columns), F32),
        in_specs=[vm, vm, vm, vm, vm, hbm],
        out_specs=hbm,
        scratch_shapes=scratch,
        name="solve",
        compiler_params=pltpu.CompilerParams(vmem_limit_bytes=60 * 1024 * 1024),
    )(own, partner, same, cross, pair_offset, pair_weight)


def local(slc_real, slc_imag, pair_offset, pair_weight):
    tiles = lax.axis_size("tile")
    own, same, cross = pack(slc_real, slc_imag)
    axes = ("tile", "date")
    place = lambda t, d: 2 * t + d
    to_same = [(place(t, 0), place(t + 1, 0)) for t in range(tiles - 1)] + [
        (place(t + 1, 1), place(t, 1)) for t in range(tiles - 1)
    ]
    to_cross = [(place(t, 1), place(t + 1, 0)) for t in range(tiles - 1)] + [
        (place(t + 1, 0), place(t, 1)) for t in range(tiles - 1)
    ]
    same = lax.ppermute(same, axes, to_same)
    cross = lax.ppermute(cross, axes, to_cross)
    partner = lax.ppermute(own, "date", [(0, 1), (1, 0)])
    return solve(own, partner, same, cross, pair_offset, pair_weight)


def solution(mesh):
    placed = (
        P("date", ("scene", "tile"), None),
        P("date", ("scene", "tile"), None),
        P(),
        P(None, ("scene", "tile", "date"), None),
    )
    return jax.shard_map(
        local,
        mesh=mesh,
        in_specs=placed,
        out_specs=P(None, ("scene", "tile", "date"), None),
        check_vma=False,
    )
```

time: 172 us -> 68.4 us (0.40); the launches traced: 169 us -> 68.2 us
  Pallas kernels: 0 us -> 54.5 us
  other arithmetic: 45.2 us -> 0 us
  starting transfers between devices: 43.2 us -> 7.95 us
  waiting for transfers between devices: 31.5 us -> 2.9 us
  local copies, waits for them, and re-layouts: 29.7 us -> 2.81 us
  matrix products: 18 us -> 0 us
    pallas_call x0 -> x2, Pallas kernels: none -> 54.5 us  [the longest x1 51.5 us: solve(): pl.pallas_call(main_kernel, out_shape=jax.ShapeDtypeStruct((dates - 1, R,...]
    ppermute x16 -> x3, starting transfers between devices: 39.7 us -> 7.95 us  [the longest x1 6.65 us: local(): cross = lax.ppermute(cross, axes, to_cross)]
    div x8 -> x0, other arithmetic: 27.8 us -> none  [relax_once(): return summed / denominator]
    ppermute x16 -> x3, waiting for transfers between devices: 30.3 us -> 2.9 us  [the longest x1 2.89 us: local(): cross = lax.ppermute(cross, axes, to_cross)]
    slice x21 -> x0, local copies, waits for them, and re-layouts: 18.2 us -> none  [the longest x11 16.9 us: from_left(): return jnp.pad(values[..., :-1], widths)]
    dot_general x15 -> x0, matrix products: 18 us -> none  [the longest x9 10.8 us: backward(): jnp.dot(design.T, values, precision=lax.Precision.HIGHEST, preferred_elem...]
    mul x5 -> x0, other arithmetic: 9.51 us -> none  [the longest x2 5.26 us: unwrap(): smooth_re = box_mean(formed[0]) * inside]
    all_to_all x1 -> x0, starting transfers between devices: 3.49 us -> none  [local(): lax.all_to_all(images, 'date', split_axis=2, concat_axis=1, tiled=True)]
  transfers between devices with their start and end apart: 17 -> 3, of which waited for: 9 -> 1; matrix products, arithmetic and copies ran while one was open for 6% -> 2% of each run, Pallas kernels for 0% -> 0%
where the time goes in v1:
time: 68.4 us; the launch traced here: 68.2 us
  Pallas kernels  54.5 us (80%)
  starting transfers between devices  7.95 us (12%)
  waiting for transfers between devices  2.9 us (4%)
  local copies, waits for them, and re-layouts  2.81 us (4%)
    pallas_call x1, Pallas kernels, solve(): pl.pallas_call(main_kernel, out_shape=jax.ShapeDtypeStruct((dates - 1, R,...  51.5 us
    ppermute x1, starting transfers between devices, local(): cross = lax.ppermute(cross, axes, to_cross)  6.65 us
    pallas_call x1, Pallas kernels, pack(): pl.pallas_call(functools.partial(pack_kernel, HALO), out_shape=(shape(row...  3.04 us
    ppermute x1, waiting for transfers between devices, local(): cross = lax.ppermute(cross, axes, to_cross)  2.89 us
    unnamed x7, local copies, waits for them, and re-layouts  2.81 us
  transfers between devices with their start and end apart: 3, of which 1 were waited for; matrix products, arithmetic and copies ran while one was open for 2% of the time, Pallas kernels for 0%

profile of v1, /device:TPU:1, one launch (start us, length us, event | category | flops | bytes accessed | tf_op | source)
XLA Modules:
  0.0 68.2 jit_solution(8611194725852282151)
XLA Ops:
  0.0 3.0 %pack.1 = (bf16[32,2,2,16,128]{4,3,2,1,0:T(8,128)(2,1)}, bf16[9,2,2,16,128]{4,3,2,1,0:T(8,128)(2,1)}, bf16[9,2,2,16,128]{4,3,2,1,0:T(8,128)(2,1)}) custom-call(bf16[16,32,256]{2,1,0:T(8,128)(2,1)} %re_ref.1, bf16[16,32,256]{2,1,0:T(8,128)(2,1)} %im_ref.1), custom_call_target="tpu_custom_call" | custom-call | tf_op jit(solution)/shard_map/pack/pallas_call | solution.py:68
  3.0 0.0 collective-permute-start
  3.1 1.3 %collective-permute-start.1 = (bf16[9,2,2,16,128]{4,3,2,1,0:T(8,128)(2,1)}, bf16[9,2,2,16,128]{4,3,2,1,0:T(8,128)(2,1)S(1)}, u32[]{:S(2)}, u32[]{:S(2)}) collective-permute-start(bf16[9,2,2,16,128]{4,3,2,1,0:T(8,128)(2,1)} %get-tuple-element.9), channel_id=1, source_target_pairs={{0,2},{2,4},{4,6},{6,8},{8,10},{10,12},{12,14},{3,1},{5,3},{7,5},{... | collective-permute-start | bytes 442376 | tf_op jit(solution)/shard_map/ppermute | solution.py:534
  4.3 6.6 %collective-permute-start.2 = (bf16[9,2,2,16,128]{4,3,2,1,0:T(8,128)(2,1)}, bf16[9,2,2,16,128]{4,3,2,1,0:T(8,128)(2,1)S(1)}, u32[]{:S(2)}, u32[]{:S(2)}) collective-permute-start(bf16[9,2,2,16,128]{4,3,2,1,0:T(8,128)(2,1)} %get-tuple-element.10), channel_id=1, source_target_pairs={{1,2},{3,4},{5,6},{7,8},{9,10},{11,12},{13,14},{2,1},{4,3},{6,5},{... | collective-permute-start | bytes 442376 | tf_op jit(solution)/shard_map/ppermute | solution.py:535
  11.0 1.4 %copy.5.offset_ref = s32[32,4]{1,0:T(8,128)} copy(s32[32,4]{0,1:T(4,128)} %param.6) | data formatting | bytes 1024 | tf_op args[2]
  12.4 0.0 collective-permute-done.1.same_ref
  12.4 0.0 copy-start.1
  12.4 2.9 %collective-permute-done.2.cross_ref = bf16[9,2,2,16,128]{4,3,2,1,0:T(8,128)(2,1)S(1)} collective-permute-done((bf16[9,2,2,16,128]{4,3,2,1,0:T(8,128)(2,1)}, bf16[9,2,2,16,128]{4,3,2,1,0:T(8,128)(2,1)S(1)}, u32[]{:S(2)}, u32[]{:S(2)}) %collective-permute-start.2) | collective-permute-done | bytes 147488 | tf_op jit(solution)/shard_map/ppermute | solution.py:535
  15.3 0.0 copy-start.2
  15.3 0.0 collective-permute-done.partner_ref
  15.3 0.0 copy-done.1
  15.3 0.7 copy-done.2
  15.9 0.0 copy-start
  15.9 0.8 %copy-done = bf16[32,2,2,16,128]{4,3,2,1,0:T(8,128)(2,1)} copy-done((bf16[32,2,2,16,128]{4,3,2,1,0:T(8,128)(2,1)}, bf16[32,2,2,16,128]{4,3,2,1,0:T(8,128)(2,1)S(1)}, u32[]{:S(2)}) %copy-start) | copy-done | bytes 524312
  16.7 51.5 %solve.1 = f32[31,16,256]{2,1,0:T(8,128)} custom-call(bf16[32,2,2,16,128]{4,3,2,1,0:T(8,128)(2,1)} %get-tuple-element.8.own_ref, bf16[32,2,2,16,128]{4,3,2,1,0:T(8,128)(2,1)} %copy-done, bf16[9,2,2,16,128]{4,3,2,1,0:T(8,128)(2,1)} %copy-done.1, bf16[9,2,2,16,128]{4,3,2,1,0:T(8,128)(2,1)} %copy-done.2, s32[32,4]{1,0:T(8,128)} %copy.5.offset_ref, ...), custom_call_target="tpu_custom_call" | custom-call | tf_op jit(solution)/shard_map/solve/pallas_call | solution.py:512
Async XLA Ops:
  3.0 12.2 %collective-permute-start = (bf16[32,2,2,16,128]{4,3,2,1,0:T(8,128)(2,1)}, bf16[32,2,2,16,128]{4,3,2,1,0:T(8,128)(2,1)S(1)}, u32[]{:S(2)}, u32[]{:S(2)}) collective-permute-start(bf16[32,2,2,16,128]{4,3,2,1,0:T(8,128)(2,1)} %get-tuple-element.8.own_ref), channel_id=1, source_target_pairs={{0,1},{1,0},{2,3},{3,2},{4,5},{5,4},{6,7},{7,6},{8,9},{9,8},{10,11... | collective-permute-start | bytes 1572872 | tf_op jit(solution)/shard_map/ppermute | solution.py:536
  3.1 9.3 %collective-permute-start.1 = (bf16[9,2,2,16,128]{4,3,2,1,0:T(8,128)(2,1)}, bf16[9,2,2,16,128]{4,3,2,1,0:T(8,128)(2,1)S(1)}, u32[]{:S(2)}, u32[]{:S(2)}) collective-permute-start(bf16[9,2,2,16,128]{4,3,2,1,0:T(8,128)(2,1)} %get-tuple-element.9), channel_id=1, source_target_pairs={{0,2},{2,4},{4,6},{6,8},{8,10},{10,12},{12,14},{3,1},{5,3},{7,5},{... | collective-permute-start | bytes 442376 | tf_op jit(solution)/shard_map/ppermute | solution.py:534
  4.3 10.9 %collective-permute-start.2 = (bf16[9,2,2,16,128]{4,3,2,1,0:T(8,128)(2,1)}, bf16[9,2,2,16,128]{4,3,2,1,0:T(8,128)(2,1)S(1)}, u32[]{:S(2)}, u32[]{:S(2)}) collective-permute-start(bf16[9,2,2,16,128]{4,3,2,1,0:T(8,128)(2,1)} %get-tuple-element.10), channel_id=1, source_target_pairs={{1,2},{3,4},{5,6},{7,8},{9,10},{11,12},{13,14},{2,1},{4,3},{6,5},{... | collective-permute-start | bytes 442376 | tf_op jit(solution)/shard_map/ppermute | solution.py:535
  12.4 2.9 %copy-start.1 = (bf16[9,2,2,16,128]{4,3,2,1,0:T(8,128)(2,1)}, bf16[9,2,2,16,128]{4,3,2,1,0:T(8,128)(2,1)S(1)}, u32[]{:S(2)}) copy-start(bf16[9,2,2,16,128]{4,3,2,1,0:T(8,128)(2,1)S(1)} %collective-permute-done.1.same_ref) | copy-start | bytes 442372
  15.3 0.7 copy-start.2
  15.9 0.8 %copy-start = (bf16[32,2,2,16,128]{4,3,2,1,0:T(8,128)(2,1)}, bf16[32,2,2,16,128]{4,3,2,1,0:T(8,128)(2,1)S(1)}, u32[]{:S(2)}) copy-start(bf16[32,2,2,16,128]{4,3,2,1,0:T(8,128)(2,1)S(1)} %collective-permute-done.partner_ref) | copy-start | bytes 1572868

commit v2 on v1

--- a/solution.py
+++ b/solution.py
@@ -20,6 +20,9 @@
 
 LANES = 128
 SUB = 8
+CLASSES = 4
+GROUPS = 64
+UA, UB, UC, CK = 2, 2, 5, 2
 HALO = SWEEPS + 1
 F32 = jnp.float32
 BF16 = jnp.bfloat16
@@ -33,32 +36,50 @@
     return ref[pl.ds(row, SUB), :]
 
 
-def perm_matrix(transpose):
-    n = 2 * LANES
+def perm_matrix(transpose, swap=0):
+    n = CLASSES * GROUPS
     a = lax.broadcasted_iota(jnp.int32, (n, n), 0)
     b = lax.broadcasted_iota(jnp.int32, (n, n), 1)
     col, place = (b, a) if transpose else (a, b)
-    target = (col % 2) * LANES + col // 2
+    target = ((col % CLASSES) ^ swap) * GROUPS + col // CLASSES
     return jnp.where(place == target, 1.0, 0.0).astype(BF16)
 
 
 def pack_kernel(halo, re_ref, im_ref, all_ref, same_ref, cross_ref, flat):
     dates, rows, columns = re_ref.shape
     side = lax.axis_index("date")
-    perm = perm_matrix(False)
-    for part, ref in enumerate((re_ref, im_ref)):
-        block = ref[...].reshape(dates * rows, columns)
-        out = jnp.dot(block, perm, preferred_element_type=F32)
-        for half in range(2):
-            flat[part, half] = out[:, half * LANES : (half + 1) * LANES]
-    for row in range(rows):
-        for part in range(2):
+    perm = perm_matrix(False, side)
+    CH = 4
+
+    def permute(i, c):
+        for part, ref in enumerate((re_ref, im_ref)):
+            block = ref[pl.ds(i * CH, CH)].reshape(CH * rows, columns)
+            out = jnp.dot(block, perm, preferred_element_type=F32)
             for half in range(2):
-                tile = flat[part, half, pl.ds(row, dates, stride=rows), :]
-                all_ref[row, part, half] = tile.astype(BF16)
+                flat[part, half, pl.ds(al(i * CH * rows), CH * rows), :] = out[:, half * LANES : (half + 1) * LANES]
+        return c
+
+    lax.fori_loop(0, dates // CH, permute, 0)
+    RW = 4
+
+    def turn(i, c):
+        for u in range(RW):
+            row = i * RW + u
+            for part in range(2):
+                for half in range(2):
+                    tile = flat[part, half, pl.ds(row, dates, stride=rows), :]
+                    all_ref[row, part, half] = tile.astype(BF16)
+        return c
+
+    lax.fori_loop(0, rows // RW, turn, 0)
     last = rows - halo
-    same_ref[...] = all_ref[pl.ds(last * (1 - side), halo)]
-    cross_ref[...] = all_ref[pl.ds(last * side, halo)]
+
+    def send(i, c):
+        same_ref[i] = all_ref[last * (1 - side) + i]
+        cross_ref[i] = all_ref[last * side + i]
+        return c
+
+    lax.fori_loop(0, halo, send, 0)
 
 
 def pack(slc_real, slc_imag):
@@ -77,8 +98,8 @@
 
 def main_kernel(
     own_ref, partner_ref, same_ref, cross_ref, offset_ref, weight_hbm, out_hbm,
-    img, cre, cim, zre, zim, mag, hle, hlo, dh, sh, rr, ss, aa, ya, yb,
-    yy, wraw, wf, vv, aw, ag, wk, msk, vfin, obuf, wsem, osem,
+    img, cre, cim, zre, zim, mag, hle, hlo, dh, sh, rr, ss, aa, ya, yb, yc,
+    yy, wraw, wf, vv, aw, ag, wk, msk, lmsk, vfin, obuf, wsem, osem,
 ):
     half_dates = own_ref.shape[3]
     dates = 2 * half_dates
@@ -87,8 +108,9 @@
     H = HALO
     NR = R + 2 * H
     NZ = NR - 2
-    DP = dates + SUB
+    DP = half_dates + SUB
     NF = dates // SUB
+    NB = NF // 2
     side = lax.axis_index("date")
     tile = lax.axis_index("tile")
     tiles = lax.axis_size("tile")
@@ -114,25 +136,33 @@
         msk[2 + k] = jnp.broadcast_to(ok, (dates, LANES))
 
     lane = lax.broadcasted_iota(jnp.int32, (SUB, LANES), 1)
-    at_first = lane == 0
-    at_last = lane == LANES - 1
+    at_first = lane % GROUPS == 0
+    at_last = lane % GROUPS == GROUPS - 1
+    low = lane < GROUPS
     zero = jnp.zeros((SUB, LANES), F32)
+    low2 = lax.broadcasted_iota(jnp.int32, (half_dates, LANES), 1) < GROUPS
+    for n in range(2):
+        lmsk[n] = jnp.where(low2, msk[n, :half_dates], msk[n, half_dates:])
+    own2 = (lax.broadcasted_iota(jnp.int32, (half_dates, LANES), 1) // GROUPS) == side
+
+    def swap_halves(x):
+        return pltpu.roll(x, GROUPS, 1)
 
     third = 1.0 / 3.0
-    o_date = al(half_dates * side)
-    p_date = al(half_dates * (1 - side))
 
     def put(rho, o_tile_ref, o_row, p_tile_ref, p_row):
         for part in range(2):
-            for half in range(2):
-                base = ((rho * 2 + part) * 2 + half) * DP
-                img[pl.ds(al(base + o_date), half_dates), :] = (
-                    o_tile_ref[o_row, part, half].astype(F32) * third
-                )
-                img[pl.ds(al(base + p_date), half_dates), :] = (
-                    p_tile_ref[p_row, part, half].astype(F32) * third
-                )
-                img[pl.ds(al(base + dates), SUB), :] = zero
+            for pair in range(2):
+                mine = o_tile_ref[o_row, part, pair].astype(F32) * third
+                other = p_tile_ref[p_row, part, pair].astype(F32) * third
+                for odd in range(2):
+                    if odd:
+                        x = swap_halves(jnp.where(own2, other, mine))
+                    else:
+                        x = jnp.where(own2, mine, other)
+                    base = ((rho * 2 + part) * CLASSES + pair * 2 + odd) * DP
+                    img[pl.ds(al(base), half_dates), :] = x
+                    img[pl.ds(al(base + half_dates), SUB), :] = jnp.where(low, swap_halves(x[:SUB]), 0.0)
 
     base_row = (R - H) * side
     base_rho = H * (1 - side)
@@ -156,38 +186,43 @@
     def roll_left(x):
         return pltpu.roll(x, LANES - 1, 1)
 
-    def gix(row, k, half):
-        return al(((row * K + k) * 2 + half) * SUB)
+    def gix(row, k, cls):
+        return al(((row * K + k) * CLASSES + cls) * SUB)
 
     def block(ft, carry):
         f0 = al(ft * SUB)
-        sel1 = vreg(msk.at[0], f0) > 0.5
-        sel2 = vreg(msk.at[1], f0) > 0.5
 
         def form(rho):
-            def image(part, half, shift):
-                return vreg(img, ((rho * 2 + part) * 2 + half) * DP + f0 + shift)
+            sel1 = vreg(lmsk.at[0], f0) > 0.5
+            sel2 = vreg(lmsk.at[1], f0) > 0.5
+
+            def image(part, cls, shift):
+                return vreg(img, ((rho * 2 + part) * CLASSES + cls) * DP + f0 + shift)
 
             pair = {}
-            for half in range(2):
-                a_re, a_im = image(0, half, 0), image(1, half, 0)
-                second = [(image(0, half, o), image(1, half, o)) for o in range(1, SPAN + 1)]
+            for cls in range(CLASSES):
+                a_re, a_im = image(0, cls, 0), image(1, cls, 0)
+                second = [(image(0, cls, o), image(1, cls, o)) for o in range(1, SPAN + 1)]
                 pick = lambda mask, i, j: tuple(
                     jnp.where(mask, x, y) for x, y in zip(second[i - 1], second[j - 1])
                 )
                 chosen = (second[0], pick(sel1, 2, 3), pick(sel2, 4, 3), second[4])
                 for k in range(K):
                     b_re, b_im = chosen[k]
-                    pair[0, k, half] = a_re * b_re + a_im * b_im
-                    pair[1, k, half] = a_im * b_re - a_re * b_im
+                    pair[0, k, cls] = a_re * b_re + a_im * b_im
+                    pair[1, k, cls] = a_im * b_re - a_re * b_im
             for part, ref in enumerate((cre, cim)):
                 for k in range(K):
-                    even, odd = pair[part, k, 0], pair[part, k, 1]
-                    both = even + odd
-                    ref[pl.ds(gix(rho, k, 0), SUB), :] = both + jnp.where(at_first, 0.0, roll_right(odd))
-                    ref[pl.ds(gix(rho, k, 1), SUB), :] = both + jnp.where(at_last, 0.0, roll_left(even))
-
-        UA = 2
+                    x = [pair[part, k, cls] for cls in range(CLASSES)]
+                    x01, x23 = x[0] + x[1], x[2] + x[3]
+                    sums = (
+                        x01 + jnp.where(at_first, 0.0, roll_right(x[3])),
+                        x01 + x[2],
+                        x[1] + x23,
+                        x23 + jnp.where(at_last, 0.0, roll_left(x[0])),
+                    )
+                    for cls in range(CLASSES):
+                        ref[pl.ds(gix(rho, k, cls), SUB), :] = sums[cls]
 
         def phase_a(i, c):
             for u in range(UA):
@@ -204,35 +239,43 @@
             return link, link * (cross * q)
 
         def smooth(j):
-            z = {}
             for k in range(K):
-                for half in range(2):
-                    i0, i1, i2 = (gix(j + d, k, half) for d in range(3))
-                    re = vreg(cre, i0) + vreg(cre, i1) + vreg(cre, i2)
-                    im = vreg(cim, i0) + vreg(cim, i1) + vreg(cim, i2)
-                    sq = re * re + im * im
-                    mg = sq * lax.rsqrt(jnp.maximum(sq, 1e-30))
-                    zre[pl.ds(i0, SUB), :] = re
-                    zim[pl.ds(i0, SUB), :] = im
-                    mag[pl.ds(i0, SUB), :] = mg
-                    z[k, half] = re, im, mg
-            for k in range(K):
-                e_re, e_im, e_mg = z[k, 0]
-                o_re, o_im, o_mg = z[k, 1]
-                le, ge = edge(e_mg * o_mg, e_im * o_re - e_re * o_im, column_weight)
-                n_re, n_im, n_mg = roll_left(e_re), roll_left(e_im), roll_left(e_mg)
-                m = jnp.where(at_last, 0.0, o_mg * n_mg)
-                lo, go = edge(m, o_im * n_re - o_re * n_im, column_weight)
-                i0, i1 = gix(j, k, 0), gix(j, k, 1)
-                damped = le + unwrap_damping
-                hle[pl.ds(i0, SUB), :] = le
-                hle[pl.ds(i1, SUB), :] = lo
-                dh[pl.ds(i0, SUB), :] = damped + roll_right(lo)
-                dh[pl.ds(i1, SUB), :] = damped + lo
-                sh[pl.ds(i0, SUB), :] = ge - roll_right(go)
-                sh[pl.ds(i1, SUB), :] = go - ge
-
-        UB = 2
+                re, im, mg = [], [], []
+                for cls in range(CLASSES):
+                    i0, i1, i2 = (gix(j + d, k, cls) for d in range(3))
+                    x = vreg(cre, i0) + vreg(cre, i1) + vreg(cre, i2)
+                    y = vreg(cim, i0) + vreg(cim, i1) + vreg(cim, i2)
+                    sq = x * x + y * y
+                    m = sq * lax.rsqrt(jnp.maximum(sq, 1e-30))
+                    zre[pl.ds(i0, SUB), :] = x
+                    zim[pl.ds(i0, SUB), :] = y
+                    mag[pl.ds(i0, SUB), :] = m
+                    re.append(x)
+                    im.append(y)
+                    mg.append(m)
+                links, flows = [], []
+                for cls in range(CLASSES):
+                    if cls < CLASSES - 1:
+                        n_re, n_im, m = re[cls + 1], im[cls + 1], mg[cls] * mg[cls + 1]
+                    else:
+                        n_re, n_im = roll_left(re[0]), roll_left(im[0])
+                        m = jnp.where(at_last, 0.0, mg[cls] * roll_left(mg[0]))
+                    link, flow = edge(m, im[cls] * n_re - re[cls] * n_im, column_weight)
+                    hle[pl.ds(gix(j, k, cls), SUB), :] = link
+                    links.append(link)
+                    flows.append(flow)
+                mid = links[1] + unwrap_damping
+                end = links[3] + unwrap_damping
+                dens = (links[0] + roll_right(end), links[0] + mid, mid + links[2], links[2] + end)
+                srcs = (
+                    flows[0] - roll_right(flows[3]),
+                    flows[1] - flows[0],
+                    flows[2] - flows[1],
+                    flows[3] - flows[2],
+                )
+                for cls in range(CLASSES):
+                    dh[pl.ds(gix(j, k, cls), SUB), :] = dens[cls]
+                    sh[pl.ds(gix(j, k, cls), SUB), :] = srcs[cls]
 
         def phase_b(i, c):
             for u in range(UB):
@@ -244,89 +287,114 @@
         @pl.when((tile == 0) & (side == 0))
         def _():
             for k in range(K):
-                for half in range(2):
-                    mag[pl.ds(gix(H - 2, k, half), SUB), :] = zero
+                for cls in range(CLASSES):
+                    mag[pl.ds(gix(H - 2, k, cls), SUB), :] = zero
 
         @pl.when((tile == tiles - 1) & (side == 1))
         def _():
             for k in range(K):
-                for half in range(2):
-                    mag[pl.ds(gix(H - 1 + R, k, half), SUB), :] = zero
-
-        def vertical(j, k, half):
-            i0, i1 = gix(j, k, half), gix(j + 1, k, half)
+                for cls in range(CLASSES):
+                    mag[pl.ds(gix(H - 1 + R, k, cls), SUB), :] = zero
+
+        def vertical(j, k, cls):
+            i0, i1 = gix(j, k, cls), gix(j + 1, k, cls)
             m = vreg(mag, i0) * vreg(mag, i1)
             return edge(m, vreg(zim, i0) * vreg(zre, i1) - vreg(zre, i0) * vreg(zim, i1), None)
 
-        start = []
-        for k in range(K):
-            for half in range(2):
-                start += [*vertical(0, k, half), zero]
-
-        def stencil(j, before):
+        def stencil(j, ks, before):
             after = []
-            for k in range(K):
-                root = {}
-                for half in range(2):
-                    i0 = gix(j, k, half)
-                    v, f = vertical(j, k, half)
-                    n = (k * 2 + half) * 3
+            n = 0
+            for k in ks:
+                root = []
+                for cls in range(CLASSES):
+                    i0 = gix(j, k, cls)
+                    v, f = vertical(j, k, cls)
                     vm, fm, rm = before[n : n + 3]
+                    n += 3
                     den = vreg(dh, i0) + vm + v
                     src = vreg(sh, i0) + f - fm
                     r = lax.rsqrt(den)
                     rr[pl.ds(i0, SUB), :] = r
                     ss[pl.ds(i0, SUB), :] = src * r
                     aa[pl.ds(i0, SUB), :] = vm * (r * rm)
-                    root[half] = r
+                    root.append(r)
                     after += [v, f, r]
-                i0, i1 = gix(j, k, 0), gix(j, k, 1)
-                hlo[pl.ds(i0, SUB), :] = vreg(hle, i0) * (root[0] * root[1])
-                hlo[pl.ds(i1, SUB), :] = vreg(hle, i1) * (root[1] * roll_left(root[0]))
+                for cls in range(CLASSES):
+                    other = root[cls + 1] if cls < CLASSES - 1 else roll_left(root[0])
+                    i0 = gix(j, k, cls)
+                    hlo[pl.ds(i0, SUB), :] = vreg(hle, i0) * (root[cls] * other)
             return after
 
-        UC = 2
-
-        def phase_c(i, c):
-            for u in range(UC):
-                c = stencil(1 + i * UC + u, c)
-            return tuple(c)
-
-        lax.fori_loop(0, (NZ - 2) // UC, phase_c, tuple(start))
+        def phase_c(ks):
+            def body(i, c):
+                for u in range(UC):
+                    c = stencil(1 + i * UC + u, ks, c)
+                return tuple(c)
+
+            start = []
+            for k in ks:
+                for cls in range(CLASSES):
+                    start += [*vertical(0, k, cls), zero]
+            lax.fori_loop(0, (NZ - 2) // UC, body, tuple(start))
+
+        for k in range(0, K, CK):
+            phase_c(range(k, k + CK))
 
         def sweeps(k, c):
-            src_ref = ss
-            for s in range(1, SWEEPS):
-                left = SWEEPS - 1 - s
-                dst_ref = (ya, yb)[s % 2]
-                lo, hi = H - 1 - left, H - 1 + R + left
-                for j in range(lo, hi):
-                    y = [[vreg(src_ref, gix(j + d, k, half)) for half in range(2)] for d in (-1, 0, 1)]
-                    i0, i1 = gix(j, k, 0), gix(j, k, 1)
-                    e, o = vreg(hlo, i0), vreg(hlo, i1)
+            steps = []
+            buffers = [ya, yb, yc]
+            held = ss
+            power = SWEEPS // 2
+            while power >= 1:
+                source = held
+                for n in range(power):
+                    free = [x for x in buffers if x is not source and x is not held]
+                    steps.append((source, held if n == power - 1 else None, free[0]))
+                    source = free[0]
+                held = source
+                power //= 2
+            for n, (source, added, target) in enumerate(steps):
+                left = len(steps) - 1 - n
+                for j in range(H - 1 - left, H - 1 + R + left):
+                    y = [
+                        [vreg(source, gix(j + d, k, cls)) for cls in range(CLASSES)] for d in (-1, 0, 1)
+                    ]
+                    h = [vreg(hlo, gix(j, k, cls)) for cls in range(CLASSES)]
+                    right = [h[cls] * y[1][cls + 1] for cls in range(CLASSES - 1)] + [h[3] * roll_left(y[1][0])]
+                    back = [roll_right(h[3] * y[1][3])] + [h[cls] * y[1][cls] for cls in range(CLASSES - 1)]
                     new = []
-                    for half in range(2):
-                        i = (i0, i1)[half]
-                        up, dn = vreg(aa, i), vreg(aa, gix(j + 1, k, half))
-                        new.append(vreg(ss, i) + up * y[0][half] + dn * y[2][half])
-                    even = new[0] + e * y[1][1] + roll_right(o * y[1][1])
-                    odd = new[1] + e * y[1][0] + o * roll_left(y[1][0])
-                    if s < SWEEPS - 1:
-                        dst_ref[pl.ds(i0, SUB), :] = even
-                        dst_ref[pl.ds(i1, SUB), :] = odd
+                    for cls in range(CLASSES):
+                        i0 = gix(j, k, cls)
+                        x = vreg(aa, i0) * y[0][cls] + vreg(aa, gix(j + 1, k, cls)) * y[2][cls]
+                        if added is not None:
+                            x = x + (y[1][cls] if added is source else vreg(added, i0))
+                        if cls in (0, CLASSES - 1):
+                            x = (x + right[cls]) + back[cls] if cls == 0 else (x + back[cls]) + right[cls]
+                        else:
+                            x = x + (right[cls] + back[cls])
+                        new.append(x)
+                    if left:
+                        for cls in range(CLASSES):
+                            target[pl.ds(gix(j, k, cls), SUB), :] = new[cls]
                     else:
                         row = j - (H - 1)
-                        for half, value in enumerate((even, odd)):
-                            r = vreg(rr, gix(j, k, half)) * (1.0 / residual_scale)
-                            place = (((row * K + k) * NF + ft) * 2 + half) * SUB
-                            yy[pl.ds(al(place), SUB), :] = value * r
-                src_ref = dst_ref
+                        u = [
+                            new[cls] * (vreg(rr, gix(j, k, cls)) * (1.0 / residual_scale))
+                            for cls in range(CLASSES)
+                        ]
+                        for pair in range(2):
+                            even, odd = u[2 * pair], u[2 * pair + 1]
+                            first = jnp.where(low, even, swap_halves(odd))
+                            second = jnp.where(low, swap_halves(even), odd)
+                            for upper, value in enumerate((first, second)):
+                                place = (((row * K + k) * NF + upper * NB + ft) * 2 + pair) * SUB
+                                yy[pl.ds(al(place), SUB), :] = value
             return c
 
         lax.fori_loop(0, K, sweeps, 0)
         return carry
 
-    lax.fori_loop(0, NF, block, 0)
+    lax.fori_loop(0, NB, block, 0)
 
     for copy in copies:
         copy.wait()
@@ -483,27 +551,28 @@
     NR = R + 2 * H
     NZ = NR - 2
     NF = dates // SUB
-    group = K * 2 * SUB
+    group = K * CLASSES * SUB
     vm = pl.BlockSpec(memory_space=pltpu.VMEM)
     hbm = pl.BlockSpec(memory_space=pl.ANY)
     U = 1
     v2 = lambda rows: pltpu.VMEM((rows, LANES), F32)
     scratch = [
-        v2(NR * 4 * (dates + SUB)),
+        v2(NR * 2 * CLASSES * (dates // 2 + SUB)),
         v2(NR * group), v2(NR * group),
         v2(NZ * group), v2(NZ * group), v2(NZ * group),
         v2(NZ * group), v2(NZ * group),
         v2(NZ * group), v2(NZ * group),
         v2(NZ * group), v2(NZ * group), v2(NZ * group),
-        v2(NZ * group), v2(NZ * group),
-        v2(R * NF * group),
+        v2(NZ * group), v2(NZ * group), v2(NZ * group),
+        v2(R * NF * K * 2 * SUB),
         pltpu.VMEM((2, pairs, R, LANES), jnp.int32),
-        v2(R * NF * group),
+        v2(R * NF * K * 2 * SUB),
         pltpu.VMEM((U, 2, dates + SUB, LANES), F32),
         pltpu.VMEM((U, 2, SPAN, dates + SUB, LANES), F32),
         pltpu.VMEM((U, 2, SPAN, dates + SUB, LANES), F32),
         pltpu.VMEM((U, NF, 2, K, SUB, LANES), F32),
         pltpu.VMEM((2 + K, dates, LANES), F32),
+        pltpu.VMEM((2, dates // 2, LANES), F32),
         pltpu.VMEM((R, 2, dates, LANES), F32),
         pltpu.VMEM((2, dates, R, LANES), F32),
         pltpu.SemaphoreType.DMA((2,)),

time: 68.4 us -> 56.6 us (0.83)
  Pallas kernels: 54.5 us -> 42.7 us
    pallas_call x1, Pallas kernels: 51.5 us -> 39.2 us  [solve(): pl.pallas_call(main_kernel, out_shape=jax.ShapeDtypeStruct((dates - 1, R,...]
where the time goes in v2:
time: 56.6 us; the launch traced here: 56.4 us
  Pallas kernels  42.7 us (75%)
  starting transfers between devices  7.95 us (14%)
  waiting for transfers between devices  2.9 us (5%)
  local copies, waits for them, and re-layouts  2.81 us (5%)
    pallas_call x1, Pallas kernels, solve(): pl.pallas_call(main_kernel, out_shape=jax.ShapeDtypeStruct((dates - 1, R,...  39.2 us
    ppermute x1, starting transfers between devices, local(): cross = lax.ppermute(cross, axes, to_cross)  6.65 us
    pallas_call x1, Pallas kernels, pack(): pl.pallas_call(functools.partial(pack_kernel, HALO), out_shape=(shape(row...  3.52 us
    ppermute x1, waiting for transfers between devices, local(): cross = lax.ppermute(cross, axes, to_cross)  2.9 us
    unnamed x7, local copies, waits for them, and re-layouts  2.81 us
    ppermute x1, starting transfers between devices, local(): same = lax.ppermute(same, axes, to_same)  1.28 us
  transfers between devices with their start and end apart: 3, of which 1 were waited for; matrix products, arithmetic and copies ran while one was open for 2% of the time, Pallas kernels for 0%

profile of v2, /device:TPU:1, one launch (start us, length us, event | category | flops | bytes accessed | tf_op | source)
XLA Modules:
  0.0 56.4 jit_solution(11057340759958628837)
XLA Ops:
  0.0 3.5 %pack.1 = (bf16[32,2,2,16,128]{4,3,2,1,0:T(8,128)(2,1)}, bf16[9,2,2,16,128]{4,3,2,1,0:T(8,128)(2,1)}, bf16[9,2,2,16,128]{4,3,2,1,0:T(8,128)(2,1)}) custom-call(bf16[16,32,256]{2,1,0:T(8,128)(2,1)} %re_ref.1, bf16[16,32,256]{2,1,0:T(8,128)(2,1)} %im_ref.1), custom_call_target="tpu_custom_call" | custom-call | tf_op jit(solution)/shard_map/pack/pallas_call | solution.py:89
  3.5 0.0 collective-permute-start
  3.5 1.3 %collective-permute-start.1 = (bf16[9,2,2,16,128]{4,3,2,1,0:T(8,128)(2,1)}, bf16[9,2,2,16,128]{4,3,2,1,0:T(8,128)(2,1)S(1)}, u32[]{:S(2)}, u32[]{:S(2)}) collective-permute-start(bf16[9,2,2,16,128]{4,3,2,1,0:T(8,128)(2,1)} %get-tuple-element.9), channel_id=1, source_target_pairs={{0,2},{2,4},{4,6},{6,8},{8,10},{10,12},{12,14},{3,1},{5,3},{7,5},{... | collective-permute-start | bytes 442376 | tf_op jit(solution)/shard_map/ppermute | solution.py:603
  4.8 6.6 %collective-permute-start.2 = (bf16[9,2,2,16,128]{4,3,2,1,0:T(8,128)(2,1)}, bf16[9,2,2,16,128]{4,3,2,1,0:T(8,128)(2,1)S(1)}, u32[]{:S(2)}, u32[]{:S(2)}) collective-permute-start(bf16[9,2,2,16,128]{4,3,2,1,0:T(8,128)(2,1)} %get-tuple-element.10), channel_id=1, source_target_pairs={{1,2},{3,4},{5,6},{7,8},{9,10},{11,12},{13,14},{2,1},{4,3},{6,5},{... | collective-permute-start | bytes 442376 | tf_op jit(solution)/shard_map/ppermute | solution.py:604
  11.5 1.4 %copy.5.offset_ref = s32[32,4]{1,0:T(8,128)} copy(s32[32,4]{0,1:T(4,128)} %param.6) | data formatting | bytes 1024 | tf_op args[2]
  12.8 0.0 collective-permute-done.1.same_ref
  12.8 0.0 copy-start.1
  12.8 2.9 %collective-permute-done.2.cross_ref = bf16[9,2,2,16,128]{4,3,2,1,0:T(8,128)(2,1)S(1)} collective-permute-done((bf16[9,2,2,16,128]{4,3,2,1,0:T(8,128)(2,1)}, bf16[9,2,2,16,128]{4,3,2,1,0:T(8,128)(2,1)S(1)}, u32[]{:S(2)}, u32[]{:S(2)}) %collective-permute-start.2) | collective-permute-done | bytes 147488 | tf_op jit(solution)/shard_map/ppermute | solution.py:604
  15.7 0.0 copy-start.2
  15.7 0.0 collective-permute-done.partner_ref
  15.7 0.0 copy-done.1
  15.8 0.7 %copy-done.2 = bf16[9,2,2,16,128]{4,3,2,1,0:T(8,128)(2,1)} copy-done((bf16[9,2,2,16,128]{4,3,2,1,0:T(8,128)(2,1)}, bf16[9,2,2,16,128]{4,3,2,1,0:T(8,128)(2,1)S(1)}, u32[]{:S(2)}) %copy-start.2) | copy-done | bytes 147480
  16.4 0.0 copy-start
  16.4 0.8 %copy-done = bf16[32,2,2,16,128]{4,3,2,1,0:T(8,128)(2,1)} copy-done((bf16[32,2,2,16,128]{4,3,2,1,0:T(8,128)(2,1)}, bf16[32,2,2,16,128]{4,3,2,1,0:T(8,128)(2,1)S(1)}, u32[]{:S(2)}) %copy-start) | copy-done | bytes 524312
  17.2 39.2 %solve.1 = f32[31,16,256]{2,1,0:T(8,128)} custom-call(bf16[32,2,2,16,128]{4,3,2,1,0:T(8,128)(2,1)} %get-tuple-element.8.own_ref, bf16[32,2,2,16,128]{4,3,2,1,0:T(8,128)(2,1)} %copy-done, bf16[9,2,2,16,128]{4,3,2,1,0:T(8,128)(2,1)} %copy-done.1, bf16[9,2,2,16,128]{4,3,2,1,0:T(8,128)(2,1)} %copy-done.2, s32[32,4]{1,0:T(8,128)} %copy.5.offset_ref, ...), custom_call_target="tpu_custom_call" | custom-call | tf_op jit(solution)/shard_map/solve/pallas_call | solution.py:581
Async XLA Ops:
  3.5 12.2 %collective-permute-start = (bf16[32,2,2,16,128]{4,3,2,1,0:T(8,128)(2,1)}, bf16[32,2,2,16,128]{4,3,2,1,0:T(8,128)(2,1)S(1)}, u32[]{:S(2)}, u32[]{:S(2)}) collective-permute-start(bf16[32,2,2,16,128]{4,3,2,1,0:T(8,128)(2,1)} %get-tuple-element.8.own_ref), channel_id=1, source_target_pairs={{0,1},{1,0},{2,3},{3,2},{4,5},{5,4},{6,7},{7,6},{8,9},{9,8},{10,11... | collective-permute-start | bytes 1572872 | tf_op jit(solution)/shard_map/ppermute | solution.py:605
  3.5 9.3 %collective-permute-start.1 = (bf16[9,2,2,16,128]{4,3,2,1,0:T(8,128)(2,1)}, bf16[9,2,2,16,128]{4,3,2,1,0:T(8,128)(2,1)S(1)}, u32[]{:S(2)}, u32[]{:S(2)}) collective-permute-start(bf16[9,2,2,16,128]{4,3,2,1,0:T(8,128)(2,1)} %get-tuple-element.9), channel_id=1, source_target_pairs={{0,2},{2,4},{4,6},{6,8},{8,10},{10,12},{12,14},{3,1},{5,3},{7,5},{... | collective-permute-start | bytes 442376 | tf_op jit(solution)/shard_map/ppermute | solution.py:603
  4.8 10.9 %collective-permute-start.2 = (bf16[9,2,2,16,128]{4,3,2,1,0:T(8,128)(2,1)}, bf16[9,2,2,16,128]{4,3,2,1,0:T(8,128)(2,1)S(1)}, u32[]{:S(2)}, u32[]{:S(2)}) collective-permute-start(bf16[9,2,2,16,128]{4,3,2,1,0:T(8,128)(2,1)} %get-tuple-element.10), channel_id=1, source_target_pairs={{1,2},{3,4},{5,6},{7,8},{9,10},{11,12},{13,14},{2,1},{4,3},{6,5},{... | collective-permute-start | bytes 442376 | tf_op jit(solution)/shard_map/ppermute | solution.py:604
  12.8 2.9 %copy-start.1 = (bf16[9,2,2,16,128]{4,3,2,1,0:T(8,128)(2,1)}, bf16[9,2,2,16,128]{4,3,2,1,0:T(8,128)(2,1)S(1)}, u32[]{:S(2)}) copy-start(bf16[9,2,2,16,128]{4,3,2,1,0:T(8,128)(2,1)S(1)} %collective-permute-done.1.same_ref) | copy-start | bytes 442372
  15.7 0.7 %copy-start.2 = (bf16[9,2,2,16,128]{4,3,2,1,0:T(8,128)(2,1)}, bf16[9,2,2,16,128]{4,3,2,1,0:T(8,128)(2,1)S(1)}, u32[]{:S(2)}) copy-start(bf16[9,2,2,16,128]{4,3,2,1,0:T(8,128)(2,1)S(1)} %collective-permute-done.2.cross_ref) | copy-start | bytes 442372
  16.4 0.8 %copy-start = (bf16[32,2,2,16,128]{4,3,2,1,0:T(8,128)(2,1)}, bf16[32,2,2,16,128]{4,3,2,1,0:T(8,128)(2,1)S(1)}, u32[]{:S(2)}) copy-start(bf16[32,2,2,16,128]{4,3,2,1,0:T(8,128)(2,1)S(1)} %collective-permute-done.partner_ref) | copy-start | bytes 1572868

commit v3 on v2

--- a/solution.py
+++ b/solution.py
@@ -22,6 +22,7 @@
 SUB = 8
 CLASSES = 4
 GROUPS = 64
+UI, UH, UW, UO = 5, 3, 8, 4
 UA, UB, UC, CK = 2, 2, 5, 2
 HALO = SWEEPS + 1
 F32 = jnp.float32
@@ -45,18 +46,22 @@
     return jnp.where(place == target, 1.0, 0.0).astype(BF16)
 
 
-def pack_kernel(halo, re_ref, im_ref, all_ref, same_ref, cross_ref, flat):
+def pack_kernel(halo, re_ref, im_ref, all_ref, same_ref, cross_ref, flat, perm_ref):
     dates, rows, columns = re_ref.shape
     side = lax.axis_index("date")
-    perm = perm_matrix(False, side)
+    perm_ref[...] = perm_matrix(False, side)
     CH = 4
+    pitch = rows + 1
 
     def permute(i, c):
         for part, ref in enumerate((re_ref, im_ref)):
             block = ref[pl.ds(i * CH, CH)].reshape(CH * rows, columns)
-            out = jnp.dot(block, perm, preferred_element_type=F32)
-            for half in range(2):
-                flat[part, half, pl.ds(al(i * CH * rows), CH * rows), :] = out[:, half * LANES : (half + 1) * LANES]
+            out = jnp.dot(block, perm_ref[...], preferred_element_type=F32)
+            for n in range(CH):
+                for half in range(2):
+                    flat[part, half, pl.ds((i * CH + n) * pitch, rows), :] = out[
+                        n * rows : (n + 1) * rows, half * LANES : (half + 1) * LANES
+                    ]
         return c
 
     lax.fori_loop(0, dates // CH, permute, 0)
@@ -67,7 +72,7 @@
             row = i * RW + u
             for part in range(2):
                 for half in range(2):
-                    tile = flat[part, half, pl.ds(row, dates, stride=rows), :]
+                    tile = flat[part, half, pl.ds(row, dates, stride=pitch), :]
                     all_ref[row, part, half] = tile.astype(BF16)
         return c
 
@@ -91,7 +96,7 @@
         out_shape=(shape(rows), shape(HALO), shape(HALO)),
         in_specs=[vm, vm],
         out_specs=(vm, vm, vm),
-        scratch_shapes=[pltpu.VMEM((2, 2, dates * rows, LANES), F32)],
+        scratch_shapes=[pltpu.VMEM((2, 2, dates * (rows + 1), LANES), F32), pltpu.VMEM((columns, columns), BF16)],
         name="pack",
     )(slc_real, slc_imag)
 
@@ -99,7 +104,7 @@
 def main_kernel(
     own_ref, partner_ref, same_ref, cross_ref, offset_ref, weight_hbm, out_hbm,
     img, cre, cim, zre, zim, mag, hle, hlo, dh, sh, rr, ss, aa, ya, yb, yc,
-    yy, wraw, wf, vv, aw, ag, wk, msk, lmsk, vfin, obuf, wsem, osem,
+    yy, wraw, wf, vv, aw, ag, wk, msk, lmsk, vfin, fbuf, obuf, perm_ref, wsem, osem,
 ):
     half_dates = own_ref.shape[3]
     dates = 2 * half_dates
@@ -168,17 +173,21 @@
     base_rho = H * (1 - side)
 
     def put_tile(i, c):
-        put(base_rho + i, own_ref, base_row + i, partner_ref, base_row + i)
-        return c
-
-    lax.fori_loop(0, R + H, put_tile, 0)
+        for u in range(UI):
+            n = i * UI + u
+            put(base_rho + n, own_ref, base_row + n, partner_ref, base_row + n)
+        return c
+
+    lax.fori_loop(0, (R + H) // UI, put_tile, 0)
     halo_rho = (R + H) * side
 
     def put_halo(i, c):
-        put(halo_rho + i, same_ref, i, cross_ref, i)
-        return c
-
-    lax.fori_loop(0, H, put_halo, 0)
+        for u in range(UH):
+            n = i * UH + u
+            put(halo_rho + n, same_ref, n, cross_ref, n)
+        return c
+
+    lax.fori_loop(0, H // UH, put_halo, 0)
 
     def roll_right(x):
         return pltpu.roll(x, 1, 1)
@@ -355,17 +364,21 @@
                 power //= 2
             for n, (source, added, target) in enumerate(steps):
                 left = len(steps) - 1 - n
+                classes = range(CLASSES)
+                get = lambda ref, row: [vreg(ref, gix(row, k, cls)) for cls in classes]
+                top = H - 1 - left
+                y = [None, get(source, top - 1), get(source, top)]
+                links = [None, get(aa, top)]
                 for j in range(H - 1 - left, H - 1 + R + left):
-                    y = [
-                        [vreg(source, gix(j + d, k, cls)) for cls in range(CLASSES)] for d in (-1, 0, 1)
-                    ]
+                    y = [y[1], y[2], get(source, j + 1)]
+                    links = [links[1], get(aa, j + 1)]
                     h = [vreg(hlo, gix(j, k, cls)) for cls in range(CLASSES)]
                     right = [h[cls] * y[1][cls + 1] for cls in range(CLASSES - 1)] + [h[3] * roll_left(y[1][0])]
                     back = [roll_right(h[3] * y[1][3])] + [h[cls] * y[1][cls] for cls in range(CLASSES - 1)]
                     new = []
                     for cls in range(CLASSES):
                         i0 = gix(j, k, cls)
-                        x = vreg(aa, i0) * y[0][cls] + vreg(aa, gix(j + 1, k, cls)) * y[2][cls]
+                        x = links[0][cls] * y[0][cls] + links[1][cls] * y[2][cls]
                         if added is not None:
                             x = x + (y[1][cls] if added is source else vreg(added, i0))
                         if cls in (0, CLASSES - 1):
@@ -398,28 +411,34 @@
 
     for copy in copies:
         copy.wait()
-    perm = perm_matrix(False)
-
-    def weights(row, c):
-        rows = []
-        for k in range(K):
-            halves = [
-                wraw.at[half].reshape(K * dates * R, LANES)[pl.ds(k * R + row, dates, stride=K * R), :]
-                for half in range(2)
-            ]
-            rows.append(jnp.concatenate(halves, axis=1).astype(F32).astype(BF16))
-        out = jnp.dot(jnp.concatenate(rows, axis=0), perm, preferred_element_type=F32)
+    perm_ref[...] = perm_matrix(False)
+    pairs = K * dates
+    WR = K * NF * 2 * SUB + 1
+
+    def weights(i, c):
+        p0 = i * UW
+        rows = [
+            wraw[half, pl.ds(p0, UW)].reshape(UW * R, LANES).astype(F32).astype(BF16) for half in range(2)
+        ]
+        out = jnp.dot(jnp.concatenate(rows, axis=1), perm_ref[...], preferred_element_type=F32)
+        for n in range(UW):
+            f, k = i * (UW // K) + n // K, n % K
+            t, sub = f // SUB, f % SUB
+            for block in range(R // SUB):
+                for half in range(2):
+                    x = out[n * R + block * SUB : n * R + (block + 1) * SUB, half * LANES : (half + 1) * LANES]
+                    place = ((k * NF + t) * 2 + half) * SUB + sub + block * SUB * WR
+                    wf[pl.ds(place, SUB, stride=WR), :] = x
+        return c
+
+    lax.fori_loop(0, pairs // UW, weights, 0)
+    for row in range(R):
         for k in range(K):
             for t in range(NF):
-                for half in range(2):
-                    place = (((row * K + k) * NF + t) * 2 + half) * SUB
-                    x = out[(k * NF + t) * SUB : (k * NF + t + 1) * SUB, half * LANES : (half + 1) * LANES]
-                    if (t + 1) * SUB + SPAN - 1 >= dates:
-                        x = x * msk[2 + k, pl.ds(t * SUB, SUB), :]
-                    wf[pl.ds(al(place), SUB), :] = x
-        return c
-
-    lax.fori_loop(0, R, weights, 0)
+                if (t + 1) * SUB + SPAN - 1 >= dates:
+                    for half in range(2):
+                        place = row * WR + ((k * NF + t) * 2 + half) * SUB
+                        wf[pl.ds(place, SUB), :] = wf[pl.ds(place, SUB), :] * msk[2 + k, pl.ds(t * SUB, SUB), :]
 
     damping = solve_damping * 255.0
     inv_span = 1.0 / SPAN
@@ -480,7 +499,7 @@
                         w_all = []
                         for k in range(K):
                             if step == 0:
-                                place = al((((row * K + k) * NF + t) * 2 + half) * SUB)
+                                place = row * WR + ((k * NF + t) * 2 + half) * SUB
                                 w = vreg(wf, place) * (1.0 / (1.0 + res[k] * res[k]))
                                 wk[u, t, half, k] = w
                                 w_all.append(w)
@@ -509,25 +528,35 @@
 
     lax.fori_loop(0, R // U, invert_rows, 0)
 
-    back = perm_matrix(True)
+    perm_ref[...] = perm_matrix(True)
     unknowns = dates - 1
-
-    def finish(row, c):
-        value = jnp.concatenate([vfin[row, 0], vfin[row, 1]], axis=1)
-        high = value.astype(BF16)
-        rest = value - high.astype(F32)
-        mid = rest.astype(BF16)
-        low = (rest - mid.astype(F32)).astype(BF16)
-        stack = jnp.concatenate([high, mid, low], axis=0)
-        out = jnp.dot(stack, back, preferred_element_type=F32)
-        out = out[:dates] + out[dates : 2 * dates] + out[2 * dates :]
+    OP = dates + 1
+
+    def finish(i, c):
+        split = [[], [], []]
+        for u in range(UO):
+            rest = jnp.concatenate([vfin[i * UO + u, 0], vfin[i * UO + u, 1]], axis=1)
+            for part in split:
+                part.append(rest.astype(BF16))
+                rest = rest - part[-1].astype(F32)
+        stack = jnp.concatenate(split[0] + split[1] + split[2], axis=0)
+        out = jnp.dot(stack, perm_ref[...], preferred_element_type=F32)
+        n = UO * dates
+        out = out[:n] + (out[n : 2 * n] + out[2 * n :])
+        for u in range(UO):
+            for half in range(2):
+                fbuf[half, pl.ds((i * UO + u) * OP, dates), :] = out[
+                    u * dates : (u + 1) * dates, half * LANES : (half + 1) * LANES
+                ]
+        return c
+
+    lax.fori_loop(0, R // UO, finish, 0)
+    for j in range(unknowns):
         for half in range(2):
-            obuf.at[half].reshape(dates * R, LANES)[pl.ds(row, dates, stride=R), :] = out[
-                :, half * LANES : (half + 1) * LANES
-            ]
-        return c
-
-    lax.fori_loop(0, R, finish, 0)
+            for block in range(R // SUB):
+                obuf[half, j, pl.ds(block * SUB, SUB), :] = fbuf[
+                    half, pl.ds(block * SUB * OP + j, SUB, stride=OP), :
+                ]
     outs = []
     for half in range(2):
         outs.append(
@@ -566,7 +595,7 @@
         v2(NZ * group), v2(NZ * group), v2(NZ * group),
         v2(R * NF * K * 2 * SUB),
         pltpu.VMEM((2, pairs, R, LANES), jnp.int32),
-        v2(R * NF * K * 2 * SUB),
+        v2(R * (NF * K * 2 * SUB + 1)),
         pltpu.VMEM((U, 2, dates + SUB, LANES), F32),
         pltpu.VMEM((U, 2, SPAN, dates + SUB, LANES), F32),
         pltpu.VMEM((U, 2, SPAN, dates + SUB, LANES), F32),
@@ -574,7 +603,9 @@
         pltpu.VMEM((2 + K, dates, LANES), F32),
         pltpu.VMEM((2, dates // 2, LANES), F32),
         pltpu.VMEM((R, 2, dates, LANES), F32),
+        pltpu.VMEM((2, R * (dates + 1), LANES), F32),
         pltpu.VMEM((2, dates, R, LANES), F32),
+        pltpu.VMEM((columns, columns), BF16),
         pltpu.SemaphoreType.DMA((2,)),
         pltpu.SemaphoreType.DMA((2,)),
     ]

time: 56.6 us -> 48.8 us (0.86)
  Pallas kernels: 42.7 us -> 34.9 us
    pallas_call x1, Pallas kernels: 39.2 us -> 32 us  [solve(): pl.pallas_call(main_kernel, out_shape=jax.ShapeDtypeStruct((dates - 1, R,...]
    pallas_call x1, Pallas kernels: 3.52 us -> 2.86 us  [pack(): pl.pallas_call(functools.partial(pack_kernel, HALO), out_shape=(shape(row...]
  transfers between devices with their start and end apart: 3 -> 3, of which waited for: 1 -> 1; matrix products, arithmetic and copies ran while one was open for 2% -> 3% of each run, Pallas kernels for 0% -> 0%
where the time goes in v3:
time: 48.8 us; the launch traced here: 48.6 us
  Pallas kernels  34.9 us (72%)
  starting transfers between devices  7.94 us (16%)
  waiting for transfers between devices  2.9 us (6%)
  local copies, waits for them, and re-layouts  2.81 us (6%)
    pallas_call x1, Pallas kernels, solve(): pl.pallas_call(main_kernel, out_shape=jax.ShapeDtypeStruct((dates - 1, R,...  32 us
    ppermute x1, starting transfers between devices, local(): cross = lax.ppermute(cross, axes, to_cross)  6.65 us
    ppermute x1, waiting for transfers between devices, local(): cross = lax.ppermute(cross, axes, to_cross)  2.9 us
    pallas_call x1, Pallas kernels, pack(): pl.pallas_call(functools.partial(pack_kernel, HALO), out_shape=(shape(row...  2.86 us
    unnamed x7, local copies, waits for them, and re-layouts  2.81 us
    ppermute x1, starting transfers between devices, local(): same = lax.ppermute(same, axes, to_same)  1.28 us
  transfers between devices with their start and end apart: 3, of which 1 were waited for; matrix products, arithmetic and copies ran while one was open for 3% of the time, Pallas kernels for 0%

profile of v3, /device:TPU:1, one launch (start us, length us, event | category | flops | bytes accessed | tf_op | source)
XLA Modules:
  0.0 48.6 jit_solution(5126463915346997258)
XLA Ops:
  0.0 2.9 %pack.1 = (bf16[32,2,2,16,128]{4,3,2,1,0:T(8,128)(2,1)}, bf16[9,2,2,16,128]{4,3,2,1,0:T(8,128)(2,1)}, bf16[9,2,2,16,128]{4,3,2,1,0:T(8,128)(2,1)}) custom-call(bf16[16,32,256]{2,1,0:T(8,128)(2,1)} %re_ref.1, bf16[16,32,256]{2,1,0:T(8,128)(2,1)} %im_ref.1), custom_call_target="tpu_custom_call" | custom-call | tf_op jit(solution)/shard_map/pack/pallas_call | solution.py:94
  2.9 0.0 collective-permute-start
  2.9 1.3 %collective-permute-start.1 = (bf16[9,2,2,16,128]{4,3,2,1,0:T(8,128)(2,1)}, bf16[9,2,2,16,128]{4,3,2,1,0:T(8,128)(2,1)S(1)}, u32[]{:S(2)}, u32[]{:S(2)}) collective-permute-start(bf16[9,2,2,16,128]{4,3,2,1,0:T(8,128)(2,1)} %get-tuple-element.9), channel_id=1, source_target_pairs={{0,2},{2,4},{4,6},{6,8},{8,10},{10,12},{12,14},{3,1},{5,3},{7,5},{... | collective-permute-start | bytes 442376 | tf_op jit(solution)/shard_map/ppermute | solution.py:634
  4.2 6.6 %collective-permute-start.2 = (bf16[9,2,2,16,128]{4,3,2,1,0:T(8,128)(2,1)}, bf16[9,2,2,16,128]{4,3,2,1,0:T(8,128)(2,1)S(1)}, u32[]{:S(2)}, u32[]{:S(2)}) collective-permute-start(bf16[9,2,2,16,128]{4,3,2,1,0:T(8,128)(2,1)} %get-tuple-element.10), channel_id=1, source_target_pairs={{1,2},{3,4},{5,6},{7,8},{9,10},{11,12},{13,14},{2,1},{4,3},{6,5},{... | collective-permute-start | bytes 442376 | tf_op jit(solution)/shard_map/ppermute | solution.py:635
  10.8 1.4 %copy.5.offset_ref = s32[32,4]{1,0:T(8,128)} copy(s32[32,4]{0,1:T(4,128)} %param.6) | data formatting | bytes 1024 | tf_op args[2]
  12.2 0.0 collective-permute-done.1.same_ref
  12.2 0.0 copy-start.1
  12.2 2.9 %collective-permute-done.2.cross_ref = bf16[9,2,2,16,128]{4,3,2,1,0:T(8,128)(2,1)S(1)} collective-permute-done((bf16[9,2,2,16,128]{4,3,2,1,0:T(8,128)(2,1)}, bf16[9,2,2,16,128]{4,3,2,1,0:T(8,128)(2,1)S(1)}, u32[]{:S(2)}, u32[]{:S(2)}) %collective-permute-start.2) | collective-permute-done | bytes 147488 | tf_op jit(solution)/shard_map/ppermute | solution.py:635
  15.1 0.0 copy-start.2
  15.1 0.0 collective-permute-done.partner_ref
  15.1 0.0 copy-done.1
  15.1 0.7 %copy-done.2 = bf16[9,2,2,16,128]{4,3,2,1,0:T(8,128)(2,1)} copy-done((bf16[9,2,2,16,128]{4,3,2,1,0:T(8,128)(2,1)}, bf16[9,2,2,16,128]{4,3,2,1,0:T(8,128)(2,1)S(1)}, u32[]{:S(2)}) %copy-start.2) | copy-done | bytes 147480
  15.7 0.0 copy-start
  15.7 0.8 %copy-done = bf16[32,2,2,16,128]{4,3,2,1,0:T(8,128)(2,1)} copy-done((bf16[32,2,2,16,128]{4,3,2,1,0:T(8,128)(2,1)}, bf16[32,2,2,16,128]{4,3,2,1,0:T(8,128)(2,1)S(1)}, u32[]{:S(2)}) %copy-start) | copy-done | bytes 524312
  16.5 32.0 %solve.1 = f32[31,16,256]{2,1,0:T(8,128)} custom-call(bf16[32,2,2,16,128]{4,3,2,1,0:T(8,128)(2,1)} %get-tuple-element.8.own_ref, bf16[32,2,2,16,128]{4,3,2,1,0:T(8,128)(2,1)} %copy-done, bf16[9,2,2,16,128]{4,3,2,1,0:T(8,128)(2,1)} %copy-done.1, bf16[9,2,2,16,128]{4,3,2,1,0:T(8,128)(2,1)} %copy-done.2, s32[32,4]{1,0:T(8,128)} %copy.5.offset_ref, ...), custom_call_target="tpu_custom_call" | custom-call | tf_op jit(solution)/shard_map/solve/pallas_call | solution.py:612
Async XLA Ops:
  2.9 12.2 %collective-permute-start = (bf16[32,2,2,16,128]{4,3,2,1,0:T(8,128)(2,1)}, bf16[32,2,2,16,128]{4,3,2,1,0:T(8,128)(2,1)S(1)}, u32[]{:S(2)}, u32[]{:S(2)}) collective-permute-start(bf16[32,2,2,16,128]{4,3,2,1,0:T(8,128)(2,1)} %get-tuple-element.8.own_ref), channel_id=1, source_target_pairs={{0,1},{1,0},{2,3},{3,2},{4,5},{5,4},{6,7},{7,6},{8,9},{9,8},{10,11... | collective-permute-start | bytes 1572872 | tf_op jit(solution)/shard_map/ppermute | solution.py:636
  2.9 9.3 %collective-permute-start.1 = (bf16[9,2,2,16,128]{4,3,2,1,0:T(8,128)(2,1)}, bf16[9,2,2,16,128]{4,3,2,1,0:T(8,128)(2,1)S(1)}, u32[]{:S(2)}, u32[]{:S(2)}) collective-permute-start(bf16[9,2,2,16,128]{4,3,2,1,0:T(8,128)(2,1)} %get-tuple-element.9), channel_id=1, source_target_pairs={{0,2},{2,4},{4,6},{6,8},{8,10},{10,12},{12,14},{3,1},{5,3},{7,5},{... | collective-permute-start | bytes 442376 | tf_op jit(solution)/shard_map/ppermute | solution.py:634
  4.2 10.9 %collective-permute-start.2 = (bf16[9,2,2,16,128]{4,3,2,1,0:T(8,128)(2,1)}, bf16[9,2,2,16,128]{4,3,2,1,0:T(8,128)(2,1)S(1)}, u32[]{:S(2)}, u32[]{:S(2)}) collective-permute-start(bf16[9,2,2,16,128]{4,3,2,1,0:T(8,128)(2,1)} %get-tuple-element.10), channel_id=1, source_target_pairs={{1,2},{3,4},{5,6},{7,8},{9,10},{11,12},{13,14},{2,1},{4,3},{6,5},{... | collective-permute-start | bytes 442376 | tf_op jit(solution)/shard_map/ppermute | solution.py:635
  12.2 2.9 %copy-start.1 = (bf16[9,2,2,16,128]{4,3,2,1,0:T(8,128)(2,1)}, bf16[9,2,2,16,128]{4,3,2,1,0:T(8,128)(2,1)S(1)}, u32[]{:S(2)}) copy-start(bf16[9,2,2,16,128]{4,3,2,1,0:T(8,128)(2,1)S(1)} %collective-permute-done.1.same_ref) | copy-start | bytes 442372
  15.1 0.7 %copy-start.2 = (bf16[9,2,2,16,128]{4,3,2,1,0:T(8,128)(2,1)}, bf16[9,2,2,16,128]{4,3,2,1,0:T(8,128)(2,1)S(1)}, u32[]{:S(2)}) copy-start(bf16[9,2,2,16,128]{4,3,2,1,0:T(8,128)(2,1)S(1)} %collective-permute-done.2.cross_ref) | copy-start | bytes 442372
  15.7 0.8 %copy-start = (bf16[32,2,2,16,128]{4,3,2,1,0:T(8,128)(2,1)}, bf16[32,2,2,16,128]{4,3,2,1,0:T(8,128)(2,1)S(1)}, u32[]{:S(2)}) copy-start(bf16[32,2,2,16,128]{4,3,2,1,0:T(8,128)(2,1)S(1)} %collective-permute-done.partner_ref) | copy-start | bytes 1572868

commit v4 on v3

--- a/solution.py
+++ b/solution.py
@@ -23,7 +23,9 @@
 CLASSES = 4
 GROUPS = 64
 UI, UH, UW, UO = 5, 3, 8, 4
-UA, UB, UC, CK = 2, 2, 5, 2
+UNROLL_1 = (5, 4, 7)
+UNROLL_2 = (7, 4, 10)
+MORE = 5
 HALO = SWEEPS + 1
 F32 = jnp.float32
 BF16 = jnp.bfloat16
@@ -46,16 +48,32 @@
     return jnp.where(place == target, 1.0, 0.0).astype(BF16)
 
 
-def pack_kernel(halo, re_ref, im_ref, all_ref, same_ref, cross_ref, flat, perm_ref):
-    dates, rows, columns = re_ref.shape
+def pack_kernel(
+    re_hbm, im_hbm, offset_hbm, weight_hbm, all_ref, msk, lmsk, wraw,
+    images, offset_ref, flat, turned, perm_ref, sems,
+):
+    _, dates, rows, columns = images.shape
     side = lax.axis_index("date")
+    copies = [
+        pltpu.make_async_copy(re_hbm, images.at[0], sems.at[0]),
+        pltpu.make_async_copy(im_hbm, images.at[1], sems.at[1]),
+        pltpu.make_async_copy(offset_hbm, offset_ref, sems.at[2]),
+    ]
+    copies += [
+        pltpu.make_async_copy(weight_hbm.at[:, :, pl.ds(half * LANES, LANES)], wraw.at[half], sems.at[3 + half])
+        for half in range(2)
+    ]
+    for copy in copies:
+        copy.start()
     perm_ref[...] = perm_matrix(False, side)
     CH = 4
     pitch = rows + 1
+    copies[0].wait()
+    copies[1].wait()
 
     def permute(i, c):
-        for part, ref in enumerate((re_ref, im_ref)):
-            block = ref[pl.ds(i * CH, CH)].reshape(CH * rows, columns)
+        for part in range(2):
+            block = images[part, pl.ds(i * CH, CH)].reshape(CH * rows, columns)
             out = jnp.dot(block, perm_ref[...], preferred_element_type=F32)
             for n in range(CH):
                 for half in range(2):
@@ -65,7 +83,7 @@
         return c
 
     lax.fori_loop(0, dates // CH, permute, 0)
-    RW = 4
+    RW = 8
 
     def turn(i, c):
         for u in range(RW):
@@ -77,126 +95,140 @@
         return c
 
     lax.fori_loop(0, rows // RW, turn, 0)
-    last = rows - halo
-
-    def send(i, c):
-        same_ref[i] = all_ref[last * (1 - side) + i]
-        cross_ref[i] = all_ref[last * side + i]
-        return c
-
-    lax.fori_loop(0, halo, send, 0)
-
-
-def pack(slc_real, slc_imag):
+    copies[2].wait()
+    offset_masks(offset_ref, msk, lmsk, turned)
+    copies[3].wait()
+    copies[4].wait()
+
+
+def pack(slc_real, slc_imag, offsets, pair_weight):
     dates, rows, columns = slc_real.shape
-    shape = lambda count: jax.ShapeDtypeStruct((count, 2, 2, dates, LANES), BF16)
+    pairs, R, _ = pair_weight.shape
+    inputs = [pltpu.with_memory_space_constraint(x, pltpu.HBM) for x in (slc_real, slc_imag, offsets, pair_weight)]
+    vm = pl.BlockSpec(memory_space=pltpu.VMEM)
+    hbm = pl.BlockSpec(memory_space=pltpu.HBM)
+    per_date, all_dates = offsets.shape
+    return pl.pallas_call(
+        pack_kernel,
+        out_shape=(
+            pltpu.VMEM((rows, 2, 2, dates, LANES), BF16),
+            pltpu.VMEM((2 + per_date, all_dates, LANES), F32),
+            pltpu.VMEM((2, all_dates // 2, LANES), F32),
+            pltpu.VMEM((2, pairs, R, LANES), jnp.int32),
+        ),
+        in_specs=[hbm] * 4,
+        out_specs=(vm,) * 4,
+        scratch_shapes=[
+            pltpu.VMEM((2, dates, rows, columns), BF16),
+            pltpu.VMEM(offsets.shape, jnp.int32),
+            pltpu.VMEM((2, 2, dates * (rows + 1), LANES), F32),
+            pltpu.VMEM((SUB, LANES), F32),
+            pltpu.VMEM((columns, columns), BF16),
+            pltpu.SemaphoreType.DMA((5,)),
+        ],
+        name="pack",
+        compiler_params=pltpu.CompilerParams(vmem_limit_bytes=12 * 1024 * 1024),
+    )(*inputs)
+
+
+def edge_kernel(own_ref, partner_ref, _, sent_ref):
+    side = lax.axis_index("date")
+    first = (own_ref.shape[0] - HALO) * side
+    for i in range(HALO):
+        sent_ref[0, i] = own_ref[first + i]
+        sent_ref[1, i] = partner_ref[first + i]
+
+
+def edges(own, partner, after):
     vm = pl.BlockSpec(memory_space=pltpu.VMEM)
     return pl.pallas_call(
-        functools.partial(pack_kernel, HALO),
-        out_shape=(shape(rows), shape(HALO), shape(HALO)),
-        in_specs=[vm, vm],
-        out_specs=(vm, vm, vm),
-        scratch_shapes=[pltpu.VMEM((2, 2, dates * (rows + 1), LANES), F32), pltpu.VMEM((columns, columns), BF16)],
-        name="pack",
-    )(slc_real, slc_imag)
-
-
-def main_kernel(
-    own_ref, partner_ref, same_ref, cross_ref, offset_ref, weight_hbm, out_hbm,
-    img, cre, cim, zre, zim, mag, hle, hlo, dh, sh, rr, ss, aa, ya, yb, yc,
-    yy, wraw, wf, vv, aw, ag, wk, msk, lmsk, vfin, fbuf, obuf, perm_ref, wsem, osem,
-):
-    half_dates = own_ref.shape[3]
-    dates = 2 * half_dates
-    tile_rows = own_ref.shape[0]
-    R = tile_rows // 2
-    H = HALO
-    NR = R + 2 * H
-    NZ = NR - 2
+        edge_kernel,
+        out_shape=pltpu.VMEM((2, HALO, *own.shape[1:]), own.dtype),
+        in_specs=[vm, vm, pl.BlockSpec(memory_space=pl.ANY)],
+        out_specs=vm,
+        name="edges",
+        compiler_params=pltpu.CompilerParams(vmem_limit_bytes=4 * 1024 * 1024),
+    )(own, partner, after)
+
+
+def gix(row, k, cls):
+    return al(((row * K + k) * CLASSES + cls) * SUB)
+
+
+def roll_right(x):
+    return pltpu.roll(x, 1, 1)
+
+
+def roll_left(x):
+    return pltpu.roll(x, LANES - 1, 1)
+
+
+def swap_halves(x):
+    return pltpu.roll(x, GROUPS, 1)
+
+
+def run(count, unroll, step):
+    def body(i, c):
+        for u in range(unroll):
+            step(i * unroll + u)
+        return c
+
+    whole = count // unroll
+    lax.fori_loop(0, whole, body, 0)
+    for n in range(whole * unroll, count):
+        step(n)
+
+
+def lane_masks():
+    lane = lax.broadcasted_iota(jnp.int32, (SUB, LANES), 1)
+    return lane < GROUPS, lane % GROUPS == 0, lane % GROUPS == GROUPS - 1
+
+
+def offset_masks(offset_ref, msk, lmsk, turned):
+    dates = offset_ref.shape[1]
+    turned[...] = jnp.zeros(turned.shape, F32)
+    turned[pl.ds(0, K), pl.ds(0, dates)] = offset_ref[...].astype(F32)
+    offsets = jnp.transpose(turned[...])[:dates]
+    first = lax.broadcasted_iota(jnp.int32, (dates, 1), 0).astype(F32)
+    tests = [offsets[:, 1:2] == 2.0, offsets[:, 2:3] == 4.0]
+    tests += [first + offsets[:, k : k + 1] < dates for k in range(K)]
+    for n, test in enumerate(tests[: msk.shape[0]]):
+        msk[n] = jnp.broadcast_to(jnp.where(test, 1.0, 0.0).astype(F32), (dates, LANES))
+    if lmsk is not None:
+        half = dates // 2
+        low = lax.broadcasted_iota(jnp.int32, (half, LANES), 1) < GROUPS
+        for n in range(2):
+            lmsk[n] = jnp.where(low, msk[n, :half], msk[n, half:])
+
+
+def place_images(img, side, row, mine_ref, mine_row, other_ref, other_row):
+    half_dates = mine_ref.shape[3]
     DP = half_dates + SUB
-    NF = dates // SUB
-    NB = NF // 2
-    side = lax.axis_index("date")
-    tile = lax.axis_index("tile")
-    tiles = lax.axis_size("tile")
-
-    copies = []
-    for half in range(2):
-        copies.append(
-            pltpu.make_async_copy(
-                weight_hbm.at[:, :, pl.ds(half * LANES, LANES)], wraw.at[half], wsem.at[half]
-            )
-        )
-    for copy in copies:
-        copy.start()
-
-    offsets = offset_ref[...]
-    m1 = jnp.where(offsets[:, 1:2] == 2, 1.0, 0.0).astype(F32)
-    m2 = jnp.where(offsets[:, 2:3] == 4, 1.0, 0.0).astype(F32)
-    msk[0] = jnp.broadcast_to(m1, (dates, LANES))
-    msk[1] = jnp.broadcast_to(m2, (dates, LANES))
-    first = lax.broadcasted_iota(jnp.int32, (dates, 1), 0)
-    for k in range(K):
-        ok = jnp.where(first + offsets[:, k : k + 1] < dates, 1.0, 0.0).astype(F32)
-        msk[2 + k] = jnp.broadcast_to(ok, (dates, LANES))
-
-    lane = lax.broadcasted_iota(jnp.int32, (SUB, LANES), 1)
-    at_first = lane % GROUPS == 0
-    at_last = lane % GROUPS == GROUPS - 1
-    low = lane < GROUPS
-    zero = jnp.zeros((SUB, LANES), F32)
-    low2 = lax.broadcasted_iota(jnp.int32, (half_dates, LANES), 1) < GROUPS
-    for n in range(2):
-        lmsk[n] = jnp.where(low2, msk[n, :half_dates], msk[n, half_dates:])
-    own2 = (lax.broadcasted_iota(jnp.int32, (half_dates, LANES), 1) // GROUPS) == side
-
-    def swap_halves(x):
-        return pltpu.roll(x, GROUPS, 1)
-
+    own = (lax.broadcasted_iota(jnp.int32, (half_dates, LANES), 1) // GROUPS) == side
+    low = lane_masks()[0]
     third = 1.0 / 3.0
-
-    def put(rho, o_tile_ref, o_row, p_tile_ref, p_row):
-        for part in range(2):
-            for pair in range(2):
-                mine = o_tile_ref[o_row, part, pair].astype(F32) * third
-                other = p_tile_ref[p_row, part, pair].astype(F32) * third
-                for odd in range(2):
-                    if odd:
-                        x = swap_halves(jnp.where(own2, other, mine))
-                    else:
-                        x = jnp.where(own2, mine, other)
-                    base = ((rho * 2 + part) * CLASSES + pair * 2 + odd) * DP
-                    img[pl.ds(al(base), half_dates), :] = x
-                    img[pl.ds(al(base + half_dates), SUB), :] = jnp.where(low, swap_halves(x[:SUB]), 0.0)
-
-    base_row = (R - H) * side
-    base_rho = H * (1 - side)
-
-    def put_tile(i, c):
-        for u in range(UI):
-            n = i * UI + u
-            put(base_rho + n, own_ref, base_row + n, partner_ref, base_row + n)
-        return c
-
-    lax.fori_loop(0, (R + H) // UI, put_tile, 0)
-    halo_rho = (R + H) * side
-
-    def put_halo(i, c):
-        for u in range(UH):
-            n = i * UH + u
-            put(halo_rho + n, same_ref, n, cross_ref, n)
-        return c
-
-    lax.fori_loop(0, H // UH, put_halo, 0)
-
-    def roll_right(x):
-        return pltpu.roll(x, 1, 1)
-
-    def roll_left(x):
-        return pltpu.roll(x, LANES - 1, 1)
-
-    def gix(row, k, cls):
-        return al(((row * K + k) * CLASSES + cls) * SUB)
+    for part in range(2):
+        for pair in range(2):
+            mine = mine_ref[mine_row, part, pair].astype(F32) * third
+            other = other_ref[other_row, part, pair].astype(F32) * third
+            for odd in range(2):
+                if odd:
+                    x = swap_halves(jnp.where(own, other, mine))
+                else:
+                    x = jnp.where(own, mine, other)
+                base = ((row * 2 + part) * CLASSES + pair * 2 + odd) * DP
+                img[pl.ds(al(base), half_dates), :] = x
+                img[pl.ds(al(base + half_dates), SUB), :] = jnp.where(low, swap_halves(x[:SUB]), 0.0)
+
+
+def construct(img, lmsk, count, base, outside, resume, unroll, work, outs, NZ):
+    cre, cim, zre, zim, mag, hle, dh, sh = work
+    rr, ss, aa, hlo = outs
+    DP = lmsk.shape[1] + SUB
+    NB = lmsk.shape[1] // SUB
+    low, at_first, at_last = lane_masks()
+    ua, ub, uc = unroll
+    fix = lambda ft, row, k, cls: al((((ft * NZ + row) * K + k) * CLASSES + cls) * SUB)
 
     def block(ft, carry):
         f0 = al(ft * SUB)
@@ -233,12 +265,7 @@
                     for cls in range(CLASSES):
                         ref[pl.ds(gix(rho, k, cls), SUB), :] = sums[cls]
 
-        def phase_a(i, c):
-            for u in range(UA):
-                form(i * UA + u)
-            return c
-
-        lax.fori_loop(0, NR // UA, phase_a, 0)
+        run(count, ua, form)
 
         def edge(m, cross, scale):
             q = 1.0 / (m + 1.0)
@@ -286,24 +313,14 @@
                     dh[pl.ds(gix(j, k, cls), SUB), :] = dens[cls]
                     sh[pl.ds(gix(j, k, cls), SUB), :] = srcs[cls]
 
-        def phase_b(i, c):
-            for u in range(UB):
-                smooth(i * UB + u)
-            return c
-
-        lax.fori_loop(0, NZ // UB, phase_b, 0)
-
-        @pl.when((tile == 0) & (side == 0))
-        def _():
-            for k in range(K):
-                for cls in range(CLASSES):
-                    mag[pl.ds(gix(H - 2, k, cls), SUB), :] = zero
-
-        @pl.when((tile == tiles - 1) & (side == 1))
-        def _():
-            for k in range(K):
-                for cls in range(CLASSES):
-                    mag[pl.ds(gix(H - 1 + R, k, cls), SUB), :] = zero
+        run(count - 2, ub, smooth)
+
+        for condition, row in outside:
+            @pl.when(condition)
+            def _():
+                for k in range(K):
+                    for cls in range(CLASSES):
+                        mag[pl.ds(gix(row, k, cls), SUB), :] = jnp.zeros((SUB, LANES), F32)
 
         def vertical(j, k, cls):
             i0, i1 = gix(j, k, cls), gix(j + 1, k, cls)
@@ -323,31 +340,138 @@
                     den = vreg(dh, i0) + vm + v
                     src = vreg(sh, i0) + f - fm
                     r = lax.rsqrt(den)
-                    rr[pl.ds(i0, SUB), :] = r
-                    ss[pl.ds(i0, SUB), :] = src * r
-                    aa[pl.ds(i0, SUB), :] = vm * (r * rm)
+                    place = fix(ft, base + j, k, cls)
+                    rr[pl.ds(place, SUB), :] = r
+                    ss[pl.ds(place, SUB), :] = src * r
+                    aa[pl.ds(place, SUB), :] = vm * (r * rm)
                     root.append(r)
                     after += [v, f, r]
                 for cls in range(CLASSES):
                     other = root[cls + 1] if cls < CLASSES - 1 else roll_left(root[0])
                     i0 = gix(j, k, cls)
-                    hlo[pl.ds(i0, SUB), :] = vreg(hle, i0) * (root[cls] * other)
+                    hlo[pl.ds(fix(ft, base + j, k, cls), SUB), :] = vreg(hle, i0) * (root[cls] * other)
             return after
 
-        def phase_c(ks):
+        def phase_c(k):
+            start = []
+            for cls in range(CLASSES):
+                above = jnp.zeros((SUB, LANES), F32)
+                if resume is not None:
+                    above = jnp.where(resume, vreg(rr, fix(ft, base, k, cls)), above)
+                start += [*vertical(0, k, cls), above]
+
             def body(i, c):
-                for u in range(UC):
-                    c = stencil(1 + i * UC + u, ks, c)
+                for u in range(uc):
+                    c = stencil(1 + i * uc + u, [k], c)
                 return tuple(c)
 
-            start = []
-            for k in ks:
-                for cls in range(CLASSES):
-                    start += [*vertical(0, k, cls), zero]
-            lax.fori_loop(0, (NZ - 2) // UC, body, tuple(start))
-
-        for k in range(0, K, CK):
-            phase_c(range(k, k + CK))
+            lax.fori_loop(0, (count - 4) // uc, body, tuple(start))
+
+        for k in range(K):
+            phase_c(k)
+        return carry
+
+    lax.fori_loop(0, NB, block, 0)
+
+
+def work_scratch(count):
+    group = K * CLASSES * SUB
+    v2 = lambda rows: pltpu.VMEM((rows, LANES), F32)
+    return [v2(count * group)] * 2 + [v2((count - 2) * group)] * 6
+
+
+def weight_kernel(wraw, msk, wf, perm_ref):
+    dates = msk.shape[1]
+    R = wraw.shape[2]
+    NF = dates // SUB
+    perm_ref[...] = perm_matrix(False)
+    pairs = K * dates
+    WR = K * NF * 2 * SUB + 1
+
+    def weights(i, c):
+        p0 = i * UW
+        rows = [
+            wraw[half, pl.ds(p0, UW)].reshape(UW * R, LANES).astype(F32).astype(BF16) for half in range(2)
+        ]
+        out = jnp.dot(jnp.concatenate(rows, axis=1), perm_ref[...], preferred_element_type=F32)
+        for n in range(UW):
+            f, k = i * (UW // K) + n // K, n % K
+            t, sub = f // SUB, f % SUB
+            for block in range(R // SUB):
+                for half in range(2):
+                    x = out[n * R + block * SUB : n * R + (block + 1) * SUB, half * LANES : (half + 1) * LANES]
+                    place = ((k * NF + t) * 2 + half) * SUB + sub + block * SUB * WR
+                    wf[pl.ds(place, SUB, stride=WR), :] = x
+        return c
+
+    lax.fori_loop(0, pairs // UW, weights, 0)
+    for row in range(R):
+        for k in range(K):
+            for t in range(NF):
+                if (t + 1) * SUB + SPAN - 1 >= dates:
+                    for half in range(2):
+                        place = row * WR + ((k * NF + t) * 2 + half) * SUB
+                        wf[pl.ds(place, SUB), :] = wf[pl.ds(place, SUB), :] * msk[2 + k, pl.ds(t * SUB, SUB), :]
+
+
+def inner_kernel(
+    own_ref, partner_ref, lmsk, rr, ss, aa, hlo,
+    img, cre, cim, zre, zim, mag, hle, dh, sh,
+):
+    R = own_ref.shape[0] // 2
+    H = HALO
+    NZ = R + 2 * H - 2
+    side = lax.axis_index("date")
+    row0 = (R - H) * side
+    run(R + H, UI, lambda i: place_images(img, side, i, own_ref, row0 + i, partner_ref, row0 + i))
+    construct(
+        img, lmsk, R + H, H * (1 - side), (), None, UNROLL_1,
+        (cre, cim, zre, zim, mag, hle, dh, sh), (rr, ss, aa, hlo), NZ,
+    )
+
+
+def outer_kernel(
+    own_ref, partner_ref, halo_ref, msk, lmsk, rr_in, ss_in, aa_in, hlo_in, wf,
+    out_hbm, rr, ss, aa, hlo,
+    img, cre, cim, zre, zim, mag, hle, dh, sh, ya, yb, yc, yy,
+    vv, aw, ag, wk, vfin, fbuf, obuf, perm_ref, osem,
+):
+    dates = 2 * own_ref.shape[3]
+    R = own_ref.shape[0] // 2
+    H = HALO
+    NR = R + 2 * H
+    NZ = NR - 2
+    NF = dates // SUB
+    NB = NF // 2
+    side = lax.axis_index("date")
+    tile = lax.axis_index("tile")
+    tiles = lax.axis_size("tile")
+    zero = jnp.zeros((SUB, LANES), F32)
+    low = lane_masks()[0]
+    WR = K * NF * 2 * SUB + 1
+
+    count = H + MORE
+    base = (NR - count) * side
+    run(H, UH, lambda i: place_images(img, side, MORE * side + i, halo_ref.at[1], i, halo_ref.at[0], i))
+    row0 = (2 * R - MORE) * side
+    run(
+        MORE, MORE,
+        lambda i: place_images(img, side, H * (1 - side) + i, own_ref, row0 + i, partner_ref, row0 + i),
+    )
+    outside = (
+        ((tile == 0) & (side == 0), H - 2),
+        ((tile == tiles - 1) & (side == 1), H - 1 + R - (NR - count)),
+    )
+    construct(
+        img, lmsk, count, base, outside, side == 1, UNROLL_2,
+        (cre, cim, zre, zim, mag, hle, dh, sh), (rr, ss, aa, hlo), NZ,
+    )
+
+    def sweep_block(ft, carry):
+        def at(ref, row, k, cls):
+            if any(ref is x for x in (ya, yb, yc)):
+                return gix(row, k, cls)
+            return al((((ft * NZ + row) * K + k) * CLASSES + cls) * SUB)
 
         def sweeps(k, c):
             steps = []
@@ -365,22 +489,21 @@
             for n, (source, added, target) in enumerate(steps):
                 left = len(steps) - 1 - n
                 classes = range(CLASSES)
-                get = lambda ref, row: [vreg(ref, gix(row, k, cls)) for cls in classes]
+                get = lambda ref, row: [vreg(ref, at(ref, row, k, cls)) for cls in classes]
                 top = H - 1 - left
                 y = [None, get(source, top - 1), get(source, top)]
                 links = [None, get(aa, top)]
                 for j in range(H - 1 - left, H - 1 + R + left):
                     y = [y[1], y[2], get(source, j + 1)]
                     links = [links[1], get(aa, j + 1)]
-                    h = [vreg(hlo, gix(j, k, cls)) for cls in range(CLASSES)]
+                    h = get(hlo, j)
                     right = [h[cls] * y[1][cls + 1] for cls in range(CLASSES - 1)] + [h[3] * roll_left(y[1][0])]
                     back = [roll_right(h[3] * y[1][3])] + [h[cls] * y[1][cls] for cls in range(CLASSES - 1)]
                     new = []
                     for cls in range(CLASSES):
-                        i0 = gix(j, k, cls)
                         x = links[0][cls] * y[0][cls] + links[1][cls] * y[2][cls]
                         if added is not None:
-                            x = x + (y[1][cls] if added is source else vreg(added, i0))
+                            x = x + (y[1][cls] if added is source else vreg(added, at(added, j, k, cls)))
                         if cls in (0, CLASSES - 1):
                             x = (x + right[cls]) + back[cls] if cls == 0 else (x + back[cls]) + right[cls]
                         else:
@@ -392,7 +515,7 @@
                     else:
                         row = j - (H - 1)
                         u = [
-                            new[cls] * (vreg(rr, gix(j, k, cls)) * (1.0 / residual_scale))
+                            new[cls] * (vreg(rr, at(rr, j, k, cls)) * (1.0 / residual_scale))
                             for cls in range(CLASSES)
                         ]
                         for pair in range(2):
@@ -407,38 +530,7 @@
         lax.fori_loop(0, K, sweeps, 0)
         return carry
 
-    lax.fori_loop(0, NB, block, 0)
-
-    for copy in copies:
-        copy.wait()
-    perm_ref[...] = perm_matrix(False)
-    pairs = K * dates
-    WR = K * NF * 2 * SUB + 1
-
-    def weights(i, c):
-        p0 = i * UW
-        rows = [
-            wraw[half, pl.ds(p0, UW)].reshape(UW * R, LANES).astype(F32).astype(BF16) for half in range(2)
-        ]
-        out = jnp.dot(jnp.concatenate(rows, axis=1), perm_ref[...], preferred_element_type=F32)
-        for n in range(UW):
-            f, k = i * (UW // K) + n // K, n % K
-            t, sub = f // SUB, f % SUB
-            for block in range(R // SUB):
-                for half in range(2):
-                    x = out[n * R + block * SUB : n * R + (block + 1) * SUB, half * LANES : (half + 1) * LANES]
-                    place = ((k * NF + t) * 2 + half) * SUB + sub + block * SUB * WR
-                    wf[pl.ds(place, SUB, stride=WR), :] = x
-        return c
-
-    lax.fori_loop(0, pairs // UW, weights, 0)
-    for row in range(R):
-        for k in range(K):
-            for t in range(NF):
-                if (t + 1) * SUB + SPAN - 1 >= dates:
-                    for half in range(2):
-                        place = row * WR + ((k * NF + t) * 2 + half) * SUB
-                        wf[pl.ds(place, SUB), :] = wf[pl.ds(place, SUB), :] * msk[2 + k, pl.ds(t * SUB, SUB), :]
+    lax.fori_loop(0, NB, sweep_block, 0)
 
     damping = solve_damping * 255.0
     inv_span = 1.0 / SPAN
@@ -572,69 +664,83 @@
         copy.wait()
 
 
-def solve(own, partner, same, cross, pair_offset, pair_weight):
+def weigh(wraw, msk):
+    _, pairs, R, _ = wraw.shape
+    vm = pl.BlockSpec(memory_space=pltpu.VMEM)
+    return pl.pallas_call(
+        weight_kernel,
+        out_shape=pltpu.VMEM((R * (2 * pairs + 1), LANES), F32),
+        in_specs=[vm, vm],
+        out_specs=vm,
+        scratch_shapes=[pltpu.VMEM((2 * LANES, 2 * LANES), BF16)],
+        name="weigh",
+        compiler_params=pltpu.CompilerParams(vmem_limit_bytes=4 * 1024 * 1024),
+    )(wraw, msk)
+
+
+def solve(own, partner, halo, msk, lmsk, wf):
     tile_rows = own.shape[0]
     dates = 2 * own.shape[3]
-    pairs, R, columns = pair_weight.shape
+    R = tile_rows // 2
+    columns = 2 * LANES
     H = HALO
-    NR = R + 2 * H
-    NZ = NR - 2
+    NZ = R + 2 * H - 2
     NF = dates // SUB
     group = K * CLASSES * SUB
+    image = 2 * CLASSES * (dates // 2 + SUB)
     vm = pl.BlockSpec(memory_space=pltpu.VMEM)
     hbm = pl.BlockSpec(memory_space=pl.ANY)
     U = 1
     v2 = lambda rows: pltpu.VMEM((rows, LANES), F32)
-    scratch = [
-        v2(NR * 2 * CLASSES * (dates // 2 + SUB)),
-        v2(NR * group), v2(NR * group),
-        v2(NZ * group), v2(NZ * group), v2(NZ * group),
-        v2(NZ * group), v2(NZ * group),
-        v2(NZ * group), v2(NZ * group),
-        v2(NZ * group), v2(NZ * group), v2(NZ * group),
-        v2(NZ * group), v2(NZ * group), v2(NZ * group),
-        v2(R * NF * K * 2 * SUB),
-        pltpu.VMEM((2, pairs, R, LANES), jnp.int32),
-        v2(R * (NF * K * 2 * SUB + 1)),
-        pltpu.VMEM((U, 2, dates + SUB, LANES), F32),
-        pltpu.VMEM((U, 2, SPAN, dates + SUB, LANES), F32),
-        pltpu.VMEM((U, 2, SPAN, dates + SUB, LANES), F32),
-        pltpu.VMEM((U, NF, 2, K, SUB, LANES), F32),
-        pltpu.VMEM((2 + K, dates, LANES), F32),
-        pltpu.VMEM((2, dates // 2, LANES), F32),
-        pltpu.VMEM((R, 2, dates, LANES), F32),
-        pltpu.VMEM((2, R * (dates + 1), LANES), F32),
-        pltpu.VMEM((2, dates, R, LANES), F32),
-        pltpu.VMEM((columns, columns), BF16),
-        pltpu.SemaphoreType.DMA((2,)),
-        pltpu.SemaphoreType.DMA((2,)),
-    ]
-    return pl.pallas_call(
-        main_kernel,
-        out_shape=jax.ShapeDtypeStruct((dates - 1, R, columns), F32),
-        in_specs=[vm, vm, vm, vm, vm, hbm],
-        out_specs=hbm,
-        scratch_shapes=scratch,
-        name="solve",
-        compiler_params=pltpu.CompilerParams(vmem_limit_bytes=60 * 1024 * 1024),
-    )(own, partner, same, cross, pair_offset, pair_weight)
+    stencil = [v2(NF // 2 * NZ * group)] * 4
+    inner = pl.pallas_call(
+        inner_kernel,
+        out_shape=tuple(stencil),
+        in_specs=[vm] * 3,
+        out_specs=(vm,) * 4,
+        scratch_shapes=[
+            v2((R + H) * image),
+            *work_scratch(R + H),
+        ],
+        name="inner",
+        compiler_params=pltpu.CompilerParams(vmem_limit_bytes=24 * 1024 * 1024),
+    )
+    rr, ss, aa, hlo = inner(own, partner, lmsk)
+    outer = pl.pallas_call(
+        outer_kernel,
+        out_shape=(jax.ShapeDtypeStruct((dates - 1, R, columns), F32), *stencil),
+        in_specs=[vm] * 10,
+        out_specs=(hbm,) + (vm,) * 4,
+        input_output_aliases={5: 1, 6: 2, 7: 3, 8: 4},
+        scratch_shapes=[
+            v2((H + MORE) * image),
+            *work_scratch(H + MORE),
+            v2(NZ * group), v2(NZ * group), v2(NZ * group),
+            v2(R * NF * K * 2 * SUB),
+            pltpu.VMEM((U, 2, dates + SUB, LANES), F32),
+            pltpu.VMEM((U, 2, SPAN, dates + SUB, LANES), F32),
+            pltpu.VMEM((U, 2, SPAN, dates + SUB, LANES), F32),
+            pltpu.VMEM((U, NF, 2, K, SUB, LANES), F32),
+            pltpu.VMEM((R, 2, dates, LANES), F32),
+            pltpu.VMEM((2, R * (dates + 1), LANES), F32),
+            pltpu.VMEM((2, dates, R, LANES), F32),
+            pltpu.VMEM((columns, columns), BF16),
+            pltpu.SemaphoreType.DMA((2,)),
+        ],
+        name="outer",
+        compiler_params=pltpu.CompilerParams(vmem_limit_bytes=28 * 1024 * 1024),
+    )
+    return outer(own, partner, halo, msk, lmsk, rr, ss, aa, hlo, wf)[0]
 
 
 def local(slc_real, slc_imag, pair_offset, pair_weight):
     tiles = lax.axis_size("tile")
-    own, same, cross = pack(slc_real, slc_imag)
-    axes = ("tile", "date")
-    place = lambda t, d: 2 * t + d
-    to_same = [(place(t, 0), place(t + 1, 0)) for t in range(tiles - 1)] + [
-        (place(t + 1, 1), place(t, 1)) for t in range(tiles - 1)
-    ]
-    to_cross = [(place(t, 1), place(t + 1, 0)) for t in range(tiles - 1)] + [
-        (place(t + 1, 0), place(t, 1)) for t in range(tiles - 1)
-    ]
-    same = lax.ppermute(same, axes, to_same)
-    cross = lax.ppermute(cross, axes, to_cross)
+    own, msk, lmsk, wraw = pack(slc_real, slc_imag, pair_offset.T, pair_weight)
     partner = lax.ppermute(own, "date", [(0, 1), (1, 0)])
-    return solve(own, partner, same, cross, pair_offset, pair_weight)
+    wf = weigh(wraw, msk)
+    moves = [(2 * t + 1, 2 * t + 2) for t in range(tiles - 1)] + [(2 * t + 2, 2 * t + 1) for t in range(tiles - 1)]
+    halo = lax.ppermute(edges(own, partner, wf), ("tile", "date"), moves)
+    return solve(own, partner, halo, msk, lmsk, wf)
 
 
 def solution(mesh):

time: 48.8 us -> 35.3 us (0.72)
  Pallas kernels: 34.9 us -> 30.5 us
  starting transfers between devices: 7.94 us -> 4.6 us
  waiting for transfers between devices: 2.9 us -> 0.01 us
  local copies, waits for them, and re-layouts: 2.81 us -> 0 us
    pallas_call x2 -> x5, Pallas kernels: 34.9 us -> 30.5 us  [the longest x1 17.6 us: solve(): return outer(own, partner, halo, msk, lmsk, rr, ss, aa, hlo, wf)[0]]
    ppermute x2 -> x1, starting transfers between devices: 7.93 us -> 4.52 us  [local(): halo = lax.ppermute(edges(own, partner, wf), ('tile', 'date'), moves)]
    ppermute x2 -> x1, waiting for transfers between devices: 2.9 us -> 0.01 us  [local(): halo = lax.ppermute(edges(own, partner, wf), ('tile', 'date'), moves)]
    unnamed x7 -> x0, local copies, waits for them, and re-layouts: 2.81 us -> none
  transfers between devices with their start and end apart: 3 -> 2, of which waited for: 1 -> 0; matrix products, arithmetic and copies ran while one was open for 3% -> 0% of each run, Pallas kernels for 0% -> 31%
where the time goes in v4:
time: 35.3 us; the launch traced here: 35.2 us
  Pallas kernels  30.5 us (86%)
  starting transfers between devices  4.6 us (13%)
    pallas_call x1, Pallas kernels, solve(): return outer(own, partner, halo, msk, lmsk, rr, ss, aa, hlo, wf)[0]  17.6 us
    pallas_call x1, Pallas kernels, solve(): rr, ss, aa, hlo = inner(own, partner, lmsk)  7.97 us
    ppermute x1, starting transfers between devices, local(): halo = lax.ppermute(edges(own, partner, wf), ('tile', 'date'), moves)  4.52 us
    pallas_call x1, Pallas kernels, weigh(): pl.pallas_call(weight_kernel, out_shape=pltpu.VMEM((R * (2 * pairs + 1),...  2.8 us
    pallas_call x1, Pallas kernels, pack(): pl.pallas_call(pack_kernel, out_shape=(pltpu.VMEM((rows, 2, 2, dates, LAN...  2.07 us
  transfers between devices with their start and end apart: 2, of which 0 were waited for; matrix products, arithmetic and copies ran while one was open for 0% of the time, Pallas kernels for 31%

profile of v4, /device:TPU:1, one launch (start us, length us, event | category | flops | bytes accessed | tf_op | source)
XLA Modules:
  0.0 35.2 jit_solution(17052092841868355485)
XLA Ops:
  0.0 2.1 %pack.1 = (bf16[32,2,2,16,128]{4,3,2,1,0:T(8,128)(2,1)S(1)}, f32[6,32,128]{2,1,0:T(8,128)S(1)}, f32[2,16,128]{2,1,0:T(8,128)S(1)}, s32[2,128,16,128]{3,2,1,0:T(8,128)S(1)}) custom-call(bf16[16,32,256]{2,1,0:T(8,128)(2,1)} %re_hbm.1, bf16[16,32,256]{2,1,0:T(8,128)(2,1)} %im_hbm.1, s32[4,32]{1,0:T(4,128)} %bitcast.1, s32[128,16,256]{2,1,0:T(8,128)} %weight_hbm.1), custom_call_target="tpu_custom_call" | custom-call | tf_op jit(solution)/shard_map/pack/pallas_call | solution.py:111
  2.1 0.1 collective-permute-start
  2.2 2.8 %weigh.1._.wf = f32[4112,128]{1,0:T(8,128)S(1)} custom-call(s32[2,128,16,128]{3,2,1,0:T(8,128)S(1)} %get-tuple-element.15.wraw, f32[6,32,128]{2,1,0:T(8,128)S(1)} %get-tuple-element.16.msk), custom_call_target="tpu_custom_call" | custom-call | tf_op jit(solution)/shard_map/weigh/pallas_call | solution.py:670
  5.0 0.0 collective-permute-done.partner_ref
  5.0 4.5 %collective-permute-start.1 = (bf16[2,9,2,2,16,128]{5,4,3,2,1,0:T(8,128)(2,1)S(1)}, bf16[2,9,2,2,16,128]{5,4,3,2,1,0:T(8,128)(2,1)S(1)}, u32[]{:S(2)}, u32[]{:S(2)}) collective-permute-start(bf16[2,9,2,2,16,128]{5,4,3,2,1,0:T(8,128)(2,1)S(1)} %edges.1), channel_id=1, source_target_pairs={{1,2},{3,4},{5,6},{7,8},{9,10},{11,12},{13,14},{2,1},{4,3},{6,5},{... | collective-permute-start | bytes 884744 | tf_op jit(solution)/shard_map/ppermute | solution.py:742
  9.6 8.0 %inner.1 = (f32[8192,128]{1,0:T(8,128)S(1)}, f32[8192,128]{1,0:T(8,128)S(1)}, f32[8192,128]{1,0:T(8,128)S(1)}, f32[8192,128]{1,0:T(8,128)S(1)}) custom-call(bf16[32,2,2,16,128]{4,3,2,1,0:T(8,128)(2,1)S(1)} %get-tuple-element.14.own_ref, bf16[32,2,2,16,128]{4,3,2,1,0:T(8,128)(2,1)S(1)} %collective-permute-done.partner_ref, ...), custom_call_target="tpu_custom_call" | custom-call | tf_op jit(solution)/shard_map/inner/pallas_call | solution.py:708
  17.5 0.0 collective-permute-done.1.halo_ref
  17.5 17.6 %outer.1 = (f32[31,16,256]{2,1,0:T(8,128)}, f32[8192,128]{1,0:T(8,128)S(1)}, f32[8192,128]{1,0:T(8,128)S(1)}, f32[8192,128]{1,0:T(8,128)S(1)}, f32[8192,128]{1,0:T(8,128)S(1)}) custom-call(bf16[32,2,2,16,128]{4,3,2,1,0:T(8,128)(2,1)S(1)} %get-tuple-element.14.own_ref, ...), custom_call_target="tpu_custom_call", output_to_operand_aliasing={{1}: (5, {}), {2}: (6, {}), {3}: (7, {}), {4}: (8, {})} | custom-call | tf_op jit(solution)/shard_map/outer/pallas_call | solution.py:733
  (1 shorter events, 0.0 us)
Async XLA Ops:
  2.1 2.9 %collective-permute-start = (bf16[32,2,2,16,128]{4,3,2,1,0:T(8,128)(2,1)S(1)}, bf16[32,2,2,16,128]{4,3,2,1,0:T(8,128)(2,1)S(1)}, u32[]{:S(2)}, u32[]{:S(2)}) collective-permute-start(bf16[32,2,2,16,128]{4,3,2,1,0:T(8,128)(2,1)S(1)} %get-tuple-element.14.own_ref), channel_id=1, source_target_pairs={{0,1},{1,0},{2,3},{3,2},{4,5},{5,4},{6,7},{7,6},{8,9},{9,8},{10,11... | collective-permute-start | bytes 1572872 | tf_op jit(solution)/shard_map/ppermute | solution.py:739
  5.0 12.5 %collective-permute-start.1 = (bf16[2,9,2,2,16,128]{5,4,3,2,1,0:T(8,128)(2,1)S(1)}, bf16[2,9,2,2,16,128]{5,4,3,2,1,0:T(8,128)(2,1)S(1)}, u32[]{:S(2)}, u32[]{:S(2)}) collective-permute-start(bf16[2,9,2,2,16,128]{5,4,3,2,1,0:T(8,128)(2,1)S(1)} %edges.1), channel_id=1, source_target_pairs={{1,2},{3,4},{5,6},{7,8},{9,10},{11,12},{13,14},{2,1},{4,3},{6,5},{... | collective-permute-start | bytes 884744 | tf_op jit(solution)/shard_map/ppermute | solution.py:742

commit v5 on v4

--- a/solution.py
+++ b/solution.py
@@ -1,5 +1,3 @@
-import functools
-
 import jax
 import jax.numpy as jnp
 from jax import lax
@@ -7,6 +5,7 @@
 from jax.experimental.pallas import tpu as pltpu
 from jax.sharding import PartitionSpec as P
 
+
 K = 4
 SPAN = 5
 SWEEPS = 8
@@ -22,9 +21,9 @@
 SUB = 8
 CLASSES = 4
 GROUPS = 64
-UI, UH, UW, UO = 5, 3, 8, 4
-UNROLL_1 = (5, 4, 7)
-UNROLL_2 = (7, 4, 10)
+UI, UH, UW, KS = 4, 3, 32, 1
+UNROLL_1 = (25, 8, 7)
+UNROLL_2 = (14, 6, 10)
 MORE = 5
 HALO = SWEEPS + 1
 F32 = jnp.float32
@@ -49,7 +48,7 @@
 
 
 def pack_kernel(
-    re_hbm, im_hbm, offset_hbm, weight_hbm, all_ref, msk, lmsk, wraw,
+    re_hbm, im_hbm, offset_hbm, weight_hbm, all_ref, near_ref, rest_ref, msk, lmsk, wraw,
     images, offset_ref, flat, turned, perm_ref, sems,
 ):
     _, dates, rows, columns = images.shape
@@ -66,23 +65,18 @@
     for copy in copies:
         copy.start()
     perm_ref[...] = perm_matrix(False, side)
-    CH = 4
+    CH = dates // 2
     pitch = rows + 1
-    copies[0].wait()
-    copies[1].wait()
-
-    def permute(i, c):
-        for part in range(2):
-            block = images[part, pl.ds(i * CH, CH)].reshape(CH * rows, columns)
+    for part in range(2):
+        copies[part].wait()
+        for first in range(0, dates, CH):
+            block = images[part, first : first + CH].reshape(CH * rows, columns)
             out = jnp.dot(block, perm_ref[...], preferred_element_type=F32)
             for n in range(CH):
                 for half in range(2):
-                    flat[part, half, pl.ds((i * CH + n) * pitch, rows), :] = out[
+                    flat[part, half, pl.ds((first + n) * pitch, rows), :] = out[
                         n * rows : (n + 1) * rows, half * LANES : (half + 1) * LANES
                     ]
-        return c
-
-    lax.fori_loop(0, dates // CH, permute, 0)
     RW = 8
 
     def turn(i, c):
@@ -95,6 +89,12 @@
         return c
 
     lax.fori_loop(0, rows // RW, turn, 0)
+    near = near_ref.shape[0]
+    rest = rest_ref.shape[0]
+    for i in range(near):
+        near_ref[i] = all_ref[(rows - near) * (1 - side) + i]
+    for i in range(rest):
+        rest_ref[i] = all_ref[near * side + (rows - near - rest) * (1 - side) + i]
     copies[2].wait()
     offset_masks(offset_ref, msk, lmsk, turned)
     copies[3].wait()
@@ -112,12 +112,14 @@
         pack_kernel,
         out_shape=(
             pltpu.VMEM((rows, 2, 2, dates, LANES), BF16),
+            pltpu.VMEM((HALO, 2, 2, dates, LANES), BF16),
+            pltpu.VMEM((rows // 2, 2, 2, dates, LANES), BF16),
             pltpu.VMEM((2 + per_date, all_dates, LANES), F32),
             pltpu.VMEM((2, all_dates // 2, LANES), F32),
             pltpu.VMEM((2, pairs, R, LANES), jnp.int32),
         ),
         in_specs=[hbm] * 4,
-        out_specs=(vm,) * 4,
+        out_specs=(vm,) * 6,
         scratch_shapes=[
             pltpu.VMEM((2, dates, rows, columns), BF16),
             pltpu.VMEM(offsets.shape, jnp.int32),
@@ -131,24 +133,24 @@
     )(*inputs)
 
 
-def edge_kernel(own_ref, partner_ref, _, sent_ref):
+def edge_kernel(own_ref, near_ref, sent_ref):
     side = lax.axis_index("date")
     first = (own_ref.shape[0] - HALO) * side
     for i in range(HALO):
         sent_ref[0, i] = own_ref[first + i]
-        sent_ref[1, i] = partner_ref[first + i]
-
-
-def edges(own, partner, after):
+        sent_ref[1, i] = near_ref[i]
+
+
+def edges(own, near):
     vm = pl.BlockSpec(memory_space=pltpu.VMEM)
     return pl.pallas_call(
         edge_kernel,
         out_shape=pltpu.VMEM((2, HALO, *own.shape[1:]), own.dtype),
-        in_specs=[vm, vm, pl.BlockSpec(memory_space=pl.ANY)],
+        in_specs=[vm, vm],
         out_specs=vm,
         name="edges",
         compiler_params=pltpu.CompilerParams(vmem_limit_bytes=4 * 1024 * 1024),
-    )(own, partner, after)
+    )(own, near)
 
 
 def gix(row, k, cls):
@@ -226,7 +228,7 @@
     rr, ss, aa, hlo = outs
     DP = lmsk.shape[1] + SUB
     NB = lmsk.shape[1] // SUB
-    low, at_first, at_last = lane_masks()
+    _, at_first, at_last = lane_masks()
     ua, ub, uc = unroll
     fix = lambda ft, row, k, cls: al((((ft * NZ + row) * K + k) * CLASSES + cls) * SUB)
 
@@ -415,7 +417,7 @@
 
 
 def inner_kernel(
-    own_ref, partner_ref, lmsk, rr, ss, aa, hlo,
+    own_ref, near_ref, rest_ref, lmsk, rr, ss, aa, hlo,
     img, cre, cim, zre, zim, mag, hle, dh, sh,
 ):
     R = own_ref.shape[0] // 2
@@ -423,7 +425,10 @@
     NZ = R + 2 * H - 2
     side = lax.axis_index("date")
     row0 = (R - H) * side
-    run(R + H, UI, lambda i: place_images(img, side, i, own_ref, row0 + i, partner_ref, row0 + i))
+    far = R * side
+    run(H, UH, lambda i: place_images(img, side, far + i, own_ref, row0 + far + i, near_ref, i))
+    far = H * (1 - side)
+    run(R, UI, lambda i: place_images(img, side, far + i, own_ref, row0 + far + i, rest_ref, i))
     construct(
         img, lmsk, R + H, H * (1 - side), (), None, UNROLL_1,
         (cre, cim, zre, zim, mag, hle, dh, sh), (rr, ss, aa, hlo), NZ,
@@ -431,7 +436,7 @@
 
 
 def outer_kernel(
-    own_ref, partner_ref, halo_ref, msk, lmsk, rr_in, ss_in, aa_in, hlo_in, wf,
+    own_ref, near_ref, halo_ref, msk, lmsk, rr_in, ss_in, aa_in, hlo_in, wf,
     out_hbm, rr, ss, aa, hlo,
     img, cre, cim, zre, zim, mag, hle, dh, sh, ya, yb, yc, yy,
     vv, aw, ag, wk, vfin, fbuf, obuf, perm_ref, osem,
@@ -456,7 +461,9 @@
     row0 = (2 * R - MORE) * side
     run(
         MORE, MORE,
-        lambda i: place_images(img, side, H * (1 - side) + i, own_ref, row0 + i, partner_ref, row0 + i),
+        lambda i: place_images(
+            img, side, H * (1 - side) + i, own_ref, row0 + i, near_ref, (H - MORE) * side + i
+        ),
     )
     outside = (
         ((tile == 0) & (side == 0), H - 2),
@@ -473,7 +480,8 @@
                 return gix(row, k, cls)
             return al((((ft * NZ + row) * K + k) * CLASSES + cls) * SUB)
 
-        def sweeps(k, c):
+        def sweeps(i, c):
+            ks = [i * KS + u for u in range(KS)]
             steps = []
             buffers = [ya, yb, yc]
             held = ss
@@ -489,52 +497,55 @@
             for n, (source, added, target) in enumerate(steps):
                 left = len(steps) - 1 - n
                 classes = range(CLASSES)
-                get = lambda ref, row: [vreg(ref, at(ref, row, k, cls)) for cls in classes]
+                get = lambda ref, row, k: [vreg(ref, at(ref, row, k, cls)) for cls in classes]
                 top = H - 1 - left
-                y = [None, get(source, top - 1), get(source, top)]
-                links = [None, get(aa, top)]
+                window = [
+                    ([None, get(source, top - 1, k), get(source, top, k)], [None, get(aa, top, k)]) for k in ks
+                ]
                 for j in range(H - 1 - left, H - 1 + R + left):
-                    y = [y[1], y[2], get(source, j + 1)]
-                    links = [links[1], get(aa, j + 1)]
-                    h = get(hlo, j)
-                    right = [h[cls] * y[1][cls + 1] for cls in range(CLASSES - 1)] + [h[3] * roll_left(y[1][0])]
-                    back = [roll_right(h[3] * y[1][3])] + [h[cls] * y[1][cls] for cls in range(CLASSES - 1)]
-                    new = []
-                    for cls in range(CLASSES):
-                        x = links[0][cls] * y[0][cls] + links[1][cls] * y[2][cls]
-                        if added is not None:
-                            x = x + (y[1][cls] if added is source else vreg(added, at(added, j, k, cls)))
-                        if cls in (0, CLASSES - 1):
-                            x = (x + right[cls]) + back[cls] if cls == 0 else (x + back[cls]) + right[cls]
+                    for u, k in enumerate(ks):
+                        y, links = window[u]
+                        y = [y[1], y[2], get(source, j + 1, k)]
+                        links = [links[1], get(aa, j + 1, k)]
+                        window[u] = y, links
+                        h = get(hlo, j, k)
+                        right = [h[cls] * y[1][cls + 1] for cls in range(CLASSES - 1)] + [h[3] * roll_left(y[1][0])]
+                        back = [roll_right(h[3] * y[1][3])] + [h[cls] * y[1][cls] for cls in range(CLASSES - 1)]
+                        new = []
+                        for cls in range(CLASSES):
+                            x = links[0][cls] * y[0][cls] + links[1][cls] * y[2][cls]
+                            if added is not None:
+                                x = x + (y[1][cls] if added is source else vreg(added, at(added, j, k, cls)))
+                            if cls in (0, CLASSES - 1):
+                                x = (x + right[cls]) + back[cls] if cls == 0 else (x + back[cls]) + right[cls]
+                            else:
+                                x = x + (right[cls] + back[cls])
+                            new.append(x)
+                        if left:
+                            for cls in range(CLASSES):
+                                target[pl.ds(gix(j, k, cls), SUB), :] = new[cls]
                         else:
-                            x = x + (right[cls] + back[cls])
-                        new.append(x)
-                    if left:
-                        for cls in range(CLASSES):
-                            target[pl.ds(gix(j, k, cls), SUB), :] = new[cls]
-                    else:
-                        row = j - (H - 1)
-                        u = [
-                            new[cls] * (vreg(rr, at(rr, j, k, cls)) * (1.0 / residual_scale))
-                            for cls in range(CLASSES)
-                        ]
-                        for pair in range(2):
-                            even, odd = u[2 * pair], u[2 * pair + 1]
-                            first = jnp.where(low, even, swap_halves(odd))
-                            second = jnp.where(low, swap_halves(even), odd)
-                            for upper, value in enumerate((first, second)):
-                                place = (((row * K + k) * NF + upper * NB + ft) * 2 + pair) * SUB
-                                yy[pl.ds(al(place), SUB), :] = value
+                            row = j - (H - 1)
+                            scaled = [
+                                new[cls] * (vreg(rr, at(rr, j, k, cls)) * (1.0 / residual_scale))
+                                for cls in range(CLASSES)
+                            ]
+                            for pair in range(2):
+                                even, odd = scaled[2 * pair], scaled[2 * pair + 1]
+                                first = jnp.where(low, even, swap_halves(odd))
+                                second = jnp.where(low, swap_halves(even), odd)
+                                for upper, value in enumerate((first, second)):
+                                    place = (((row * K + k) * NF + upper * NB + ft) * 2 + pair) * SUB
+                                    yy[pl.ds(al(place), SUB), :] = value
             return c
 
-        lax.fori_loop(0, K, sweeps, 0)
+        lax.fori_loop(0, K // KS, sweeps, 0)
         return carry
 
     lax.fori_loop(0, NB, sweep_block, 0)
 
     damping = solve_damping * 255.0
     inv_span = 1.0 / SPAN
-    VP = dates + SUB
     for u in range(vv.shape[0]):
         for half in range(2):
             vv[u, half, pl.ds(dates, SUB), :] = zero
@@ -618,48 +629,42 @@
                             vv[u, half, place, :] = v
         return c
 
-    lax.fori_loop(0, R // U, invert_rows, 0)
-
     perm_ref[...] = perm_matrix(True)
     unknowns = dates - 1
     OP = dates + 1
 
-    def finish(i, c):
+    def finish(first):
         split = [[], [], []]
-        for u in range(UO):
-            rest = jnp.concatenate([vfin[i * UO + u, 0], vfin[i * UO + u, 1]], axis=1)
+        for u in range(SUB):
+            rest = jnp.concatenate([vfin[first + u, 0], vfin[first + u, 1]], axis=1)
             for part in split:
                 part.append(rest.astype(BF16))
                 rest = rest - part[-1].astype(F32)
-        stack = jnp.concatenate(split[0] + split[1] + split[2], axis=0)
-        out = jnp.dot(stack, perm_ref[...], preferred_element_type=F32)
-        n = UO * dates
-        out = out[:n] + (out[n : 2 * n] + out[2 * n :])
-        for u in range(UO):
+        out = None
+        for part in split:
+            x = jnp.dot(jnp.concatenate(part, axis=0), perm_ref[...], preferred_element_type=F32)
+            out = x if out is None else out + x
+        for u in range(SUB):
             for half in range(2):
-                fbuf[half, pl.ds((i * UO + u) * OP, dates), :] = out[
+                fbuf[half, pl.ds(u * OP, dates), :] = out[
                     u * dates : (u + 1) * dates, half * LANES : (half + 1) * LANES
                 ]
-        return c
-
-    lax.fori_loop(0, R // UO, finish, 0)
-    for j in range(unknowns):
+        for j in range(unknowns):
+            for half in range(2):
+                obuf[half, j, pl.ds(first, SUB), :] = fbuf[half, pl.ds(j, SUB, stride=OP), :]
+
+    outs = []
+    for first in range(0, R, SUB):
+        lax.fori_loop(first // U, (first + SUB) // U, invert_rows, 0)
+        finish(first)
         for half in range(2):
-            for block in range(R // SUB):
-                obuf[half, j, pl.ds(block * SUB, SUB), :] = fbuf[
-                    half, pl.ds(block * SUB * OP + j, SUB, stride=OP), :
-                ]
-    outs = []
-    for half in range(2):
-        outs.append(
-            pltpu.make_async_copy(
-                obuf.at[half, pl.ds(0, unknowns)],
-                out_hbm.at[:, :, pl.ds(half * LANES, LANES)],
-                osem.at[half],
+            copy = pltpu.make_async_copy(
+                obuf.at[half, pl.ds(0, unknowns), pl.ds(first, SUB)],
+                out_hbm.at[:, pl.ds(first, SUB), pl.ds(half * LANES, LANES)],
+                osem.at[first // SUB, half],
             )
-        )
-    for copy in outs:
-        copy.start()
+            copy.start()
+            outs.append(copy)
     for copy in outs:
         copy.wait()
 
@@ -678,7 +683,7 @@
     )(wraw, msk)
 
 
-def solve(own, partner, halo, msk, lmsk, wf):
+def solve(own, near, rest, halo, msk, lmsk, wf):
     tile_rows = own.shape[0]
     dates = 2 * own.shape[3]
     R = tile_rows // 2
@@ -696,7 +701,7 @@
     inner = pl.pallas_call(
         inner_kernel,
         out_shape=tuple(stencil),
-        in_specs=[vm] * 3,
+        in_specs=[vm] * 4,
         out_specs=(vm,) * 4,
         scratch_shapes=[
             v2((R + H) * image),
@@ -705,7 +710,7 @@
         name="inner",
         compiler_params=pltpu.CompilerParams(vmem_limit_bytes=24 * 1024 * 1024),
     )
-    rr, ss, aa, hlo = inner(own, partner, lmsk)
+    rr, ss, aa, hlo = inner(own, near, rest, lmsk)
     outer = pl.pallas_call(
         outer_kernel,
         out_shape=(jax.ShapeDtypeStruct((dates - 1, R, columns), F32), *stencil),
@@ -722,25 +727,28 @@
             pltpu.VMEM((U, 2, SPAN, dates + SUB, LANES), F32),
             pltpu.VMEM((U, NF, 2, K, SUB, LANES), F32),
             pltpu.VMEM((R, 2, dates, LANES), F32),
-            pltpu.VMEM((2, R * (dates + 1), LANES), F32),
+            pltpu.VMEM((2, SUB * (dates + 1), LANES), F32),
             pltpu.VMEM((2, dates, R, LANES), F32),
             pltpu.VMEM((columns, columns), BF16),
-            pltpu.SemaphoreType.DMA((2,)),
+            pltpu.SemaphoreType.DMA((R // SUB, 2)),
         ],
         name="outer",
         compiler_params=pltpu.CompilerParams(vmem_limit_bytes=28 * 1024 * 1024),
     )
-    return outer(own, partner, halo, msk, lmsk, rr, ss, aa, hlo, wf)[0]
+    return outer(own, near, halo, msk, lmsk, rr, ss, aa, hlo, wf)[0]
 
 
 def local(slc_real, slc_imag, pair_offset, pair_weight):
     tiles = lax.axis_size("tile")
-    own, msk, lmsk, wraw = pack(slc_real, slc_imag, pair_offset.T, pair_weight)
-    partner = lax.ppermute(own, "date", [(0, 1), (1, 0)])
+    swap = [(0, 1), (1, 0)]
+    moves = [(2 * t + 1, 2 * t + 2) for t in range(tiles - 1)] + [(2 * t + 2, 2 * t + 1) for t in range(tiles - 1)]
+    own, near, rest, msk, lmsk, wraw = pack(slc_real, slc_imag, pair_offset.T, pair_weight)
+    near = lax.ppermute(near, "date", swap)
+    rest = lax.ppermute(rest, "date", swap)
+    sent = edges(own, near)
+    halo = lax.ppermute(sent, ("tile", "date"), moves)
     wf = weigh(wraw, msk)
-    moves = [(2 * t + 1, 2 * t + 2) for t in range(tiles - 1)] + [(2 * t + 2, 2 * t + 1) for t in range(tiles - 1)]
-    halo = lax.ppermute(edges(own, partner, wf), ("tile", "date"), moves)
-    return solve(own, partner, halo, msk, lmsk, wf)
+    return solve(own, near, rest, halo, msk, lmsk, wf)
 
 
 def solution(mesh):

time: 35.3 us -> 34.5 us (0.977)
  Pallas kernels: 30.5 us -> 27.7 us
  waiting for transfers between devices: 0.01 us -> 1.79 us
    ppermute x2 -> x3, waiting for transfers between devices: 0.01 us -> 1.79 us  [the longest x1 1.35 us: local(): near = lax.ppermute(near, 'date', swap)]
    pallas_call x1, Pallas kernels: 2.8 us -> 1.08 us  [weigh(): pl.pallas_call(weight_kernel, out_shape=pltpu.VMEM((R * (2 * pairs + 1),...]
    pallas_call x2, Pallas kernels: 25.6 us -> 24.9 us  [the longest x1 17.4 us: solve(): return outer(own, near, halo, msk, lmsk, rr, ss, aa, hlo, wf)[0]]
    ppermute x2 -> x3, starting transfers between devices: 4.6 us -> 4.68 us  [the longest x1 4.53 us: local(): halo = lax.ppermute(sent, ('tile', 'date'), moves)]
  transfers between devices with their start and end apart: 2 -> 3, of which waited for: 0 -> 2; matrix products, arithmetic and copies ran while one was open for 0% -> 0% of each run, Pallas kernels for 31% -> 25%
where the time goes in v5:
time: 34.5 us; the launch traced here: 34.3 us
  Pallas kernels  27.7 us (80%)
  starting transfers between devices  4.68 us (14%)
  waiting for transfers between devices  1.79 us (5%)
    pallas_call x1, Pallas kernels, solve(): return outer(own, near, halo, msk, lmsk, rr, ss, aa, hlo, wf)[0]  17.4 us
    pallas_call x1, Pallas kernels, solve(): rr, ss, aa, hlo = inner(own, near, rest, lmsk)  7.52 us
    ppermute x1, starting transfers between devices, local(): halo = lax.ppermute(sent, ('tile', 'date'), moves)  4.53 us
    pallas_call x1, Pallas kernels, pack(): pl.pallas_call(pack_kernel, out_shape=(pltpu.VMEM((rows, 2, 2, dates, LAN...  1.77 us
    ppermute x1, waiting for transfers between devices, local(): near = lax.ppermute(near, 'date', swap)  1.35 us
    pallas_call x1, Pallas kernels, weigh(): pl.pallas_call(weight_kernel, out_shape=pltpu.VMEM((R * (2 * pairs + 1),...  1.08 us
  transfers between devices with their start and end apart: 3, of which 2 were waited for; matrix products, arithmetic and copies ran while one was open for 0% of the time, Pallas kernels for 25%

profile of v5, /device:TPU:1, one launch (start us, length us, event | category | flops | bytes accessed | tf_op | source)
XLA Modules:
  0.0 34.3 jit_solution(326825355671831761)
XLA Ops:
  0.0 1.8 %pack.1 = (bf16[32,2,2,16,128]{4,3,2,1,0:T(8,128)(2,1)S(1)}, bf16[9,2,2,16,128]{4,3,2,1,0:T(8,128)(2,1)S(1)}, bf16[16,2,2,16,128]{4,3,2,1,0:T(8,128)(2,1)S(1)}, ...) custom-call(bf16[16,32,256]{2,1,0:T(8,128)(2,1)} %re_hbm.1, ...), custom_call_target="tpu_custom_call" | custom-call | tf_op jit(solution)/shard_map/pack/pallas_call | solution.py:111
  1.8 0.1 collective-permute-start
  1.9 1.4 %collective-permute-done.near_ref = bf16[9,2,2,16,128]{4,3,2,1,0:T(8,128)(2,1)S(1)} collective-permute-done((bf16[9,2,2,16,128]{4,3,2,1,0:T(8,128)(2,1)S(1)}, bf16[9,2,2,16,128]{4,3,2,1,0:T(8,128)(2,1)S(1)}, u32[]{:S(2)}, u32[]{:S(2)}) %collective-permute-start) | collective-permute-done | bytes 147488 | tf_op jit(solution)/shard_map/ppermute | solution.py:746
  3.2 4.5 %collective-permute-start.1 = (bf16[2,9,2,2,16,128]{5,4,3,2,1,0:T(8,128)(2,1)S(1)}, bf16[2,9,2,2,16,128]{5,4,3,2,1,0:T(8,128)(2,1)S(1)}, u32[]{:S(2)}, u32[]{:S(2)}) collective-permute-start(bf16[2,9,2,2,16,128]{5,4,3,2,1,0:T(8,128)(2,1)S(1)} %edges.1), channel_id=1, source_target_pairs={{1,2},{3,4},{5,6},{7,8},{9,10},{11,12},{13,14},{2,1},{4,3},{6,5},{... | collective-permute-start | bytes 884744 | tf_op jit(solution)/shard_map/ppermute | solution.py:749
  7.8 0.1 collective-permute-start.2
  7.9 1.1 %weigh.1.wf = f32[4112,128]{1,0:T(8,128)S(1)} custom-call(s32[2,128,16,128]{3,2,1,0:T(8,128)S(1)} %get-tuple-element.25.wraw, f32[6,32,128]{2,1,0:T(8,128)S(1)} %get-tuple-element.18.msk), custom_call_target="tpu_custom_call" | custom-call | tf_op jit(solution)/shard_map/weigh/pallas_call | solution.py:675
  8.9 0.4 %collective-permute-done.2.rest_ref = bf16[16,2,2,16,128]{4,3,2,1,0:T(8,128)(2,1)S(1)} collective-permute-done((bf16[16,2,2,16,128]{4,3,2,1,0:T(8,128)(2,1)S(1)}, bf16[16,2,2,16,128]{4,3,2,1,0:T(8,128)(2,1)S(1)}, u32[]{:S(2)}, u32[]{:S(2)}) %collective-permute-start.2) | collective-permute-done | bytes 262176 | tf_op jit(solution)/shard_map/ppermute | solution.py:747
  9.4 7.5 %inner.1 = (f32[8192,128]{1,0:T(8,128)S(1)}, f32[8192,128]{1,0:T(8,128)S(1)}, f32[8192,128]{1,0:T(8,128)S(1)}, f32[8192,128]{1,0:T(8,128)S(1)}) custom-call(bf16[32,2,2,16,128]{4,3,2,1,0:T(8,128)(2,1)S(1)} %get-tuple-element.16.own_ref, bf16[9,2,2,16,128]{4,3,2,1,0:T(8,128)(2,1)S(1)} %collective-permute-done.near_ref, ...), custom_call_target="tpu_custom_call" | custom-call | tf_op jit(solution)/shard_map/inner/pallas_call | solution.py:713
  16.9 0.0 collective-permute-done.1.halo_ref
  16.9 17.4 %outer.1 = (f32[31,16,256]{2,1,0:T(8,128)}, f32[8192,128]{1,0:T(8,128)S(1)}, f32[8192,128]{1,0:T(8,128)S(1)}, f32[8192,128]{1,0:T(8,128)S(1)}, f32[8192,128]{1,0:T(8,128)S(1)}) custom-call(bf16[32,2,2,16,128]{4,3,2,1,0:T(8,128)(2,1)S(1)} %get-tuple-element.16.own_ref, ...), custom_call_target="tpu_custom_call", output_to_operand_aliasing={{1}: (5, {}), {2}: (6, {}), {3}: (7, {}), {4}: (8, {})} | custom-call | tf_op jit(solution)/shard_map/outer/pallas_call | solution.py:738
  (1 shorter events, 0.0 us)
Async XLA Ops:
  1.8 1.4 %collective-permute-start = (bf16[9,2,2,16,128]{4,3,2,1,0:T(8,128)(2,1)S(1)}, bf16[9,2,2,16,128]{4,3,2,1,0:T(8,128)(2,1)S(1)}, u32[]{:S(2)}, u32[]{:S(2)}) collective-permute-start(bf16[9,2,2,16,128]{4,3,2,1,0:T(8,128)(2,1)S(1)} %get-tuple-element.17), channel_id=1, source_target_pairs={{0,1},{1,0},{2,3},{3,2},{4,5},{5,4},{6,7},{7,6},{8,9},{9,8},{10,11... | collective-permute-start | bytes 442376 | tf_op jit(solution)/shard_map/ppermute | solution.py:746
  3.2 13.7 %collective-permute-start.1 = (bf16[2,9,2,2,16,128]{5,4,3,2,1,0:T(8,128)(2,1)S(1)}, bf16[2,9,2,2,16,128]{5,4,3,2,1,0:T(8,128)(2,1)S(1)}, u32[]{:S(2)}, u32[]{:S(2)}) collective-permute-start(bf16[2,9,2,2,16,128]{5,4,3,2,1,0:T(8,128)(2,1)S(1)} %edges.1), channel_id=1, source_target_pairs={{1,2},{3,4},{5,6},{7,8},{9,10},{11,12},{13,14},{2,1},{4,3},{6,5},{... | collective-permute-start | bytes 884744 | tf_op jit(solution)/shard_map/ppermute | solution.py:749
  7.8 1.6 %collective-permute-start.2 = (bf16[16,2,2,16,128]{4,3,2,1,0:T(8,128)(2,1)S(1)}, bf16[16,2,2,16,128]{4,3,2,1,0:T(8,128)(2,1)S(1)}, u32[]{:S(2)}, u32[]{:S(2)}) collective-permute-start(bf16[16,2,2,16,128]{4,3,2,1,0:T(8,128)(2,1)S(1)} %get-tuple-element.20), channel_id=1, source_target_pairs={{0,1},{1,0},{2,3},{3,2},{4,5},{5,4},{6,7},{7,6},{8,9},{9,8},{10,11... | collective-permute-start | bytes 786440 | tf_op jit(solution)/shard_map/ppermute | solution.py:747

commit v6 on v5

--- a/solution.py
+++ b/solution.py
@@ -22,8 +22,8 @@
 CLASSES = 4
 GROUPS = 64
 UI, UH, UW, KS = 4, 3, 32, 1
-UNROLL_1 = (25, 8, 7)
-UNROLL_2 = (14, 6, 10)
+UNROLL_1 = (25, 4, 7)
+UNROLL_2 = (14, 3, 10)
 MORE = 5
 HALO = SWEEPS + 1
 F32 = jnp.float32
@@ -276,46 +276,56 @@
                 link = link * scale
             return link, link * (cross * q)
 
-        def smooth(j):
+        def smooth(j, rows):
             for k in range(K):
-                re, im, mg = [], [], []
-                for cls in range(CLASSES):
-                    i0, i1, i2 = (gix(j + d, k, cls) for d in range(3))
-                    x = vreg(cre, i0) + vreg(cre, i1) + vreg(cre, i2)
-                    y = vreg(cim, i0) + vreg(cim, i1) + vreg(cim, i2)
-                    sq = x * x + y * y
-                    m = sq * lax.rsqrt(jnp.maximum(sq, 1e-30))
-                    zre[pl.ds(i0, SUB), :] = x
-                    zim[pl.ds(i0, SUB), :] = y
-                    mag[pl.ds(i0, SUB), :] = m
-                    re.append(x)
-                    im.append(y)
-                    mg.append(m)
-                links, flows = [], []
-                for cls in range(CLASSES):
-                    if cls < CLASSES - 1:
-                        n_re, n_im, m = re[cls + 1], im[cls + 1], mg[cls] * mg[cls + 1]
-                    else:
-                        n_re, n_im = roll_left(re[0]), roll_left(im[0])
-                        m = jnp.where(at_last, 0.0, mg[cls] * roll_left(mg[0]))
-                    link, flow = edge(m, im[cls] * n_re - re[cls] * n_im, column_weight)
-                    hle[pl.ds(gix(j, k, cls), SUB), :] = link
-                    links.append(link)
-                    flows.append(flow)
-                mid = links[1] + unwrap_damping
-                end = links[3] + unwrap_damping
-                dens = (links[0] + roll_right(end), links[0] + mid, mid + links[2], links[2] + end)
-                srcs = (
-                    flows[0] - roll_right(flows[3]),
-                    flows[1] - flows[0],
-                    flows[2] - flows[1],
-                    flows[3] - flows[2],
-                )
-                for cls in range(CLASSES):
-                    dh[pl.ds(gix(j, k, cls), SUB), :] = dens[cls]
-                    sh[pl.ds(gix(j, k, cls), SUB), :] = srcs[cls]
-
-        run(count - 2, ub, smooth)
+                sums = [{}, {}]
+                for part, ref in enumerate((cre, cim)):
+                    for cls in range(CLASSES):
+                        c = [vreg(ref, gix(j + d, k, cls)) for d in range(rows + 2)]
+                        middle = c[1] + c[2]
+                        sums[part][0, cls] = c[0] + middle
+                        if rows == 2:
+                            sums[part][1, cls] = middle + c[3]
+                for d in range(rows):
+                    smooth_row(j + d, k, [[sums[part][d, cls] for cls in range(CLASSES)] for part in range(2)])
+
+        def smooth_row(j, k, sums):
+            re, im = sums
+            mg = []
+            for cls in range(CLASSES):
+                i0 = gix(j, k, cls)
+                sq = re[cls] * re[cls] + im[cls] * im[cls]
+                mg.append(sq * lax.rsqrt(jnp.maximum(sq, 1e-30)))
+                zre[pl.ds(i0, SUB), :] = re[cls]
+                zim[pl.ds(i0, SUB), :] = im[cls]
+                mag[pl.ds(i0, SUB), :] = mg[cls]
+            links, flows = [], []
+            for cls in range(CLASSES):
+                if cls < CLASSES - 1:
+                    n_re, n_im, m = re[cls + 1], im[cls + 1], mg[cls] * mg[cls + 1]
+                else:
+                    n_re, n_im = roll_left(re[0]), roll_left(im[0])
+                    m = jnp.where(at_last, 0.0, mg[cls] * roll_left(mg[0]))
+                link, flow = edge(m, im[cls] * n_re - re[cls] * n_im, column_weight)
+                hle[pl.ds(gix(j, k, cls), SUB), :] = link
+                links.append(link)
+                flows.append(flow)
+            mid = links[1] + unwrap_damping
+            end = links[3] + unwrap_damping
+            dens = (links[0] + roll_right(end), links[0] + mid, mid + links[2], links[2] + end)
+            srcs = (
+                flows[0] - roll_right(flows[3]),
+                flows[1] - flows[0],
+                flows[2] - flows[1],
+                flows[3] - flows[2],
+            )
+            for cls in range(CLASSES):
+                dh[pl.ds(gix(j, k, cls), SUB), :] = dens[cls]
+                sh[pl.ds(gix(j, k, cls), SUB), :] = srcs[cls]
+
+        run((count - 2) // 2, ub, lambda i: smooth(2 * i, 2))
+        if count % 2:
+            smooth(count - 3, 1)
 
         for condition, row in outside:
             @pl.when(condition)
@@ -532,14 +542,20 @@
                             ]
                             for pair in range(2):
                                 even, odd = scaled[2 * pair], scaled[2 * pair + 1]
-                                first = jnp.where(low, even, swap_halves(odd))
-                                second = jnp.where(low, swap_halves(even), odd)
+                                crossed = swap_halves(jnp.where(low, odd, even))
+                                first = jnp.where(low, even, crossed)
+                                second = jnp.where(low, crossed, odd)
                                 for upper, value in enumerate((first, second)):
                                     place = (((row * K + k) * NF + upper * NB + ft) * 2 + pair) * SUB
                                     yy[pl.ds(al(place), SUB), :] = value
             return c
 
-        lax.fori_loop(0, K // KS, sweeps, 0)
+        def two(i, c):
+            sweeps(2 * i, 0)
+            sweeps(2 * i + 1, 0)
+            return c
+
+        lax.fori_loop(0, K // 2, two, 0)
         return carry
 
     lax.fori_loop(0, NB, sweep_block, 0)
@@ -695,7 +711,7 @@
     image = 2 * CLASSES * (dates // 2 + SUB)
     vm = pl.BlockSpec(memory_space=pltpu.VMEM)
     hbm = pl.BlockSpec(memory_space=pl.ANY)
-    U = 1
+    U = 2
     v2 = lambda rows: pltpu.VMEM((rows, LANES), F32)
     stencil = [v2(NF // 2 * NZ * group)] * 4
     inner = pl.pallas_call(

time: 34.5 us -> 32.8 us (0.951)
  Pallas kernels: 27.7 us -> 26.1 us
    pallas_call x1, Pallas kernels: 17.4 us -> 15.8 us  [solve(): return outer(own, near, halo, msk, lmsk, rr, ss, aa, hlo, wf)[0]]
  transfers between devices with their start and end apart: 3 -> 3, of which waited for: 2 -> 2; matrix products, arithmetic and copies ran while one was open for 0% -> 0% of each run, Pallas kernels for 25% -> 26%
where the time goes in v6:
time: 32.8 us; the launch traced here: 32.6 us
  Pallas kernels  26.1 us (80%)
  starting transfers between devices  4.68 us (14%)
  waiting for transfers between devices  1.79 us (5%)
    pallas_call x1, Pallas kernels, solve(): return outer(own, near, halo, msk, lmsk, rr, ss, aa, hlo, wf)[0]  15.8 us
    pallas_call x1, Pallas kernels, solve(): rr, ss, aa, hlo = inner(own, near, rest, lmsk)  7.36 us
    ppermute x1, starting transfers between devices, local(): halo = lax.ppermute(sent, ('tile', 'date'), moves)  4.53 us
    pallas_call x1, Pallas kernels, pack(): pl.pallas_call(pack_kernel, out_shape=(pltpu.VMEM((rows, 2, 2, dates, LAN...  1.77 us
    ppermute x1, waiting for transfers between devices, local(): near = lax.ppermute(near, 'date', swap)  1.35 us
    pallas_call x1, Pallas kernels, weigh(): pl.pallas_call(weight_kernel, out_shape=pltpu.VMEM((R * (2 * pairs + 1),...  1.08 us
  transfers between devices with their start and end apart: 3, of which 2 were waited for; matrix products, arithmetic and copies ran while one was open for 0% of the time, Pallas kernels for 26%

profile of v6, /device:TPU:1, one launch (start us, length us, event | category | flops | bytes accessed | tf_op | source)
XLA Modules:
  0.0 32.6 jit_solution(8701990610772396959)
XLA Ops:
  0.0 1.8 %pack.1 = (bf16[32,2,2,16,128]{4,3,2,1,0:T(8,128)(2,1)S(1)}, bf16[9,2,2,16,128]{4,3,2,1,0:T(8,128)(2,1)S(1)}, bf16[16,2,2,16,128]{4,3,2,1,0:T(8,128)(2,1)S(1)}, ...) custom-call(bf16[16,32,256]{2,1,0:T(8,128)(2,1)} %re_hbm.1, ...), custom_call_target="tpu_custom_call" | custom-call | tf_op jit(solution)/shard_map/pack/pallas_call | solution.py:111
  1.8 0.1 collective-permute-start
  1.9 1.4 %collective-permute-done.near_ref = bf16[9,2,2,16,128]{4,3,2,1,0:T(8,128)(2,1)S(1)} collective-permute-done((bf16[9,2,2,16,128]{4,3,2,1,0:T(8,128)(2,1)S(1)}, bf16[9,2,2,16,128]{4,3,2,1,0:T(8,128)(2,1)S(1)}, u32[]{:S(2)}, u32[]{:S(2)}) %collective-permute-start) | collective-permute-done | bytes 147488 | tf_op jit(solution)/shard_map/ppermute | solution.py:762
  3.2 4.5 %collective-permute-start.1 = (bf16[2,9,2,2,16,128]{5,4,3,2,1,0:T(8,128)(2,1)S(1)}, bf16[2,9,2,2,16,128]{5,4,3,2,1,0:T(8,128)(2,1)S(1)}, u32[]{:S(2)}, u32[]{:S(2)}) collective-permute-start(bf16[2,9,2,2,16,128]{5,4,3,2,1,0:T(8,128)(2,1)S(1)} %edges.1), channel_id=1, source_target_pairs={{1,2},{3,4},{5,6},{7,8},{9,10},{11,12},{13,14},{2,1},{4,3},{6,5},{... | collective-permute-start | bytes 884744 | tf_op jit(solution)/shard_map/ppermute | solution.py:765
  7.8 0.1 collective-permute-start.2
  7.9 1.1 %weigh.1.wf = f32[4112,128]{1,0:T(8,128)S(1)} custom-call(s32[2,128,16,128]{3,2,1,0:T(8,128)S(1)} %get-tuple-element.25.wraw, f32[6,32,128]{2,1,0:T(8,128)S(1)} %get-tuple-element.18.msk), custom_call_target="tpu_custom_call" | custom-call | tf_op jit(solution)/shard_map/weigh/pallas_call | solution.py:691
  8.9 0.4 %collective-permute-done.2.rest_ref = bf16[16,2,2,16,128]{4,3,2,1,0:T(8,128)(2,1)S(1)} collective-permute-done((bf16[16,2,2,16,128]{4,3,2,1,0:T(8,128)(2,1)S(1)}, bf16[16,2,2,16,128]{4,3,2,1,0:T(8,128)(2,1)S(1)}, u32[]{:S(2)}, u32[]{:S(2)}) %collective-permute-start.2) | collective-permute-done | bytes 262176 | tf_op jit(solution)/shard_map/ppermute | solution.py:763
  9.4 7.4 %inner.1 = (f32[8192,128]{1,0:T(8,128)S(1)}, f32[8192,128]{1,0:T(8,128)S(1)}, f32[8192,128]{1,0:T(8,128)S(1)}, f32[8192,128]{1,0:T(8,128)S(1)}) custom-call(bf16[32,2,2,16,128]{4,3,2,1,0:T(8,128)(2,1)S(1)} %get-tuple-element.16.own_ref, bf16[9,2,2,16,128]{4,3,2,1,0:T(8,128)(2,1)S(1)} %collective-permute-done.near_ref, ...), custom_call_target="tpu_custom_call" | custom-call | tf_op jit(solution)/shard_map/inner/pallas_call | solution.py:729
  16.7 0.0 collective-permute-done.1.halo_ref
  16.8 15.8 %outer.1 = (f32[31,16,256]{2,1,0:T(8,128)}, f32[8192,128]{1,0:T(8,128)S(1)}, f32[8192,128]{1,0:T(8,128)S(1)}, f32[8192,128]{1,0:T(8,128)S(1)}, f32[8192,128]{1,0:T(8,128)S(1)}) custom-call(bf16[32,2,2,16,128]{4,3,2,1,0:T(8,128)(2,1)S(1)} %get-tuple-element.16.own_ref, ...), custom_call_target="tpu_custom_call", output_to_operand_aliasing={{1}: (5, {}), {2}: (6, {}), {3}: (7, {}), {4}: (8, {})} | custom-call | tf_op jit(solution)/shard_map/outer/pallas_call | solution.py:754
  (1 shorter events, 0.0 us)
Async XLA Ops:
  1.8 1.4 %collective-permute-start = (bf16[9,2,2,16,128]{4,3,2,1,0:T(8,128)(2,1)S(1)}, bf16[9,2,2,16,128]{4,3,2,1,0:T(8,128)(2,1)S(1)}, u32[]{:S(2)}, u32[]{:S(2)}) collective-permute-start(bf16[9,2,2,16,128]{4,3,2,1,0:T(8,128)(2,1)S(1)} %get-tuple-element.17), channel_id=1, source_target_pairs={{0,1},{1,0},{2,3},{3,2},{4,5},{5,4},{6,7},{7,6},{8,9},{9,8},{10,11... | collective-permute-start | bytes 442376 | tf_op jit(solution)/shard_map/ppermute | solution.py:762
  3.2 13.5 %collective-permute-start.1 = (bf16[2,9,2,2,16,128]{5,4,3,2,1,0:T(8,128)(2,1)S(1)}, bf16[2,9,2,2,16,128]{5,4,3,2,1,0:T(8,128)(2,1)S(1)}, u32[]{:S(2)}, u32[]{:S(2)}) collective-permute-start(bf16[2,9,2,2,16,128]{5,4,3,2,1,0:T(8,128)(2,1)S(1)} %edges.1), channel_id=1, source_target_pairs={{1,2},{3,4},{5,6},{7,8},{9,10},{11,12},{13,14},{2,1},{4,3},{6,5},{... | collective-permute-start | bytes 884744 | tf_op jit(solution)/shard_map/ppermute | solution.py:765
  7.8 1.6 %collective-permute-start.2 = (bf16[16,2,2,16,128]{4,3,2,1,0:T(8,128)(2,1)S(1)}, bf16[16,2,2,16,128]{4,3,2,1,0:T(8,128)(2,1)S(1)}, u32[]{:S(2)}, u32[]{:S(2)}) collective-permute-start(bf16[16,2,2,16,128]{4,3,2,1,0:T(8,128)(2,1)S(1)} %get-tuple-element.20), channel_id=1, source_target_pairs={{0,1},{1,0},{2,3},{3,2},{4,5},{5,4},{6,7},{7,6},{8,9},{9,8},{10,11... | collective-permute-start | bytes 786440 | tf_op jit(solution)/shard_map/ppermute | solution.py:763

commit v7 on v6

--- a/solution.py
+++ b/solution.py
@@ -48,7 +48,7 @@
 
 
 def pack_kernel(
-    re_hbm, im_hbm, offset_hbm, weight_hbm, all_ref, near_ref, rest_ref, msk, lmsk, wraw,
+    re_hbm, im_hbm, offset_hbm, all_ref, near_ref, rest_ref, msk, lmsk,
     images, offset_ref, flat, turned, perm_ref, sems,
 ):
     _, dates, rows, columns = images.shape
@@ -57,10 +57,6 @@
         pltpu.make_async_copy(re_hbm, images.at[0], sems.at[0]),
         pltpu.make_async_copy(im_hbm, images.at[1], sems.at[1]),
         pltpu.make_async_copy(offset_hbm, offset_ref, sems.at[2]),
-    ]
-    copies += [
-        pltpu.make_async_copy(weight_hbm.at[:, :, pl.ds(half * LANES, LANES)], wraw.at[half], sems.at[3 + half])
-        for half in range(2)
     ]
     for copy in copies:
         copy.start()
@@ -97,14 +93,11 @@
         rest_ref[i] = all_ref[near * side + (rows - near - rest) * (1 - side) + i]
     copies[2].wait()
     offset_masks(offset_ref, msk, lmsk, turned)
-    copies[3].wait()
-    copies[4].wait()
-
-
-def pack(slc_real, slc_imag, offsets, pair_weight):
+
+
+def pack(slc_real, slc_imag, offsets):
     dates, rows, columns = slc_real.shape
-    pairs, R, _ = pair_weight.shape
-    inputs = [pltpu.with_memory_space_constraint(x, pltpu.HBM) for x in (slc_real, slc_imag, offsets, pair_weight)]
+    inputs = [pltpu.with_memory_space_constraint(x, pltpu.HBM) for x in (slc_real, slc_imag, offsets)]
     vm = pl.BlockSpec(memory_space=pltpu.VMEM)
     hbm = pl.BlockSpec(memory_space=pltpu.HBM)
     per_date, all_dates = offsets.shape
@@ -116,17 +109,16 @@
             pltpu.VMEM((rows // 2, 2, 2, dates, LANES), BF16),
             pltpu.VMEM((2 + per_date, all_dates, LANES), F32),
             pltpu.VMEM((2, all_dates // 2, LANES), F32),
-            pltpu.VMEM((2, pairs, R, LANES), jnp.int32),
         ),
-        in_specs=[hbm] * 4,
-        out_specs=(vm,) * 6,
+        in_specs=[hbm] * 3,
+        out_specs=(vm,) * 5,
         scratch_shapes=[
             pltpu.VMEM((2, dates, rows, columns), BF16),
             pltpu.VMEM(offsets.shape, jnp.int32),
             pltpu.VMEM((2, 2, dates * (rows + 1), LANES), F32),
             pltpu.VMEM((SUB, LANES), F32),
             pltpu.VMEM((columns, columns), BF16),
-            pltpu.SemaphoreType.DMA((5,)),
+            pltpu.SemaphoreType.DMA((3,)),
         ],
         name="pack",
         compiler_params=pltpu.CompilerParams(vmem_limit_bytes=12 * 1024 * 1024),
@@ -392,7 +384,7 @@
     return [v2(count * group)] * 2 + [v2((count - 2) * group)] * 6
 
 
-def weight_kernel(wraw, msk, wf, perm_ref):
+def permute_weights(wraw, msk, wf, perm_ref):
     dates = msk.shape[1]
     R = wraw.shape[2]
     NF = dates // SUB
@@ -427,9 +419,15 @@
 
 
 def inner_kernel(
-    own_ref, near_ref, rest_ref, lmsk, rr, ss, aa, hlo,
-    img, cre, cim, zre, zim, mag, hle, dh, sh,
+    own_ref, near_ref, rest_ref, msk, lmsk, weight_hbm, rr, ss, aa, hlo, wf,
+    img, cre, cim, zre, zim, mag, hle, dh, sh, wraw, perm_ref, wsem,
 ):
+    copies = [
+        pltpu.make_async_copy(weight_hbm.at[:, :, pl.ds(half * LANES, LANES)], wraw.at[half], wsem.at[half])
+        for half in range(2)
+    ]
+    for copy in copies:
+        copy.start()
     R = own_ref.shape[0] // 2
     H = HALO
     NZ = R + 2 * H - 2
@@ -443,6 +441,9 @@
         img, lmsk, R + H, H * (1 - side), (), None, UNROLL_1,
         (cre, cim, zre, zim, mag, hle, dh, sh), (rr, ss, aa, hlo), NZ,
     )
+    for copy in copies:
+        copy.wait()
+    permute_weights(wraw, msk, wf, perm_ref)
 
 
 def outer_kernel(
@@ -685,25 +686,9 @@
         copy.wait()
 
 
-def weigh(wraw, msk):
-    _, pairs, R, _ = wraw.shape
-    vm = pl.BlockSpec(memory_space=pltpu.VMEM)
-    return pl.pallas_call(
-        weight_kernel,
-        out_shape=pltpu.VMEM((R * (2 * pairs + 1), LANES), F32),
-        in_specs=[vm, vm],
-        out_specs=vm,
-        scratch_shapes=[pltpu.VMEM((2 * LANES, 2 * LANES), BF16)],
-        name="weigh",
-        compiler_params=pltpu.CompilerParams(vmem_limit_bytes=4 * 1024 * 1024),
-    )(wraw, msk)
-
-
-def solve(own, near, rest, halo, msk, lmsk, wf):
-    tile_rows = own.shape[0]
+def solve(own, near, rest, halo, msk, lmsk, pair_weight):
     dates = 2 * own.shape[3]
-    R = tile_rows // 2
-    columns = 2 * LANES
+    pairs, R, columns = pair_weight.shape
     H = HALO
     NZ = R + 2 * H - 2
     NF = dates // SUB
@@ -716,17 +701,21 @@
     stencil = [v2(NF // 2 * NZ * group)] * 4
     inner = pl.pallas_call(
         inner_kernel,
-        out_shape=tuple(stencil),
-        in_specs=[vm] * 4,
-        out_specs=(vm,) * 4,
+        out_shape=(*stencil, v2(R * (2 * pairs + 1))),
+        in_specs=[vm] * 5 + [pl.BlockSpec(memory_space=pltpu.HBM)],
+        out_specs=(vm,) * 5,
         scratch_shapes=[
             v2((R + H) * image),
             *work_scratch(R + H),
+            pltpu.VMEM((2, pairs, R, LANES), jnp.int32),
+            pltpu.VMEM((columns, columns), BF16),
+            pltpu.SemaphoreType.DMA((2,)),
         ],
         name="inner",
         compiler_params=pltpu.CompilerParams(vmem_limit_bytes=24 * 1024 * 1024),
     )
-    rr, ss, aa, hlo = inner(own, near, rest, lmsk)
+    weights = pltpu.with_memory_space_constraint(pair_weight, pltpu.HBM)
+    rr, ss, aa, hlo, wf = inner(own, near, rest, msk, lmsk, weights)
     outer = pl.pallas_call(
         outer_kernel,
         out_shape=(jax.ShapeDtypeStruct((dates - 1, R, columns), F32), *stencil),
@@ -758,13 +747,12 @@
     tiles = lax.axis_size("tile")
     swap = [(0, 1), (1, 0)]
     moves = [(2 * t + 1, 2 * t + 2) for t in range(tiles - 1)] + [(2 * t + 2, 2 * t + 1) for t in range(tiles - 1)]
-    own, near, rest, msk, lmsk, wraw = pack(slc_real, slc_imag, pair_offset.T, pair_weight)
+    own, near, rest, msk, lmsk = pack(slc_real, slc_imag, pair_offset.T)
     near = lax.ppermute(near, "date", swap)
     rest = lax.ppermute(rest, "date", swap)
     sent = edges(own, near)
     halo = lax.ppermute(sent, ("tile", "date"), moves)
-    wf = weigh(wraw, msk)
-    return solve(own, near, rest, halo, msk, lmsk, wf)
+    return solve(own, near, rest, halo, msk, lmsk, pair_weight)
 
 
 def solution(mesh):

time: 32.8 us -> 33.9 us (1.034)
  waiting for transfers between devices: 1.79 us -> 2.88 us
    ppermute x1, waiting for transfers between devices: 0.43 us -> 1.52 us  [local(): rest = lax.ppermute(rest, 'date', swap)]
    pallas_call x2 -> x1, Pallas kernels: 8.45 us -> 8.46 us  [solve(): rr, ss, aa, hlo, wf = inner(own, near, rest, msk, lmsk, weights)]
  transfers between devices with their start and end apart: 3 -> 3, of which waited for: 2 -> 2; matrix products, arithmetic and copies ran while one was open for 0% -> 0% of each run, Pallas kernels for 26% -> 25%
where the time goes in v7:
time: 33.9 us; the launch traced here: 33.6 us
  Pallas kernels  26 us (77%)
  starting transfers between devices  4.66 us (14%)
  waiting for transfers between devices  2.88 us (8%)
    pallas_call x1, Pallas kernels, solve(): return outer(own, near, halo, msk, lmsk, rr, ss, aa, hlo, wf)[0]  15.8 us
    pallas_call x1, Pallas kernels, solve(): rr, ss, aa, hlo, wf = inner(own, near, rest, msk, lmsk, weights)  8.46 us
    ppermute x1, starting transfers between devices, local(): halo = lax.ppermute(sent, ('tile', 'date'), moves)  4.51 us
    pallas_call x1, Pallas kernels, pack(): pl.pallas_call(pack_kernel, out_shape=(pltpu.VMEM((rows, 2, 2, dates, LAN...  1.7 us
    ppermute x1, waiting for transfers between devices, local(): rest = lax.ppermute(rest, 'date', swap)  1.52 us
    ppermute x1, waiting for transfers between devices, local(): near = lax.ppermute(near, 'date', swap)  1.36 us
  transfers between devices with their start and end apart: 3, of which 2 were waited for; matrix products, arithmetic and copies ran while one was open for 0% of the time, Pallas kernels for 25%

profile of v7, /device:TPU:1, one launch (start us, length us, event | category | flops | bytes accessed | tf_op | source)
XLA Modules:
  0.0 33.6 jit_solution(14608662820407463537)
XLA Ops:
  0.0 1.7 %pack.1 = (bf16[32,2,2,16,128]{4,3,2,1,0:T(8,128)(2,1)S(1)}, bf16[9,2,2,16,128]{4,3,2,1,0:T(8,128)(2,1)S(1)}, bf16[16,2,2,16,128]{4,3,2,1,0:T(8,128)(2,1)S(1)}, ...) custom-call(bf16[16,32,256]{2,1,0:T(8,128)(2,1)} %re_hbm.1, bf16[16,32,256]{2,1,0:T(8,128)(2,1)} %im_hbm.1, s32[4,32]{1,0:T(4,128)} %bitcast.1), custom_call_target="tpu_custom_call" | custom-call | tf_op jit(solution)/shard_map/pack/pallas_call | solution.py:104
  1.7 0.1 collective-permute-start
  1.8 1.4 %collective-permute-done.near_ref = bf16[9,2,2,16,128]{4,3,2,1,0:T(8,128)(2,1)S(1)} collective-permute-done((bf16[9,2,2,16,128]{4,3,2,1,0:T(8,128)(2,1)S(1)}, bf16[9,2,2,16,128]{4,3,2,1,0:T(8,128)(2,1)S(1)}, u32[]{:S(2)}, u32[]{:S(2)}) %collective-permute-start) | collective-permute-done | bytes 147488 | tf_op jit(solution)/shard_map/ppermute | solution.py:751
  3.2 4.5 %collective-permute-start.1 = (bf16[2,9,2,2,16,128]{5,4,3,2,1,0:T(8,128)(2,1)S(1)}, bf16[2,9,2,2,16,128]{5,4,3,2,1,0:T(8,128)(2,1)S(1)}, u32[]{:S(2)}, u32[]{:S(2)}) collective-permute-start(bf16[2,9,2,2,16,128]{5,4,3,2,1,0:T(8,128)(2,1)S(1)} %edges.1), channel_id=1, source_target_pairs={{1,2},{3,4},{5,6},{7,8},{9,10},{11,12},{13,14},{2,1},{4,3},{6,5},{... | collective-permute-start | bytes 884744 | tf_op jit(solution)/shard_map/ppermute | solution.py:754
  7.7 0.1 collective-permute-start.2
  7.8 1.5 %collective-permute-done.2.rest_ref = bf16[16,2,2,16,128]{4,3,2,1,0:T(8,128)(2,1)S(1)} collective-permute-done((bf16[16,2,2,16,128]{4,3,2,1,0:T(8,128)(2,1)S(1)}, bf16[16,2,2,16,128]{4,3,2,1,0:T(8,128)(2,1)S(1)}, u32[]{:S(2)}, u32[]{:S(2)}) %collective-permute-start.2) | collective-permute-done | bytes 262176 | tf_op jit(solution)/shard_map/ppermute | solution.py:752
  9.3 8.5 %inner.1 = (f32[8192,128]{1,0:T(8,128)S(1)}, f32[8192,128]{1,0:T(8,128)S(1)}, f32[8192,128]{1,0:T(8,128)S(1)}, f32[8192,128]{1,0:T(8,128)S(1)}, f32[4112,128]{1,0:T(8,128)S(1)}) custom-call(bf16[32,2,2,16,128]{4,3,2,1,0:T(8,128)(2,1)S(1)} %get-tuple-element.16.own_ref, bf16[9,2,2,16,128]{4,3,2,1,0:T(8,128)(2,1)S(1)} %collective-permute-done.near_ref, ...), custom_call_target="tpu_custom_call" | custom-call | tf_op jit(solution)/shard_map/inner/pallas_call | solution.py:718
  17.8 0.0 collective-permute-done.1.halo_ref
  17.8 15.8 %outer.1 = (f32[31,16,256]{2,1,0:T(8,128)}, f32[8192,128]{1,0:T(8,128)S(1)}, f32[8192,128]{1,0:T(8,128)S(1)}, f32[8192,128]{1,0:T(8,128)S(1)}, f32[8192,128]{1,0:T(8,128)S(1)}) custom-call(bf16[32,2,2,16,128]{4,3,2,1,0:T(8,128)(2,1)S(1)} %get-tuple-element.16.own_ref, ...), custom_call_target="tpu_custom_call", output_to_operand_aliasing={{1}: (5, {}), {2}: (6, {}), {3}: (7, {}), {4}: (8, {})} | custom-call | tf_op jit(solution)/shard_map/outer/pallas_call | solution.py:743
  (1 shorter events, 0.0 us)
Async XLA Ops:
  1.7 1.4 %collective-permute-start = (bf16[9,2,2,16,128]{4,3,2,1,0:T(8,128)(2,1)S(1)}, bf16[9,2,2,16,128]{4,3,2,1,0:T(8,128)(2,1)S(1)}, u32[]{:S(2)}, u32[]{:S(2)}) collective-permute-start(bf16[9,2,2,16,128]{4,3,2,1,0:T(8,128)(2,1)S(1)} %get-tuple-element.17), channel_id=1, source_target_pairs={{0,1},{1,0},{2,3},{3,2},{4,5},{5,4},{6,7},{7,6},{8,9},{9,8},{10,11... | collective-permute-start | bytes 442376 | tf_op jit(solution)/shard_map/ppermute | solution.py:751
  3.2 14.6 %collective-permute-start.1 = (bf16[2,9,2,2,16,128]{5,4,3,2,1,0:T(8,128)(2,1)S(1)}, bf16[2,9,2,2,16,128]{5,4,3,2,1,0:T(8,128)(2,1)S(1)}, u32[]{:S(2)}, u32[]{:S(2)}) collective-permute-start(bf16[2,9,2,2,16,128]{5,4,3,2,1,0:T(8,128)(2,1)S(1)} %edges.1), channel_id=1, source_target_pairs={{1,2},{3,4},{5,6},{7,8},{9,10},{11,12},{13,14},{2,1},{4,3},{6,5},{... | collective-permute-start | bytes 884744 | tf_op jit(solution)/shard_map/ppermute | solution.py:754
  7.7 1.6 %collective-permute-start.2 = (bf16[16,2,2,16,128]{4,3,2,1,0:T(8,128)(2,1)S(1)}, bf16[16,2,2,16,128]{4,3,2,1,0:T(8,128)(2,1)S(1)}, u32[]{:S(2)}, u32[]{:S(2)}) collective-permute-start(bf16[16,2,2,16,128]{4,3,2,1,0:T(8,128)(2,1)S(1)} %get-tuple-element.20), channel_id=1, source_target_pairs={{0,1},{1,0},{2,3},{3,2},{4,5},{5,4},{6,7},{7,6},{8,9},{9,8},{10,11... | collective-permute-start | bytes 786440 | tf_op jit(solution)/shard_map/ppermute | solution.py:752
